TPU v7x, 512 devices: a whole 4x8x8 slice. The times are simulated.
512 devices in a mesh: row: 16 (over x, y_lo), col: 32 (over y_hi, z, core).
Axes of the slice: x: 4, y: 8 (y_hi: 2, y_lo: 4; y = y_hi * 4 + y_lo), z: 8, core: 2. Of those that a mesh axis runs over, the one named last changes fastest.
Arguments:
- bricks: bfloat16 [16, 32, 2, 16, 128, 128], P('row', 'col'), may hold values from -393216 to 393216
- brick_coords: int32 [16, 32, 3, 2], P('row', 'col'), may hold values from 0 to 31, as said below
- brick_counts: int32 [16, 32], P('row', 'col'), may hold values from 0 to 2, as said below
- step_sizes: float32 [2, 3], replicated, may hold values from 0.3 to 1
- init_a: float32 [16, 512, 256], P('row', 'col'), may hold values from -6 to 6
- init_b: float32 [32, 256, 256], P('col', 'row'), may hold values from -6 to 6
- init_c: float32 [512, 256], replicated, may hold values from -6 to 6
Outputs:
- factor_a: float32 [16, 512, 256], P('row', 'col')
- factor_b: float32 [32, 256, 256], P('col', 'row')
- factor_c: float32 [512, 256], replicated
Inputs may be any that keep to these rules, and one draw needn't show every extreme that they name: brick_counts of rows r and (r + half of the row axis) mod the row axis in one column add up to at most 3; some device holds 2 bricks. `brick_coords`: component 0 is below 4, component 1 below 2, component 2 below 32; dead slots hold arbitrary positions.
All inputs are finite; a program needn't handle non-finite values.
Results may differ from a plain program's by a relative error of at most 0.0003.
The roundings to bfloat16 on the way count: a program that leaves them out, or rounds other values in their place, can miss the bound.
Values may be sent and summed in bfloat16 or wider, within the bound.
No kernel may reach another device: no remote copies, remote signals or barrier semaphores. Data moves between devices by JAX's collectives and lax.ppermute only.
A program may use at most 64 MiB of HBM per device.

v0:
```python
import jax
import jax.numpy as jnp
from jax import lax
from jax.sharding import PartitionSpec as P


def brick_terms(brick, a_tile, b_tile, c_rows):
    depth, tile, _ = brick.shape
    wide = jnp.dot(
        brick.reshape(depth * tile, tile), b_tile, preferred_element_type=jnp.float32
    ).reshape(depth, tile, -1)
    c_wide = c_rows.astype(jnp.float32)[:, None, :]
    along_a = jnp.sum(wide * c_wide, axis=0)
    deep = jnp.einsum("kij,ir->kjr", brick, a_tile, preferred_element_type=jnp.float32)
    along_b = jnp.sum(deep * c_wide, axis=0)
    along_c = jnp.sum(deep * b_tile.astype(jnp.float32)[None, :, :], axis=1)
    return (along_a, along_b, along_c)


def add_tile(total, delta, start):
    old = lax.dynamic_slice_in_dim(total, start, delta.shape[0], 0)
    return lax.dynamic_update_slice_in_dim(total, old + delta, start, 0)


def gram(values):
    return jnp.dot(values.T, values, preferred_element_type=jnp.float32)


def project(state, hess, drive, rate):
    scale = jnp.sum(jnp.abs(hess), axis=1) + 1e-06
    slope = (
        jnp.dot(state, hess, precision=lax.Precision.HIGHEST, preferred_element_type=jnp.float32)
        - drive
    )
    return jnp.maximum(state - rate * slope / scale[None, :], 0.0)


def shards(bricks, brick_coords, brick_counts, step_sizes, init_a, init_b, init_c):
    slab = bricks[0, 0]
    places = brick_coords[0, 0]
    own = brick_counts[0, 0]
    depth = slab.shape[1]
    tile = slab.shape[2]
    sweeps = step_sizes.shape[0]
    state_a = init_a[0]
    state_b = init_b[0]
    state_c = init_c
    for sweep in range(sweeps):
        a_bf = state_a.astype(jnp.bfloat16)
        b_bf = state_b.astype(jnp.bfloat16)
        c_bf = state_c.astype(jnp.bfloat16)
        a_range = lax.all_gather(a_bf, "col", axis=0, tiled=True)
        b_range = lax.all_gather(b_bf, "row", axis=0, tiled=True)
        local_ga = gram(a_bf)
        local_gb = gram(b_bf)
        gram_a, gram_b = lax.psum((local_ga, local_gb), ("row", "col"))
        gram_c = gram(c_bf)

        def own_step(slot, carry):
            total_a, total_b, total_c = carry
            brick = lax.dynamic_index_in_dim(slab, slot, 0, keepdims=False)
            spot = lax.dynamic_index_in_dim(places, slot, 1, keepdims=False)
            i_low = spot[0] * tile
            j_low = spot[1] * tile
            k_low = spot[2] * depth
            a_tile = lax.dynamic_slice_in_dim(a_range, i_low, tile, 0)
            b_tile = lax.dynamic_slice_in_dim(b_range, j_low, tile, 0)
            c_rows = lax.dynamic_slice_in_dim(c_bf, k_low, depth, 0)
            delta_a, delta_b, delta_c = brick_terms(brick, a_tile, b_tile, c_rows)
            return (
                add_tile(total_a, delta_a, i_low),
                add_tile(total_b, delta_b, j_low),
                add_tile(total_c, delta_c, k_low),
            )

        empty = (
            jnp.zeros(a_range.shape, jnp.float32),
            jnp.zeros(b_range.shape, jnp.float32),
            jnp.zeros(c_bf.shape, jnp.float32),
        )
        drive_a, drive_b, drive_c = lax.fori_loop(0, own, own_step, empty)
        mine_a = lax.psum_scatter(drive_a, "col", scatter_dimension=0, tiled=True)
        mine_b = lax.psum_scatter(drive_b, "row", scatter_dimension=0, tiled=True)
        summed_c = lax.psum(drive_c, ("row", "col"))
        new_c = project(state_c, gram_a * gram_b, summed_c, step_sizes[sweep, 2])
        new_a = project(state_a, gram_b * gram_c, mine_a, step_sizes[sweep, 0])
        new_b = project(state_b, gram_a * gram_c, mine_b, step_sizes[sweep, 1])
        state_a, state_b, state_c = (new_a, new_b, new_c)
    return (state_a[None], state_b[None], state_c)


def solution(mesh):
    placed = (
        P("row", "col", None, None, None, None),
        P("row", "col", None, None),
        P("row", "col"),
        P(),
        P("row", "col", None),
        P("col", "row", None),
        P(),
    )
    return jax.shard_map(
        shards,
        mesh=mesh,
        in_specs=placed,
        out_specs=(P("row", "col", None), P("col", "row", None), P()),
        check_vma=False,
    )
```

profile of v0, /device:TPU:1, one launch (start us, length us, event | category | flops | bytes accessed | tf_op | source)
XLA Modules:
  0.0 787.4 jit_solution(12172388770690643116)
XLA Ops:
  8.1 1.7 fusion.61
  9.8 0.7 bitcast_convert_fusion
  10.5 1.7 fusion.59
  12.2 0.7 bitcast_convert_fusion.1
  13.0 37.2 %all_gather.12 = bf16[256,256]{1,0:T(8,128)(2,1)S(1)} all-gather(bf16[16,256]{1,0:T(8,128)(2,1)S(1)} %bitcast_convert_fusion), channel_id=1, replica_groups=mesh['row'=16,'col'=32] {'row'}, dimensions={0}, use_global_device_ids=true | all-gather | bytes 139264 | tf_op jit(solution)/shard_map/all_gather | solution.py:53
  50.2 65.9 %all_gather.13 = bf16[512,256]{1,0:T(8,128)(2,1)S(1)} all-gather(bf16[16,256]{1,0:T(8,128)(2,1)S(1)} %bitcast_convert_fusion.1), channel_id=1, replica_groups=mesh['row'=16,'col'=32] {'col'}, dimensions={0}, use_global_device_ids=true | all-gather | bytes 270336 | tf_op jit(solution)/shard_map/all_gather | solution.py:52
  117.0 1.0 copy.16
  120.2 272.3 %all-reduce.7.cloned.1.call-done = (f32[256,256]{1,0:T(8,128)}, f32[256,256]{1,0:T(8,128)}, f32[512,256]{0,1:T(8,128)}) async-done(((f32[256,256]{1,0:T(8,128)}, f32[256,256]{1,0:T(8,128)}, f32[512,256]{0,1:T(8,128)}), (f32[256,256]{1,0:T(8,128)}, f32[256,256]{1,0:T(8,128)}, f32[512,256]{0,1:T(8,128)})) %all-reduce.7.cloned.1.call-update) | async-done | bytes 1048592 | tf_op jit(solution)/shard_map/psum | solution.py:56
  392.5 1.5 abs_reduce_fusion.3
  394.0 1.7 fusion.69
  396.0 1.6 fusion.68
  397.6 35.6 %all_gather.14 = bf16[256,256]{1,0:T(8,128)(2,1)S(1)} all-gather(bf16[16,256]{1,0:T(8,128)(2,1)S(1)} %get-tuple-element.215), channel_id=1, replica_groups=mesh['row'=16,'col'=32] {'row'}, dimensions={0}, use_global_device_ids=true | all-gather | bytes 139264 | tf_op jit(solution)/shard_map/all_gather | solution.py:53
  433.2 0.9 fusion.71
  434.1 1.6 fusion.70
  435.8 56.0 %all_gather.15 = bf16[512,256]{1,0:T(8,128)(2,1)S(1)} all-gather(bf16[16,256]{1,0:T(8,128)(2,1)S(1)} %get-tuple-element.219), channel_id=1, replica_groups=mesh['row'=16,'col'=32] {'col'}, dimensions={0}, use_global_device_ids=true | all-gather | bytes 270336 | tf_op jit(solution)/shard_map/all_gather | solution.py:52
  491.8 1.0 fusion.72
  493.5 1.0 copy.23
  495.2 0.7 reduce-scatter.9.cloned.1.call-update
  495.9 275.6 %all-reduce.5.cloned.1.call-done = (f32[256,256]{1,0:T(8,128)}, f32[256,256]{1,0:T(8,128)}, f32[512,256]{0,1:T(8,128)}) async-done(((f32[256,256]{1,0:T(8,128)}, f32[256,256]{1,0:T(8,128)}, f32[512,256]{0,1:T(8,128)}), (f32[256,256]{1,0:T(8,128)}, f32[256,256]{1,0:T(8,128)}, f32[512,256]{0,1:T(8,128)})) %all-reduce.5.cloned.1.call-update) | async-done | bytes 1048592 | tf_op jit(solution)/shard_map/psum | solution.py:56
  771.5 1.5 abs_reduce_fusion
  773.0 1.4 fusion.30
  774.4 1.0 copy.25
  775.4 2.2 fusion.35
  777.6 2.1 fusion.40
  (62 shorter events, 4.5 us)
Async XLA Ops:
  8.0 42.2 %copy-start.4 = (f32[512,256]{1,0:T(8,128)S(1)}, f32[512,256]{1,0:T(8,128)}, u32[]{:S(2)}) copy-start(f32[512,256]{1,0:T(8,128)} %param.17) | copy-start | bytes 1572868
  8.0 384.4 %all-reduce.7.cloned.1.call-start = ((), (), s32[]{:S(2)}) async-start(), calls=%async_computation.9 | async-start | bytes 2097152 | tf_op jit(solution)/shard_map/psum | solution.py:56
  50.2 66.1 %copy-start.16 = (s32[1,1,3,2]{2,3,1,0:T(2,128)S(1)}, s32[1,1,3,2]{2,3,1,0:T(2,128)}, u32[]{:S(2)}) copy-start(s32[1,1,3,2]{2,3,1,0:T(2,128)} %param.12) | copy-start | bytes 76
  117.0 1.1 copy-start.1
  117.0 1.1 copy-start.3
  118.1 1.4 copy-start.12
  118.1 277.9 %reduce-scatter.7.cloned.1.call-start = ((), (), s32[]{:S(2)}) async-start(), calls=%async_computation.5 | async-start | bytes 278528 | tf_op jit(solution)/shard_map/reduce_scatter | solution.py:83
  118.6 315.5 %reduce-scatter.5.cloned.1.call-start = ((), (), s32[]{:S(2)}) async-start(), calls=%async_computation.4 | async-start | bytes 540672 | tf_op jit(solution)/shard_map/reduce_scatter | solution.py:82
  119.2 652.2 %all-reduce.5.cloned.1.call-start = ((), (), s32[]{:S(2)}) async-start(), calls=%async_computation.8 | async-start | bytes 2097152 | tf_op jit(solution)/shard_map/psum | solution.py:56
  392.5 1.5 copy-start.5
  392.5 1.5 copy-start.6
  392.5 1.5 copy-start.9
  394.0 2.0 copy-start.10
  395.8 38.4 %copy-start.11 = (f32[1,16,256]{2,1,0:T(8,128)S(1)}, f32[1,16,256]{2,1,0:T(8,128)}, u32[]{:S(2)}) copy-start(f32[1,16,256]{2,1,0:T(8,128)} %param.15) | copy-start | bytes 49156
  493.5 1.1 copy-start
  493.5 1.1 copy-start.2
  494.6 280.8 %reduce-scatter.11.cloned.1.call-start = ((), (), s32[]{:S(2)}) async-start(), calls=%async_computation.7 | async-start | bytes 278528 | tf_op jit(solution)/shard_map/reduce_scatter | solution.py:83
  495.2 282.5 %reduce-scatter.9.cloned.1.call-start = ((), (), s32[]{:S(2)}) async-start(), calls=%async_computation.6 | async-start | bytes 540672 | tf_op jit(solution)/shard_map/reduce_scatter | solution.py:82
  771.5 1.5 copy-start.7
  771.5 1.5 copy-start.8
  771.5 1.5 copy-start.15
Sparse Core Ops, SparseCore 0:
  118.2 274.2 all-reduce.6
  494.7 276.7 all-reduce.4
Sparse Core Ops, SparseCore 1:
  121.3 71.1 reduce-scatter.6
  197.0 130.4 reduce-scatter.4
  497.8 73.3 reduce-scatter.10
  575.8 130.9 reduce-scatter.8
where the time goes:
time: 789 us; the launch traced here: 787 us
  waiting for transfers between devices  550 us (70%)
  blocking collectives  195 us (25%)
  matrix products  19 us (2%)
  between operations  16 us (2%)
    psum x2, waiting for transfers between devices, shards(): gram_a, gram_b = lax.psum((local_ga, local_gb), ('row', 'col'))  548 us
    all_gather x2, blocking collectives, shards(): a_range = lax.all_gather(a_bf, 'col', axis=0, tiled=True)  122 us
    all_gather x2, blocking collectives, shards(): b_range = lax.all_gather(b_bf, 'row', axis=0, tiled=True)  72.9 us
  transfers between devices with their start and end apart: 6, of which 2 were waited for; matrix products, arithmetic and copies ran while one was open for 2% of the time, Pallas kernels for 0%

commit v1 on v0

v1 whole, which is shorter than its diff:
```python
import jax
import jax.numpy as jnp
from jax import lax
from jax.sharding import PartitionSpec as P

LANES = 128
HIGH = lax.Precision.HIGHEST


def swap(x, axis):
    return lax.all_to_all(x, axis, 0, 0, tiled=True)


def spread(x, peers):
    return lax.optimization_barrier(jnp.broadcast_to(x[None], (peers,) + x.shape))


def pad_lanes(x):
    short = -x.shape[-1] % LANES
    return jnp.pad(x, [(0, 0)] * (x.ndim - 1) + [(0, short)])


def fold(x):
    lead, (m, n) = x.shape[:-2], x.shape[-2:]
    parts = [x[..., t * LANES : (t + 1) * LANES] for t in range(n // LANES)]
    return jnp.concatenate(parts, axis=-2)


def unfold(x, n):
    tiles = n // LANES
    m = x.shape[-2] // tiles
    return jnp.concatenate([x[..., t * m : (t + 1) * m, :] for t in range(tiles)], axis=-1)


def take(x, sizes):
    out, at = [], 0
    for size in sizes:
        out.append(x[:, at : at + size])
        at += size
    return out


def gram(values):
    return sum(
        lax.dot_general(v, v, (((1,), (1,)), ((), ())), preferred_element_type=jnp.float32)
        for v in values
    )


def bump(state, hess, full, drive, rate):
    scale = jnp.sum(jnp.abs(hess), axis=1) + 1e-06
    push = jnp.stack(
        [jnp.dot(hess, f, precision=HIGH, preferred_element_type=jnp.float32) for f in full]
    )
    return jnp.maximum(state - rate * (push - drive) / scale[None, :, None], 0.0)


def brick_terms(brick, a_tile, b_tile, c_rows):
    c_wide = c_rows.astype(jnp.float32)[:, None, :]
    wide = jnp.einsum("kij,qj->kiq", brick, b_tile, preferred_element_type=jnp.float32)
    along_a = jnp.sum(wide * c_wide, axis=0)
    deep = jnp.einsum("kij,qi->kjq", brick, a_tile, preferred_element_type=jnp.float32)
    along_b = jnp.sum(deep * c_wide, axis=0)
    along_c = jnp.sum(deep * b_tile.T.astype(jnp.float32)[None, :, :], axis=1)
    return along_a.T, along_b.T, along_c.T


def shards(bricks, brick_coords, brick_counts, step_sizes, init_a, init_b, init_c):
    nr, nc = lax.axis_size("row"), lax.axis_size("col")
    row, col = lax.axis_index("row"), lax.axis_index("col")
    slab, places, own = bricks[0, 0], brick_coords[0, 0], brick_counts[0, 0]
    slots, depth, tile, _ = slab.shape
    sweeps = step_sizes.shape[0]
    rank = init_a.shape[-1]
    own_a, own_b = init_a.shape[1], init_b.shape[1]
    tiles_a, tiles_b = own_a * nc // tile, own_b * nr // tile
    length = init_c.shape[0]
    layers = length // depth
    qa, qb, ka = rank // nc, rank // nr, length // nr
    f32, bf16 = jnp.float32, jnp.bfloat16
    half = rank // LANES

    live = lax.iota(jnp.int32, slots) < own
    spots = jnp.where(live[None, :], places, 0)
    mine = pad_lanes(jnp.where(live[None, :], places, -1).astype(f32).reshape(1, -1))
    mine = jnp.broadcast_to(mine, (8, LANES))

    state_a, state_b = init_a[0], init_b[0]
    c_bf = init_c.astype(bf16)
    crow_t = lax.dynamic_slice_in_dim(init_c, row * ka, ka, 0).T

    for sweep in range(sweeps):
        first = sweep == 0
        if first:
            got = swap(spread(jnp.concatenate([fold(state_a), mine], 0), nc), "col")
            rows, spots_col = take(got, [own_a * half, 8])
            rows = unfold(rows, rank).reshape(tiles_a, tile, rank)
            at3 = jnp.swapaxes(rows, 1, 2)
            spots_col = spots_col[:, 0, : 3 * slots].reshape(nc, 3, slots).astype(jnp.int32)
        else:
            send = jnp.concatenate([new_a.reshape(-1, LANES), fold(pad_lanes(new_c))], 0)
            got = swap(spread(send, nc), "col")
            chunk, c_got = take(got, [tiles_a * qa, send.shape[0] - tiles_a * qa])
            at3 = jnp.swapaxes(chunk.reshape(nc, tiles_a, qa, tile), 0, 1).reshape(tiles_a, rank, tile)
            crow_t = unfold(c_got, new_c.shape[1] + -new_c.shape[1] % LANES)[:, :, :ka].reshape(rank, ka)
        at3_bf = at3.astype(bf16)
        gram_a = gram(at3_bf)
        slice_a = lax.dynamic_slice_in_dim(gram_a, col * qa, qa, 0)
        if first:
            send = jnp.concatenate([fold(state_b), fold(slice_a)], 0)
            got = swap(spread(send, nr), "row")
            rows, s_got = take(got, [own_b * half, qa * half])
            rows = unfold(rows, rank).reshape(tiles_b, tile, rank)
            bt3 = jnp.swapaxes(rows, 1, 2)
        else:
            send = jnp.concatenate(
                [new_b.reshape(-1, LANES), fold(slice_a), fold(crow_t.T)], 0
            )
            got = swap(spread(send, nr), "row")
            chunk, s_got, c_got = take(got, [tiles_b * qb, qa * half, ka * half])
            bt3 = jnp.swapaxes(chunk.reshape(nr, tiles_b, qb, tile), 0, 1).reshape(tiles_b, rank, tile)
            c_bf = unfold(c_got, rank).reshape(length, rank).astype(bf16)
        bt3_bf = bt3.astype(bf16)
        gram_b = gram(bt3_bf)
        sa_c = unfold(jnp.sum(s_got, axis=0), rank)
        gram_c = lax.dot_general(
            c_bf, c_bf, (((0,), (0,)), ((), ())), preferred_element_type=f32
        )
        parts_a, parts_c = [], []
        drive_b = jnp.zeros((tiles_b, rank, tile), f32)
        for slot in range(slots):
            ti, tj, tk = spots[0, slot], spots[1, slot], spots[2, slot]
            a_tile = lax.dynamic_index_in_dim(at3_bf, ti, 0, keepdims=False)
            b_tile = lax.dynamic_index_in_dim(bt3_bf, tj, 0, keepdims=False)
            c_rows = lax.dynamic_slice_in_dim(c_bf, tk * depth, depth, 0)
            da, db, dc = brick_terms(slab[slot], a_tile, b_tile, c_rows)
            parts_a.append(da)
            parts_c.append(dc)
            here = (lax.iota(jnp.int32, tiles_b) == tj) & live[slot]
            drive_b = drive_b + jnp.where(here[:, None, None], db[None], 0.0)
        pieces = [p.reshape(nc, qa, tile) for p in parts_a]
        pieces.append(fold(gram_b.reshape(nc, qa, rank)))
        pieces.append(pad_lanes(jnp.concatenate(parts_c, axis=1)).reshape(nc, qa, LANES))
        got = swap(jnp.concatenate(pieces, axis=1), "col")
        *a_got, s_got, c_got = take(got, [qa] * slots + [qa * half, qa])
        sb_c = unfold(jnp.sum(s_got, axis=0), rank)
        drive_a = jnp.stack(
            [
                sum(
                    jnp.sum(jnp.where((spots_col[:, 0, m] == t)[:, None, None], a_got[m], 0.0), axis=0)
                    for m in range(slots)
                )
                for t in range(tiles_a)
            ]
        )
        onehot = (spots_col[:, 2, :, None] == lax.iota(jnp.int32, layers)).astype(f32)
        c_got = c_got[:, :, : slots * depth].reshape(nc, qa, slots, depth)
        drive_c = jnp.einsum("sqmk,smb->qbk", c_got, onehot, precision=HIGH).reshape(qa, length)
        pieces = [d.reshape(nr, qb, tile) for d in drive_b]
        pieces.append(fold(gram_a.reshape(nr, qb, rank)))
        send_c = jnp.swapaxes(pad_lanes(drive_c.reshape(qa, nr, ka)), 0, 1)
        pieces.append(fold(send_c))
        got = swap(jnp.concatenate(pieces, axis=1), "row")
        b_got, s_got, c_got = take(got, [qb * tiles_b, qb * half, fold(send_c).shape[1]])
        mine_b = jnp.sum(b_got, axis=0).reshape(tiles_b, qb, tile)
        sa_r = unfold(jnp.sum(s_got, axis=0), rank)
        mine_c = unfold(jnp.sum(c_got, axis=0), send_c.shape[-1])[:, :ka]
        sc_c = lax.dynamic_slice_in_dim(gram_c, col * qa, qa, 0)
        sc_r = lax.dynamic_slice_in_dim(gram_c, row * qb, qb, 0)
        old_a = lax.dynamic_slice_in_dim(at3, col * qa, qa, 1)
        old_b = lax.dynamic_slice_in_dim(bt3, row * qb, qb, 1)
        old_c = lax.dynamic_slice_in_dim(crow_t, col * qa, qa, 0)
        new_a = bump(old_a, sb_c * sc_c, at3, drive_a, step_sizes[sweep, 0])
        new_b = bump(old_b, sa_r * sc_r, bt3, mine_b, step_sizes[sweep, 1])
        new_c = bump(old_c[None], sa_c * sb_c, crow_t[None], mine_c[None], step_sizes[sweep, 2])[0]
    per_a = tile // own_a
    cut = new_a.reshape(tiles_a, qa, per_a, own_a).transpose(0, 2, 1, 3).reshape(nc, qa, own_a)
    cut = pad_lanes(jnp.concatenate([cut, jnp.broadcast_to(new_c[None], (nc, qa, ka))], axis=2))
    got = unfold(swap(fold(cut), "col"), cut.shape[-1])
    out_a = got[:, :, :own_a].reshape(rank, own_a).T
    rows_c = got[:, :, own_a : own_a + ka].reshape(rank, ka).T
    per_b = tile // own_b
    cut = new_b.reshape(tiles_b, qb, per_b, own_b).transpose(0, 2, 1, 3).reshape(nr, qb, own_b)
    cut = fold(pad_lanes(cut))
    everyone = jnp.broadcast_to(fold(rows_c)[None], (nr, ka * half, LANES))
    got = swap(jnp.concatenate([cut, everyone], axis=1), "row")
    b_got, c_got = take(got, [cut.shape[1], ka * half])
    out_b = unfold(b_got, own_b + -own_b % LANES)[:, :, :own_b].reshape(rank, own_b).T
    out_c = unfold(c_got, rank).reshape(length, rank)
    return out_a[None], out_b[None], out_c


def solution(mesh):
    placed = (
        P("row", "col", None, None, None, None),
        P("row", "col", None, None),
        P("row", "col"),
        P(),
        P("row", "col", None),
        P("col", "row", None),
        P(),
    )
    return jax.shard_map(
        shards,
        mesh=mesh,
        in_specs=placed,
        out_specs=(P("row", "col", None), P("col", "row", None), P()),
        check_vma=False,
    )
```

time: 789 us -> 316 us (0.40)
  waiting for transfers between devices: 550 us -> 131 us
  blocking collectives: 195 us -> 0 us
  starting transfers between devices: 0.25 us -> 74.8 us
  local copies, waits for them, and re-layouts: 4.3 us -> 46 us
  other arithmetic: 1.48 us -> 26.1 us
    psum x2 -> x0, waiting for transfers between devices: 548 us -> none  [shards(): gram_a, gram_b = lax.psum((local_ga, local_gb), ('row', 'col'))]
    all_gather x4 -> x0, blocking collectives: 195 us -> none  [the longest x2 122 us: shards(): a_range = lax.all_gather(a_bf, 'col', axis=0, tiled=True)]
    all_to_all x0 -> x10, waiting for transfers between devices: none -> 131 us  [swap(): return lax.all_to_all(x, axis, 0, 0, tiled=True)]
    all_to_all x0 -> x10, starting transfers between devices: none -> 74.8 us  [swap(): return lax.all_to_all(x, axis, 0, 0, tiled=True)]
    unnamed x32 -> x90, local copies, waits for them, and re-layouts: 1.26 us -> 13.9 us
    reduce_sum x0 -> x17, other arithmetic: none -> 11 us  [the longest x3 5.6 us: brick_terms(): along_c = jnp.sum(deep * b_tile.T.astype(jnp.float32)[None, :, :], axis=1)]
    dot_general x0 -> x4, local copies, waits for them, and re-layouts: none -> 8.62 us  [brick_terms(): jnp.einsum('kij,qi->kjq', brick, a_tile, preferred_element_type=jnp.float32)]
    dot_general x12 -> x34, matrix products: 19 us -> 17.5 us  [the longest x4 7.1 us: brick_terms(): jnp.einsum('kij,qj->kiq', brick, b_tile, preferred_element_type=jnp.float32)]
  transfers between devices with their start and end apart: 6 -> 10, of which waited for: 2 -> 9; matrix products, arithmetic and copies ran while one was open for 2% -> 14% of each run, Pallas kernels for 0% -> 0%
where the time goes in v1:
time: 316 us; the launch traced here: 313 us
  waiting for transfers between devices  131 us (41%)
  starting transfers between devices  74.8 us (24%)
  local copies, waits for them, and re-layouts  46 us (15%)
  other arithmetic  26.1 us (8%)
  matrix products  24.2 us (8%)
  between operations  11.6 us (4%)
    all_to_all x10, waiting for transfers between devices, swap(): return lax.all_to_all(x, axis, 0, 0, tiled=True)  131 us
    all_to_all x10, starting transfers between devices, swap(): return lax.all_to_all(x, axis, 0, 0, tiled=True)  74.8 us
    unnamed x90, local copies, waits for them, and re-layouts  13.9 us
    dot_general x4, local copies, waits for them, and re-layouts, brick_terms(): jnp.einsum('kij,qi->kjq', brick, a_tile, preferred_element_type=jnp.float32)  8.62 us
    dot_general x4, matrix products, brick_terms(): jnp.einsum('kij,qj->kiq', brick, b_tile, preferred_element_type=jnp.float32)  7.1 us
    unnamed x4, matrix products  6.68 us
  transfers between devices with their start and end apart: 10, of which 9 were waited for; matrix products, arithmetic and copies ran while one was open for 14% of the time, Pallas kernels for 0%

profile of v1, /device:TPU:1, one launch (start us, length us, event | category | flops | bytes accessed | tf_op | source)
XLA Modules:
  0.0 313.4 jit_solution(4921443825652727031)
XLA Ops:
  3.9 17.2 %all-to-all-start = ((f32[32,40,128]{2,1,0:T(8,128)}), f32[32,40,128]{2,1,0:T(8,128)S(1)}, u32[]{:S(2)}, u32[]{:S(2)}) async-start(f32[32,40,128]{2,1,0:T(8,128)} %broadcast_in_dim.270), calls=%async_computation | async-start | bytes 1310720 | tf_op jit(solution)/shard_map/all_to_all | solution.py:11
  34.9 3.2 %compare_and_fusion = (pred[2]{0:T(512)(128)(4,1)}, pred[2]{0:T(512)(128)(4,1)}) fusion(pred[]{:T(512)} %bitcast.78, s32[]{:T(128)} %bitcast.23, pred[]{:T(512)} %bitcast.76, s32[]{:T(128)} %bitcast.15), kind=kLoop, calls=%fused_computation.245 | loop fusion | flops 8 | bytes 14 | tf_op jit(solution)/shard_map/and | solution.py:139
  43.1 9.4 %all-to-all-start.1 = ((f32[16,48,128]{2,1,0:T(8,128)}), f32[16,48,128]{2,1,0:T(8,128)}, u32[]{:S(2)}, u32[]{:S(2)}) async-start(f32[16,48,128]{2,1,0:T(8,128)} %broadcast_in_dim.271), calls=%async_computation.1 | async-start | bytes 786432 | tf_op jit(solution)/shard_map/all_to_all | solution.py:11
  57.9 2.9 copy.200
  62.0 3.0 all-to-all-done.1
  69.9 2.5 fusion.11
  75.4 2.0 fusion.10
  82.2 3.0 fusion.6
  86.0 9.1 %all-to-all-start.2 = ((f32[32,40,128]{2,1,0:T(8,128)}), f32[32,40,128]{2,1,0:T(8,128)S(1)}, u32[]{:S(2)}, u32[]{:S(2)}) async-start(f32[32,40,128]{2,1,0:T(8,128)} %bitcast_dynamic-update-slice_fusion.5), calls=%async_computation.2 | async-start | bytes 1310720 | tf_op jit(solution)/shard_map/all_to_all | solution.py:11
  98.9 17.9 %all-to-all-done.2 = f32[32,40,128]{2,1,0:T(8,128)S(1)} async-done(((f32[32,40,128]{2,1,0:T(8,128)}), f32[32,40,128]{2,1,0:T(8,128)S(1)}, u32[]{:S(2)}, u32[]{:S(2)}) %all-to-all-start.2) | async-done | bytes 655392 | tf_op jit(solution)/shard_map/all_to_all | solution.py:11
  119.8 4.7 %all-to-all-start.3 = ((f32[16,72,128]{2,1,0:T(8,128)}), f32[16,72,128]{2,1,0:T(8,128)S(1)}, u32[]{:S(2)}, u32[]{:S(2)}) async-start(f32[16,72,128]{2,1,0:T(8,128)} %copy_dynamic-update-slice_fusion), calls=%async_computation.3 | async-start | bytes 1179648 | tf_op jit(solution)/shard_map/all_to_all | solution.py:11
  125.7 16.0 %all-to-all-done.3 = f32[16,72,128]{2,1,0:T(8,128)S(1)} async-done(((f32[16,72,128]{2,1,0:T(8,128)}), f32[16,72,128]{2,1,0:T(8,128)S(1)}, u32[]{:S(2)}, u32[]{:S(2)}) %all-to-all-start.3) | async-done | bytes 589856 | tf_op jit(solution)/shard_map/all_to_all | solution.py:11
  144.2 6.3 %all-to-all-start.4 = ((f32[32,40,128]{2,1,0:T(8,128)}), f32[32,40,128]{2,1,0:T(8,128)S(1)}, u32[]{:S(2)}, u32[]{:S(2)}) async-start(f32[32,40,128]{2,1,0:T(8,128)} %broadcast_in_dim.295), calls=%async_computation.4 | async-start | bytes 1310720 | tf_op jit(solution)/shard_map/all_to_all | solution.py:11
  152.9 18.8 %all-to-all-done.4 = f32[32,40,128]{2,1,0:T(8,128)S(1)} async-done(((f32[32,40,128]{2,1,0:T(8,128)}), f32[32,40,128]{2,1,0:T(8,128)S(1)}, u32[]{:S(2)}, u32[]{:S(2)}) %all-to-all-start.4) | async-done | bytes 655392 | tf_op jit(solution)/shard_map/all_to_all | solution.py:11
  174.5 4.7 %all-to-all-start.5 = ((f32[16,112,128]{2,1,0:T(8,128)}), f32[16,112,128]{2,1,0:T(8,128)}, u32[]{:S(2)}, u32[]{:S(2)}) async-start(f32[16,112,128]{2,1,0:T(8,128)} %broadcast_in_dim.296), calls=%async_computation.5 | async-start | bytes 1835008 | tf_op jit(solution)/shard_map/all_to_all | solution.py:11
  188.8 14.7 %all-to-all-done.5 = f32[16,112,128]{2,1,0:T(8,128)} async-done(((f32[16,112,128]{2,1,0:T(8,128)}), f32[16,112,128]{2,1,0:T(8,128)}, u32[]{:S(2)}, u32[]{:S(2)}) %all-to-all-start.5) | async-done | bytes 917536 | tf_op jit(solution)/shard_map/all_to_all | solution.py:11
  215.0 7.4 %all-to-all-start.6 = ((f32[32,40,128]{2,1,0:T(8,128)}), f32[32,40,128]{2,1,0:T(8,128)S(1)}, u32[]{:S(2)}, u32[]{:S(2)}) async-start(f32[32,40,128]{2,1,0:T(8,128)} %bitcast_dynamic-update-slice_fusion.4), calls=%async_computation.6 | async-start | bytes 1310720 | tf_op jit(solution)/shard_map/all_to_all | solution.py:11
  226.4 16.4 %all-to-all-done.6 = f32[32,40,128]{2,1,0:T(8,128)S(1)} async-done(((f32[32,40,128]{2,1,0:T(8,128)}), f32[32,40,128]{2,1,0:T(8,128)S(1)}, u32[]{:S(2)}, u32[]{:S(2)}) %all-to-all-start.6) | async-done | bytes 655392 | tf_op jit(solution)/shard_map/all_to_all | solution.py:11
  245.0 4.8 %all-to-all-start.7 = ((f32[16,72,128]{2,1,0:T(8,128)}), f32[16,72,128]{2,1,0:T(8,128)S(1)}, u32[]{:S(2)}, u32[]{:S(2)}) async-start(f32[16,72,128]{2,1,0:T(8,128)} %bitcast_dynamic-update-slice_fusion.6), calls=%async_computation.7 | async-start | bytes 1179648 | tf_op jit(solution)/shard_map/all_to_all | solution.py:11
  251.8 15.2 %all-to-all-done.7 = f32[16,72,128]{2,1,0:T(8,128)S(1)} async-done(((f32[16,72,128]{2,1,0:T(8,128)}), f32[16,72,128]{2,1,0:T(8,128)S(1)}, u32[]{:S(2)}, u32[]{:S(2)}) %all-to-all-start.7) | async-done | bytes 589856 | tf_op jit(solution)/shard_map/all_to_all | solution.py:11
  268.7 7.7 %all-to-all-start.8 = ((f32[32,8,128]{2,1,0:T(8,128)}), f32[32,8,128]{2,1,0:T(8,128)S(1)}, u32[]{:S(2)}, u32[]{:S(2)}) async-start(f32[32,8,128]{2,1,0:T(8,128)} %select_maximum_fusion.1), calls=%async_computation.8 | async-start | bytes 262144 | tf_op jit(solution)/shard_map/all_to_all | solution.py:11
  277.6 10.9 %all-to-all-done.8 = f32[32,8,128]{2,1,0:T(8,128)S(1)} async-done(((f32[32,8,128]{2,1,0:T(8,128)}), f32[32,8,128]{2,1,0:T(8,128)S(1)}, u32[]{:S(2)}, u32[]{:S(2)}) %all-to-all-start.8) | async-done | bytes 131104 | tf_op jit(solution)/shard_map/all_to_all | solution.py:11
  289.7 3.6 %all-to-all-start.9 = ((f32[16,80,128]{2,1,0:T(8,128)}), f32[16,80,128]{2,1,0:T(8,128)S(1)}, u32[]{:S(2)}, u32[]{:S(2)}) async-start(f32[16,80,128]{2,1,0:T(8,128)} %select_maximum_fusion), calls=%async_computation.9 | async-start | bytes 1310720 | tf_op jit(solution)/shard_map/all_to_all | solution.py:11
  294.0 17.8 %all-to-all-done.9 = f32[16,80,128]{2,1,0:T(8,128)S(1)} async-done(((f32[16,80,128]{2,1,0:T(8,128)}), f32[16,80,128]{2,1,0:T(8,128)S(1)}, u32[]{:S(2)}, u32[]{:S(2)}) %all-to-all-start.9) | async-done | bytes 655392 | tf_op jit(solution)/shard_map/all_to_all | solution.py:11
  (270 shorter events, 82.6 us)
Async XLA Ops:
  0.6 28.4 %copy-start.8 = (f32[512,256]{1,0:T(8,128)S(1)}, f32[512,256]{1,0:T(8,128)}, u32[]{:S(2)}) copy-start(f32[512,256]{1,0:T(8,128)} %param.13) | copy-start | bytes 1572868
  3.9 36.4 %all-to-all-start = ((f32[32,40,128]{2,1,0:T(8,128)}), f32[32,40,128]{2,1,0:T(8,128)S(1)}, u32[]{:S(2)}, u32[]{:S(2)}) async-start(f32[32,40,128]{2,1,0:T(8,128)} %broadcast_in_dim.270), calls=%async_computation | async-start | bytes 1310720 | tf_op jit(solution)/shard_map/all_to_all | solution.py:11
  43.1 21.9 %all-to-all-start.1 = ((f32[16,48,128]{2,1,0:T(8,128)}), f32[16,48,128]{2,1,0:T(8,128)}, u32[]{:S(2)}, u32[]{:S(2)}) async-start(f32[16,48,128]{2,1,0:T(8,128)} %broadcast_in_dim.271), calls=%async_computation.1 | async-start | bytes 786432 | tf_op jit(solution)/shard_map/all_to_all | solution.py:11
  86.0 30.8 %all-to-all-start.2 = ((f32[32,40,128]{2,1,0:T(8,128)}), f32[32,40,128]{2,1,0:T(8,128)S(1)}, u32[]{:S(2)}, u32[]{:S(2)}) async-start(f32[32,40,128]{2,1,0:T(8,128)} %bitcast_dynamic-update-slice_fusion.5), calls=%async_computation.2 | async-start | bytes 1310720 | tf_op jit(solution)/shard_map/all_to_all | solution.py:11
  96.8 27.7 %copy-start.19 = (pred[32]{0:T(512)(128)(4,1)S(1)}, pred[32]{0:T(512)(128)(4,1)}, u32[]{:S(2)}) copy-start(pred[32]{0:T(512)(128)(4,1)} %get-tuple-element.109) | copy-start | bytes 100
  96.8 27.7 %copy-start.20 = (pred[32]{0:T(512)(128)(4,1)S(1)}, pred[32]{0:T(512)(128)(4,1)}, u32[]{:S(2)}) copy-start(pred[32]{0:T(512)(128)(4,1)} %get-tuple-element.110) | copy-start | bytes 100
  96.8 27.7 %copy-start.21 = (pred[32]{0:T(512)(128)(4,1)S(1)}, pred[32]{0:T(512)(128)(4,1)}, u32[]{:S(2)}) copy-start(pred[32]{0:T(512)(128)(4,1)} %get-tuple-element.111) | copy-start | bytes 100
  96.8 27.7 %copy-start.22 = (pred[32]{0:T(512)(128)(4,1)S(1)}, pred[32]{0:T(512)(128)(4,1)}, u32[]{:S(2)}) copy-start(pred[32]{0:T(512)(128)(4,1)} %get-tuple-element.112) | copy-start | bytes 100
  96.8 27.7 %copy-start.24 = (pred[32]{0:T(512)(128)(4,1)S(1)}, pred[32]{0:T(512)(128)(4,1)}, u32[]{:S(2)}) copy-start(pred[32]{0:T(512)(128)(4,1)} %get-tuple-element.113) | copy-start | bytes 100
  96.8 27.7 %copy-start.26 = (pred[32]{0:T(512)(128)(4,1)S(1)}, pred[32]{0:T(512)(128)(4,1)}, u32[]{:S(2)}) copy-start(pred[32]{0:T(512)(128)(4,1)} %get-tuple-element.114) | copy-start | bytes 100
  96.8 27.7 %copy-start.28 = (pred[32]{0:T(512)(128)(4,1)S(1)}, pred[32]{0:T(512)(128)(4,1)}, u32[]{:S(2)}) copy-start(pred[32]{0:T(512)(128)(4,1)} %get-tuple-element.115) | copy-start | bytes 100
  96.9 27.7 %copy-start.30 = (pred[32]{0:T(512)(128)(4,1)S(1)}, pred[32]{0:T(512)(128)(4,1)}, u32[]{:S(2)}) copy-start(pred[32]{0:T(512)(128)(4,1)} %get-tuple-element.116) | copy-start | bytes 100
  98.2 26.8 %copy-start.13 = (f32[4,128,8]{1,2,0:T(8,128)S(1)}, f32[4,128,8]{1,2,0:T(8,128)}, u32[]{:S(2)}) copy-start(f32[4,128,8]{1,2,0:T(8,128)} %copy.240) | copy-start | bytes 49156
  98.2 43.5 %copy-start.16 = (f32[32,8]{0,1:T(8,128)S(1)}, f32[32,8]{0,1:T(8,128)}, u32[]{:S(2)}) copy-start(f32[32,8]{0,1:T(8,128)} %copy.242) | copy-start | bytes 3076
  119.8 21.9 %all-to-all-start.3 = ((f32[16,72,128]{2,1,0:T(8,128)}), f32[16,72,128]{2,1,0:T(8,128)S(1)}, u32[]{:S(2)}, u32[]{:S(2)}) async-start(f32[16,72,128]{2,1,0:T(8,128)} %copy_dynamic-update-slice_fusion), calls=%async_computation.3 | async-start | bytes 1179648 | tf_op jit(solution)/shard_map/all_to_all | solution.py:11
  144.2 27.5 %all-to-all-start.4 = ((f32[32,40,128]{2,1,0:T(8,128)}), f32[32,40,128]{2,1,0:T(8,128)S(1)}, u32[]{:S(2)}, u32[]{:S(2)}) async-start(f32[32,40,128]{2,1,0:T(8,128)} %broadcast_in_dim.295), calls=%async_computation.4 | async-start | bytes 1310720 | tf_op jit(solution)/shard_map/all_to_all | solution.py:11
  174.5 29.0 %all-to-all-start.5 = ((f32[16,112,128]{2,1,0:T(8,128)}), f32[16,112,128]{2,1,0:T(8,128)}, u32[]{:S(2)}, u32[]{:S(2)}) async-start(f32[16,112,128]{2,1,0:T(8,128)} %broadcast_in_dim.296), calls=%async_computation.5 | async-start | bytes 1835008 | tf_op jit(solution)/shard_map/all_to_all | solution.py:11
  215.0 27.7 %all-to-all-start.6 = ((f32[32,40,128]{2,1,0:T(8,128)}), f32[32,40,128]{2,1,0:T(8,128)S(1)}, u32[]{:S(2)}, u32[]{:S(2)}) async-start(f32[32,40,128]{2,1,0:T(8,128)} %bitcast_dynamic-update-slice_fusion.4), calls=%async_computation.6 | async-start | bytes 1310720 | tf_op jit(solution)/shard_map/all_to_all | solution.py:11
  225.7 24.1 %copy-start.27 = (pred[32]{0:T(512)(128)(4,1)S(1)}, pred[32]{0:T(512)(128)(4,1)}, u32[]{:S(2)}) copy-start(pred[32]{0:T(512)(128)(4,1)} %get-tuple-element.114) | copy-start | bytes 100
  225.7 24.1 %copy-start.29 = (pred[32]{0:T(512)(128)(4,1)S(1)}, pred[32]{0:T(512)(128)(4,1)}, u32[]{:S(2)}) copy-start(pred[32]{0:T(512)(128)(4,1)} %get-tuple-element.115) | copy-start | bytes 100
  225.7 24.1 %copy-start.31 = (pred[32]{0:T(512)(128)(4,1)S(1)}, pred[32]{0:T(512)(128)(4,1)}, u32[]{:S(2)}) copy-start(pred[32]{0:T(512)(128)(4,1)} %get-tuple-element.116) | copy-start | bytes 100
  245.0 22.0 %all-to-all-start.7 = ((f32[16,72,128]{2,1,0:T(8,128)}), f32[16,72,128]{2,1,0:T(8,128)S(1)}, u32[]{:S(2)}, u32[]{:S(2)}) async-start(f32[16,72,128]{2,1,0:T(8,128)} %bitcast_dynamic-update-slice_fusion.6), calls=%async_computation.7 | async-start | bytes 1179648 | tf_op jit(solution)/shard_map/all_to_all | solution.py:11
  268.7 19.7 %all-to-all-start.8 = ((f32[32,8,128]{2,1,0:T(8,128)}), f32[32,8,128]{2,1,0:T(8,128)S(1)}, u32[]{:S(2)}, u32[]{:S(2)}) async-start(f32[32,8,128]{2,1,0:T(8,128)} %select_maximum_fusion.1), calls=%async_computation.8 | async-start | bytes 262144 | tf_op jit(solution)/shard_map/all_to_all | solution.py:11
  289.7 22.1 %all-to-all-start.9 = ((f32[16,80,128]{2,1,0:T(8,128)}), f32[16,80,128]{2,1,0:T(8,128)S(1)}, u32[]{:S(2)}, u32[]{:S(2)}) async-start(f32[16,80,128]{2,1,0:T(8,128)} %select_maximum_fusion), calls=%async_computation.9 | async-start | bytes 1310720 | tf_op jit(solution)/shard_map/all_to_all | solution.py:11
  (20 other events, 240.7 us)

commit v2 on v1

v2 whole, which is shorter than its diff:
```python
import jax
import jax.numpy as jnp
from jax import lax
from jax.sharding import PartitionSpec as P

LANES = 128
HIGH = lax.Precision.HIGHEST


def swap(x, axis):
    return lax.all_to_all(x, axis, 0, 0, tiled=True)


def spread(x, peers):
    return lax.optimization_barrier(jnp.broadcast_to(x[None], (peers,) + x.shape))


def pad_lanes(x):
    short = -x.shape[-1] % LANES
    return jnp.pad(x, [(0, 0)] * (x.ndim - 1) + [(0, short)])


def fold(x):
    lead, (m, n) = x.shape[:-2], x.shape[-2:]
    parts = [x[..., t * LANES : (t + 1) * LANES] for t in range(n // LANES)]
    return jnp.concatenate(parts, axis=-2)


def unfold(x, n):
    tiles = n // LANES
    m = x.shape[-2] // tiles
    return jnp.concatenate([x[..., t * m : (t + 1) * m, :] for t in range(tiles)], axis=-1)


def take(x, sizes):
    out, at = [], 0
    for size in sizes:
        out.append(x[:, at : at + size])
        at += size
    return out


def gram(values):
    return lax.dot_general(
        values, values, (((0,), (0,)), ((), ())), preferred_element_type=jnp.float32
    )


def brick_terms(brick, a_tile, b_tile, c_rows):
    c_wide = c_rows.astype(jnp.float32)[:, None, :]
    wide = jnp.einsum("kij,jq->kiq", brick, b_tile, preferred_element_type=jnp.float32)
    along_a = jnp.sum(wide * c_wide, axis=0)
    deep = jnp.einsum("kij,iq->kjq", brick, a_tile, preferred_element_type=jnp.float32)
    along_b = jnp.sum(deep * c_wide, axis=0)
    along_c = jnp.sum(deep * b_tile.astype(jnp.float32)[None, :, :], axis=1)
    return along_a, along_b, along_c


def bump(state, hess, full, drive, rate):
    scale = jnp.sum(jnp.abs(hess), axis=1) + 1e-06
    push = jnp.stack(
        [jnp.dot(hess, f, precision=HIGH, preferred_element_type=jnp.float32) for f in full]
    )
    return jnp.maximum(state - rate * (push - drive) / scale[None, :, None], 0.0)


def bump_rows(state, hess, drive, rate):
    scale = jnp.sum(jnp.abs(hess), axis=1) + 1e-06
    push = jnp.dot(state, hess, precision=HIGH, preferred_element_type=jnp.float32)
    return jnp.maximum(state - rate * (push - drive) / scale[None, :], 0.0)


def lanes(x):
    return jnp.stack([x[:, t * LANES : (t + 1) * LANES] for t in range(x.shape[1] // LANES)])


def shards(bricks, brick_coords, brick_counts, step_sizes, init_a, init_b, init_c):
    nr, nc = lax.axis_size("row"), lax.axis_size("col")
    col = lax.axis_index("col")
    slab, places, own = bricks[0, 0], brick_coords[0, 0], brick_counts[0, 0]
    slots, depth, tile, _ = slab.shape
    sweeps = step_sizes.shape[0]
    rank = init_a.shape[-1]
    own_a, own_b = init_a.shape[1], init_b.shape[1]
    tiles_a, tiles_b = own_a * nc // tile, own_b * nr // tile
    length = init_c.shape[0]
    layers, tiles_c = length // depth, length // LANES
    qa, qb = rank // nc, rank // nr
    f32, bf16 = jnp.float32, jnp.bfloat16
    half = rank // LANES

    live = lax.iota(jnp.int32, slots) < own
    spots = jnp.where(live[None, :], places, 0)
    mine = pad_lanes(jnp.where(live[None, :], places, -1).astype(f32).reshape(1, -1))
    mine = jnp.broadcast_to(mine, (8, LANES))

    state_b = init_b[0]
    c_bf = init_c.astype(bf16)

    for sweep in range(sweeps):
        b_bf = state_b.astype(bf16)
        if sweep == 0:
            got = swap(spread(jnp.concatenate([fold(init_a[0]), mine], 0), nc), "col")
            rows, spots_col = take(got, [own_a * half, 8])
            a_rows = unfold(rows, rank).reshape(tiles_a, tile, rank)
            at3 = jnp.swapaxes(a_rows, 1, 2)
            a_bf3 = a_rows.astype(bf16)
            spots_col = spots_col[:, 0, : 3 * slots].reshape(nc, 3, slots).astype(jnp.int32)
            ct3 = lanes(init_c.T)
        else:
            send = jnp.concatenate([new_a.reshape(-1, LANES), new_c.reshape(-1, LANES)], 0)
            got = swap(spread(send, nc), "col")
            chunk, c_got = take(got, [tiles_a * qa, tiles_c * qa])
            at3 = jnp.swapaxes(chunk.reshape(nc, tiles_a, qa, tile), 0, 1).reshape(tiles_a, rank, tile)
            a_bf3 = jnp.swapaxes(at3.astype(bf16), 1, 2)
            ct3 = jnp.swapaxes(c_got.reshape(nc, tiles_c, qa, LANES), 0, 1).reshape(tiles_c, rank, LANES)
            c_bf = jnp.swapaxes(ct3.astype(bf16), 1, 2).reshape(length, rank)
        a_all = a_bf3.reshape(tiles_a * tile, rank)
        gram_a = gram(a_all)
        slice_a = lax.dynamic_slice_in_dim(gram_a, col * qa, qa, 0)
        slice_a = jnp.swapaxes(slice_a.reshape(qa, nr, qb), 0, 1)
        high = lax.reduce_precision(slice_a, 8, 7)
        pair = pad_lanes(jnp.concatenate([high, slice_a - high], axis=2).astype(bf16))
        send = jnp.concatenate(
            [jnp.broadcast_to(fold(b_bf)[None], (nr, own_b * half, LANES)), fold(pair)], axis=1
        )
        got = swap(send, "row")
        b_got, s_got = take(got, [own_b * half, fold(pair).shape[1]])
        b_all = unfold(b_got, rank).reshape(tiles_b * tile, rank)
        gram_b = gram(b_all)
        s_got = unfold(s_got, pair.shape[2]).astype(f32)
        piece = jnp.sum(s_got[:, :, :qb] + s_got[:, :, qb : 2 * qb], axis=0)
        gram_c = gram(c_bf)
        parts_a, parts_c = [], []
        drive_b = jnp.zeros((tiles_b, tile, rank), f32)
        for slot in range(slots):
            ti, tj, tk = spots[0, slot], spots[1, slot], spots[2, slot]
            a_tile = lax.dynamic_index_in_dim(a_bf3, ti, 0, keepdims=False)
            b_tile = lax.dynamic_slice_in_dim(b_all, tj * tile, tile, 0)
            c_rows = lax.dynamic_slice_in_dim(c_bf, tk * depth, depth, 0)
            da, db, dc = brick_terms(slab[slot], a_tile, b_tile, c_rows)
            parts_a.append(da.T)
            parts_c.append(dc.T)
            here = (lax.iota(jnp.int32, tiles_b) == tj) & live[slot]
            drive_b = drive_b + jnp.where(here[:, None, None], db[None], 0.0)
        pieces = [p.reshape(nc, qa, tile) for p in parts_a]
        pieces.append(fold(gram_b.reshape(nc, qa, rank)))
        mixed = jnp.concatenate(parts_c, axis=1).reshape(nc, qa, slots * depth)
        mixed = jnp.concatenate([mixed, jnp.broadcast_to(piece[None], (nc, qa, qb))], axis=2)
        pieces.append(fold(pad_lanes(mixed)))
        got = swap(jnp.concatenate(pieces, axis=1), "col")
        *a_got, s_got, m_got = take(got, [qa] * slots + [qa * half, pieces[-1].shape[1]])
        sb_c = unfold(jnp.sum(s_got, axis=0), rank)
        m_got = unfold(m_got, pad_lanes(mixed).shape[2])
        drive_a = jnp.stack(
            [
                sum(
                    jnp.sum(jnp.where((spots_col[:, 0, m] == t)[:, None, None], a_got[m], 0.0), axis=0)
                    for m in range(slots)
                )
                for t in range(tiles_a)
            ]
        )
        onehot = (spots_col[:, 2, :, None] == lax.iota(jnp.int32, layers)).astype(f32)
        c_got = m_got[:, :, : slots * depth].reshape(nc, qa, slots, depth)
        drive_c = jnp.einsum("sqmk,smb->qbk", c_got, onehot, precision=HIGH).reshape(qa, length)
        strip = m_got[:, :, slots * depth : slots * depth + qb].reshape(rank, qb).T
        pieces = [
            fold(drive_b.reshape(nr, own_b, rank)),
            jnp.broadcast_to(fold(strip)[None], (nr, qb * half, LANES)),
            jnp.broadcast_to(fold(drive_c)[None], (nr, qa * tiles_c, LANES)),
        ]
        got = swap(jnp.concatenate(pieces, axis=1), "row")
        b_got, s_got, c_got = take(got, [p.shape[1] for p in pieces])
        mine_b = unfold(jnp.sum(b_got, axis=0), rank)
        sa = unfold(s_got, rank).reshape(rank, rank)
        mine_c = jnp.sum(c_got, axis=0).reshape(tiles_c, qa, LANES)
        cut = lambda x, axis=0: lax.dynamic_slice_in_dim(x, col * qa, qa, axis)
        rate = step_sizes[sweep]
        new_a = bump(cut(at3, 1), sb_c * cut(gram_c), at3, drive_a, rate[0])
        state_b = bump_rows(state_b, sa * gram_c, mine_b, rate[1])
        new_c = bump(cut(ct3, 1), cut(sa) * sb_c, ct3, mine_c, rate[2])
    per_a = tile // own_a
    own = new_a.reshape(tiles_a, qa, per_a, own_a).transpose(0, 2, 1, 3).reshape(nc, qa, own_a)
    own = fold(pad_lanes(own))
    everyone = jnp.broadcast_to(new_c.reshape(1, -1, LANES), (nc, qa * tiles_c, LANES))
    got = swap(jnp.concatenate([own, everyone], axis=1), "col")
    a_got, c_got = take(got, [own.shape[1], qa * tiles_c])
    out_a = unfold(a_got, own_a + -own_a % LANES)[:, :, :own_a].reshape(rank, own_a).T
    out_c = jnp.swapaxes(c_got.reshape(nc, tiles_c, qa, LANES), 0, 1).reshape(tiles_c, rank, LANES)
    out_c = jnp.swapaxes(out_c, 1, 2).reshape(length, rank)
    return out_a[None], state_b[None], out_c


def solution(mesh):
    placed = (
        P("row", "col", None, None, None, None),
        P("row", "col", None, None),
        P("row", "col"),
        P(),
        P("row", "col", None),
        P("col", "row", None),
        P(),
    )
    return jax.shard_map(
        shards,
        mesh=mesh,
        in_specs=placed,
        out_specs=(P("row", "col", None), P("col", "row", None), P()),
        check_vma=False,
    )
```

time: 316 us -> 319 us (level)
  waiting for transfers between devices: 131 us -> 123 us
  starting transfers between devices: 74.8 us -> 79.7 us
  matrix products: 24.2 us -> 28.2 us
  other arithmetic: 26.1 us -> 29.7 us
    all_to_all x10 -> x9, waiting for transfers between devices: 131 us -> 123 us  [swap(): return lax.all_to_all(x, axis, 0, 0, tiled=True)]
    all_to_all x10 -> x9, starting transfers between devices: 74.8 us -> 79.7 us  [swap(): return lax.all_to_all(x, axis, 0, 0, tiled=True)]
    concatenate x7 -> x13, other arithmetic: 1.68 us -> 5.88 us  [the longest x2 1.94 us: shards(): got = swap(jnp.concatenate(pieces, axis=1), 'row')]
    convert_element_type x7 -> x8, other arithmetic: 2.48 us -> 6.42 us  [the longest x4 4.87 us: brick_terms(): along_c = jnp.sum(deep * b_tile.astype(jnp.float32)[None, :, :], axis=1)]
    dot_general x18 -> x12, matrix products: 12.4 us -> 15.4 us  [the longest x4 10.1 us: brick_terms(): jnp.einsum('kij,jq->kiq', brick, b_tile, preferred_element_type=jnp.float32)]
    unnamed x90 -> x114, local copies, waits for them, and re-layouts: 13.9 us -> 15.7 us
    reduce_sum x9 -> x7, other arithmetic: 8.29 us -> 6.56 us  [the longest x3 6.33 us: brick_terms(): along_b = jnp.sum(deep * c_wide, axis=0)]
    dot_general x4 -> x6, local copies, waits for them, and re-layouts: 8.62 us -> 9.82 us  [the longest x4 9.62 us: brick_terms(): jnp.einsum('kij,iq->kjq', brick, a_tile, preferred_element_type=jnp.float32)]
  transfers between devices with their start and end apart: 10 -> 9, of which waited for: 9 -> 7; matrix products, arithmetic and copies ran while one was open for 14% -> 11% of each run, Pallas kernels for 0% -> 0%
where the time goes in v2:
time: 319 us; the launch traced here: 316 us
  waiting for transfers between devices  123 us (39%)
  starting transfers between devices  79.7 us (25%)
  local copies, waits for them, and re-layouts  45.6 us (14%)
  other arithmetic  29.7 us (9%)
  matrix products  28.2 us (9%)
  between operations  9.3 us (3%)
    all_to_all x9, waiting for transfers between devices, swap(): return lax.all_to_all(x, axis, 0, 0, tiled=True)  123 us
    all_to_all x9, starting transfers between devices, swap(): return lax.all_to_all(x, axis, 0, 0, tiled=True)  79.7 us
    unnamed x114, local copies, waits for them, and re-layouts  15.7 us
    dot_general x4, matrix products, brick_terms(): jnp.einsum('kij,jq->kiq', brick, b_tile, preferred_element_type=jnp.float32)  10.1 us
    dot_general x4, local copies, waits for them, and re-layouts, brick_terms(): jnp.einsum('kij,iq->kjq', brick, a_tile, preferred_element_type=jnp.float32)  9.62 us
    unnamed x4, matrix products  9.27 us
  transfers between devices with their start and end apart: 9, of which 7 were waited for; matrix products, arithmetic and copies ran while one was open for 11% of the time, Pallas kernels for 0%

profile of v2, /device:TPU:1, one launch (start us, length us, event | category | flops | bytes accessed | tf_op | source)
XLA Modules:
  0.0 315.6 jit_solution(8886507789722094799)
XLA Ops:
  3.9 17.2 %all-to-all-start = ((f32[32,40,128]{2,1,0:T(8,128)}), f32[32,40,128]{2,1,0:T(8,128)S(1)}, u32[]{:S(2)}, u32[]{:S(2)}) async-start(f32[32,40,128]{2,1,0:T(8,128)} %broadcast_in_dim.314), calls=%async_computation | async-start | bytes 1310720 | tf_op jit(solution)/shard_map/all_to_all | solution.py:11
  37.1 3.2 %all-to-all-done = f32[32,40,128]{2,1,0:T(8,128)S(1)} async-done(((f32[32,40,128]{2,1,0:T(8,128)}), f32[32,40,128]{2,1,0:T(8,128)S(1)}, u32[]{:S(2)}, u32[]{:S(2)}) %all-to-all-start) | async-done | bytes 655392 | tf_op jit(solution)/shard_map/all_to_all | solution.py:11
  42.0 9.5 %all-to-all-start.1 = ((bf16[16,40,128]{2,1,0:T(8,128)(2,1)}), bf16[16,40,128]{2,1,0:T(8,128)(2,1)}, u32[]{:S(2)}, u32[]{:S(2)}) async-start(bf16[16,40,128]{2,1,0:T(8,128)(2,1)} %fusion.26), calls=%async_computation.1 | async-start | bytes 327680 | tf_op jit(solution)/shard_map/all_to_all | solution.py:11
  55.2 2.8 fusion.52
  58.1 2.9 copy.177
  70.6 2.5 fusion.10
  73.2 3.1 fusion.7
  82.9 5.4 %all-to-all-start.2 = ((f32[32,40,128]{2,1,0:T(8,128)}), f32[32,40,128]{2,1,0:T(8,128)S(1)}, u32[]{:S(2)}, u32[]{:S(2)}) async-start(f32[32,40,128]{2,1,0:T(8,128)} %fusion.29), calls=%async_computation.2 | async-start | bytes 1310720 | tf_op jit(solution)/shard_map/all_to_all | solution.py:11
  91.3 15.7 %all-to-all-done.2 = f32[32,40,128]{2,1,0:T(8,128)S(1)} async-done(((f32[32,40,128]{2,1,0:T(8,128)}), f32[32,40,128]{2,1,0:T(8,128)S(1)}, u32[]{:S(2)}, u32[]{:S(2)}) %all-to-all-start.2) | async-done | bytes 655392 | tf_op jit(solution)/shard_map/all_to_all | solution.py:11
  108.8 12.2 %all-to-all-start.3 = ((f32[16,96,128]{2,1,0:T(8,128)}), f32[16,96,128]{2,1,0:T(8,128)S(1)}, u32[]{:S(2)}, u32[]{:S(2)}) async-start(f32[16,96,128]{2,1,0:T(8,128)} %pad_maximum_fusion), calls=%async_computation.3 | async-start | bytes 1572864 | tf_op jit(solution)/shard_map/all_to_all | solution.py:11
  121.9 20.6 %all-to-all-done.3 = f32[16,96,128]{2,1,0:T(8,128)S(1)} async-done(((f32[16,96,128]{2,1,0:T(8,128)}), f32[16,96,128]{2,1,0:T(8,128)S(1)}, u32[]{:S(2)}, u32[]{:S(2)}) %all-to-all-start.3) | async-done | bytes 786464 | tf_op jit(solution)/shard_map/all_to_all | solution.py:11
  147.8 5.6 %all-to-all-start.4 = ((f32[32,64,128]{2,1,0:T(8,128)}), f32[32,64,128]{2,1,0:T(8,128)S(1)}, u32[]{:S(2)}, u32[]{:S(2)}) async-start(f32[32,64,128]{2,1,0:T(8,128)} %broadcast_in_dim.348), calls=%async_computation.4 | async-start | bytes 2097152 | tf_op jit(solution)/shard_map/all_to_all | solution.py:11
  155.0 27.2 %all-to-all-done.4 = f32[32,64,128]{2,1,0:T(8,128)S(1)} async-done(((f32[32,64,128]{2,1,0:T(8,128)}), f32[32,64,128]{2,1,0:T(8,128)S(1)}, u32[]{:S(2)}, u32[]{:S(2)}) %all-to-all-start.4) | async-done | bytes 1048608 | tf_op jit(solution)/shard_map/all_to_all | solution.py:11
  187.3 4.3 %all-to-all-start.5 = ((bf16[16,40,128]{2,1,0:T(8,128)(2,1)}), bf16[16,40,128]{2,1,0:T(8,128)(2,1)}, u32[]{:S(2)}, u32[]{:S(2)}) async-start(bf16[16,40,128]{2,1,0:T(8,128)(2,1)} %fusion.27), calls=%async_computation.5 | async-start | bytes 327680 | tf_op jit(solution)/shard_map/all_to_all | solution.py:11
  192.6 2.9 fusion.48
  195.4 2.9 copy.199
  206.8 2.5 fusion.4
  209.3 2.6 fusion.5
  220.0 8.8 %all-to-all-start.6 = ((f32[32,40,128]{2,1,0:T(8,128)}), f32[32,40,128]{2,1,0:T(8,128)S(1)}, u32[]{:S(2)}, u32[]{:S(2)}) async-start(f32[32,40,128]{2,1,0:T(8,128)} %fusion.28), calls=%async_computation.6 | async-start | bytes 1310720 | tf_op jit(solution)/shard_map/all_to_all | solution.py:11
  229.2 18.0 %all-to-all-done.6 = f32[32,40,128]{2,1,0:T(8,128)S(1)} async-done(((f32[32,40,128]{2,1,0:T(8,128)}), f32[32,40,128]{2,1,0:T(8,128)S(1)}, u32[]{:S(2)}, u32[]{:S(2)}) %all-to-all-start.6) | async-done | bytes 655392 | tf_op jit(solution)/shard_map/all_to_all | solution.py:11
  249.1 11.1 %all-to-all-start.7 = ((f32[16,96,128]{2,1,0:T(8,128)}), f32[16,96,128]{2,1,0:T(8,128)S(1)}, u32[]{:S(2)}, u32[]{:S(2)}) async-start(f32[16,96,128]{2,1,0:T(8,128)} %pad_maximum_fusion.1), calls=%async_computation.7 | async-start | bytes 1572864 | tf_op jit(solution)/shard_map/all_to_all | solution.py:11
  262.5 19.3 %all-to-all-done.7 = f32[16,96,128]{2,1,0:T(8,128)S(1)} async-done(((f32[16,96,128]{2,1,0:T(8,128)}), f32[16,96,128]{2,1,0:T(8,128)S(1)}, u32[]{:S(2)}, u32[]{:S(2)}) %all-to-all-start.7) | async-done | bytes 786464 | tf_op jit(solution)/shard_map/all_to_all | solution.py:11
  287.6 5.5 %all-to-all-start.8 = ((f32[32,40,128]{2,1,0:T(8,128)}), f32[32,40,128]{2,1,0:T(8,128)S(1)}, u32[]{:S(2)}, u32[]{:S(2)}) async-start(f32[32,40,128]{2,1,0:T(8,128)} %select_maximum_fusion), calls=%async_computation.8 | async-start | bytes 1310720 | tf_op jit(solution)/shard_map/all_to_all | solution.py:11
  294.7 19.2 %all-to-all-done.8 = f32[32,40,128]{2,1,0:T(8,128)S(1)} async-done(((f32[32,40,128]{2,1,0:T(8,128)}), f32[32,40,128]{2,1,0:T(8,128)S(1)}, u32[]{:S(2)}, u32[]{:S(2)}) %all-to-all-start.8) | async-done | bytes 655392 | tf_op jit(solution)/shard_map/all_to_all | solution.py:11
  (313 shorter events, 81.2 us)
Async XLA Ops:
  0.6 27.1 %copy-start.5 = (f32[512,256]{1,0:T(8,128)S(1)}, f32[512,256]{1,0:T(8,128)}, u32[]{:S(2)}) copy-start(f32[512,256]{1,0:T(8,128)} %param.13) | copy-start | bytes 1572868
  3.9 36.3 %all-to-all-start = ((f32[32,40,128]{2,1,0:T(8,128)}), f32[32,40,128]{2,1,0:T(8,128)S(1)}, u32[]{:S(2)}, u32[]{:S(2)}) async-start(f32[32,40,128]{2,1,0:T(8,128)} %broadcast_in_dim.314), calls=%async_computation | async-start | bytes 1310720 | tf_op jit(solution)/shard_map/all_to_all | solution.py:11
  29.6 22.0 %copy-start.2 = (bf16[16,128,128]{1,2,0:T(8,128)(2,1)}, bf16[16,128,128]{1,2,0:T(8,128)(2,1)S(1)}, u32[]{:S(2)}) copy-start(bf16[16,128,128]{1,2,0:T(8,128)(2,1)S(1)} %copy.174) | copy-start | bytes 1572868
  42.0 18.9 %all-to-all-start.1 = ((bf16[16,40,128]{2,1,0:T(8,128)(2,1)}), bf16[16,40,128]{2,1,0:T(8,128)(2,1)}, u32[]{:S(2)}, u32[]{:S(2)}) async-start(bf16[16,40,128]{2,1,0:T(8,128)(2,1)} %fusion.26), calls=%async_computation.1 | async-start | bytes 327680 | tf_op jit(solution)/shard_map/all_to_all | solution.py:11
  82.9 24.1 %all-to-all-start.2 = ((f32[32,40,128]{2,1,0:T(8,128)}), f32[32,40,128]{2,1,0:T(8,128)S(1)}, u32[]{:S(2)}, u32[]{:S(2)}) async-start(f32[32,40,128]{2,1,0:T(8,128)} %fusion.29), calls=%async_computation.2 | async-start | bytes 1310720 | tf_op jit(solution)/shard_map/all_to_all | solution.py:11
  90.8 30.6 %copy-start.26 = (pred[32]{0:T(512)(128)(4,1)}, pred[32]{0:T(512)(128)(4,1)S(1)}, u32[]{:S(2)}) copy-start(pred[32]{0:T(512)(128)(4,1)S(1)} %get-tuple-element.115) | copy-start | bytes 100
  90.8 30.6 %copy-start.28 = (pred[32]{0:T(512)(128)(4,1)}, pred[32]{0:T(512)(128)(4,1)S(1)}, u32[]{:S(2)}) copy-start(pred[32]{0:T(512)(128)(4,1)S(1)} %get-tuple-element.116) | copy-start | bytes 100
  90.8 30.6 %copy-start.30 = (pred[32]{0:T(512)(128)(4,1)}, pred[32]{0:T(512)(128)(4,1)S(1)}, u32[]{:S(2)}) copy-start(pred[32]{0:T(512)(128)(4,1)S(1)} %get-tuple-element.117) | copy-start | bytes 100
  90.8 30.6 %copy-start.32 = (pred[32]{0:T(512)(128)(4,1)}, pred[32]{0:T(512)(128)(4,1)S(1)}, u32[]{:S(2)}) copy-start(pred[32]{0:T(512)(128)(4,1)S(1)} %get-tuple-element.118) | copy-start | bytes 100
  90.8 30.6 %copy-start.34 = (pred[32]{0:T(512)(128)(4,1)}, pred[32]{0:T(512)(128)(4,1)S(1)}, u32[]{:S(2)}) copy-start(pred[32]{0:T(512)(128)(4,1)S(1)} %get-tuple-element.119) | copy-start | bytes 100
  90.8 30.6 %copy-start.36 = (pred[32]{0:T(512)(128)(4,1)}, pred[32]{0:T(512)(128)(4,1)S(1)}, u32[]{:S(2)}) copy-start(pred[32]{0:T(512)(128)(4,1)S(1)} %get-tuple-element.120) | copy-start | bytes 100
  90.8 30.6 %copy-start.38 = (pred[32]{0:T(512)(128)(4,1)}, pred[32]{0:T(512)(128)(4,1)S(1)}, u32[]{:S(2)}) copy-start(pred[32]{0:T(512)(128)(4,1)S(1)} %get-tuple-element.121) | copy-start | bytes 100
  90.8 30.6 %copy-start.40 = (pred[32]{0:T(512)(128)(4,1)}, pred[32]{0:T(512)(128)(4,1)S(1)}, u32[]{:S(2)}) copy-start(pred[32]{0:T(512)(128)(4,1)S(1)} %get-tuple-element.122) | copy-start | bytes 100
  108.8 33.6 %all-to-all-start.3 = ((f32[16,96,128]{2,1,0:T(8,128)}), f32[16,96,128]{2,1,0:T(8,128)S(1)}, u32[]{:S(2)}, u32[]{:S(2)}) async-start(f32[16,96,128]{2,1,0:T(8,128)} %pad_maximum_fusion), calls=%async_computation.3 | async-start | bytes 1572864 | tf_op jit(solution)/shard_map/all_to_all | solution.py:11
  121.8 24.1 %copy-start.13 = (f32[1,256,128]{2,1,0:T(8,128)S(1)}, f32[1,256,128]{2,1,0:T(8,128)}, u32[]{:S(2)}) copy-start(f32[1,256,128]{2,1,0:T(8,128)} %get-tuple-element.62) | copy-start | bytes 393220
  121.8 24.1 %copy-start.14 = (f32[1,256,128]{2,1,0:T(8,128)S(1)}, f32[1,256,128]{2,1,0:T(8,128)}, u32[]{:S(2)}) copy-start(f32[1,256,128]{2,1,0:T(8,128)} %get-tuple-element.63) | copy-start | bytes 393220
  121.8 24.1 %copy-start.15 = (f32[1,256,128]{2,1,0:T(8,128)S(1)}, f32[1,256,128]{2,1,0:T(8,128)}, u32[]{:S(2)}) copy-start(f32[1,256,128]{2,1,0:T(8,128)} %get-tuple-element.64) | copy-start | bytes 393220
  147.8 34.5 %all-to-all-start.4 = ((f32[32,64,128]{2,1,0:T(8,128)}), f32[32,64,128]{2,1,0:T(8,128)S(1)}, u32[]{:S(2)}, u32[]{:S(2)}) async-start(f32[32,64,128]{2,1,0:T(8,128)} %broadcast_in_dim.348), calls=%async_computation.4 | async-start | bytes 2097152 | tf_op jit(solution)/shard_map/all_to_all | solution.py:11
  153.4 29.0 %copy-start.3 = (bf16[16,128,128]{1,2,0:T(8,128)(2,1)S(1)}, bf16[16,128,128]{1,2,0:T(8,128)(2,1)}, u32[]{:S(2)}) copy-start(bf16[16,128,128]{1,2,0:T(8,128)(2,1)} %copy-done.2) | copy-start | bytes 1572868
  187.3 12.3 %all-to-all-start.5 = ((bf16[16,40,128]{2,1,0:T(8,128)(2,1)}), bf16[16,40,128]{2,1,0:T(8,128)(2,1)}, u32[]{:S(2)}, u32[]{:S(2)}) async-start(bf16[16,40,128]{2,1,0:T(8,128)(2,1)} %fusion.27), calls=%async_computation.5 | async-start | bytes 327680 | tf_op jit(solution)/shard_map/all_to_all | solution.py:11
  220.0 27.3 %all-to-all-start.6 = ((f32[32,40,128]{2,1,0:T(8,128)}), f32[32,40,128]{2,1,0:T(8,128)S(1)}, u32[]{:S(2)}, u32[]{:S(2)}) async-start(f32[32,40,128]{2,1,0:T(8,128)} %fusion.28), calls=%async_computation.6 | async-start | bytes 1310720 | tf_op jit(solution)/shard_map/all_to_all | solution.py:11
  228.8 18.7 %copy-start.24 = (s32[32,2]{0,1:T(2,128)S(1)}, s32[32,2]{0,1:T(2,128)}, u32[]{:S(2)}) copy-start(s32[32,2]{0,1:T(2,128)} %copy-done.23) | copy-start | bytes 772
  249.1 32.6 %all-to-all-start.7 = ((f32[16,96,128]{2,1,0:T(8,128)}), f32[16,96,128]{2,1,0:T(8,128)S(1)}, u32[]{:S(2)}, u32[]{:S(2)}) async-start(f32[16,96,128]{2,1,0:T(8,128)} %pad_maximum_fusion.1), calls=%async_computation.7 | async-start | bytes 1572864 | tf_op jit(solution)/shard_map/all_to_all | solution.py:11
  287.6 26.3 %all-to-all-start.8 = ((f32[32,40,128]{2,1,0:T(8,128)}), f32[32,40,128]{2,1,0:T(8,128)S(1)}, u32[]{:S(2)}, u32[]{:S(2)}) async-start(f32[32,40,128]{2,1,0:T(8,128)} %select_maximum_fusion), calls=%async_computation.8 | async-start | bytes 1310720 | tf_op jit(solution)/shard_map/all_to_all | solution.py:11
  (32 other events, 287.0 us)

commit v3 on v2

--- a/solution.py
+++ b/solution.py
@@ -1,6 +1,8 @@
 import jax
 import jax.numpy as jnp
 from jax import lax
+from jax.experimental import pallas as pl
+from jax.experimental.pallas import tpu as pltpu
 from jax.sharding import PartitionSpec as P
 
 LANES = 128
@@ -46,14 +48,83 @@
     )
 
 
-def brick_terms(brick, a_tile, b_tile, c_rows):
-    c_wide = c_rows.astype(jnp.float32)[:, None, :]
-    wide = jnp.einsum("kij,jq->kiq", brick, b_tile, preferred_element_type=jnp.float32)
-    along_a = jnp.sum(wide * c_wide, axis=0)
-    deep = jnp.einsum("kij,iq->kjq", brick, a_tile, preferred_element_type=jnp.float32)
-    along_b = jnp.sum(deep * c_wide, axis=0)
-    along_c = jnp.sum(deep * b_tile.astype(jnp.float32)[None, :, :], axis=1)
-    return along_a, along_b, along_c
+def deep_kernel(meta, slab, a_ref, c_ref, out, drive):
+    slots, depth, tile, _ = slab.shape
+    nr, rows, _ = out.shape
+    half = a_ref.shape[2] // LANES
+    own = rows // half
+    drive[...] = jnp.zeros_like(drive)
+    for slot in range(slots):
+        a_tile = a_ref[meta[0, slot]]
+        c_rows = c_ref[pl.ds(pl.multiple_of(meta[2, slot] * depth, depth), depth), :]
+        c_rows = c_rows.astype(jnp.float32)
+        total = jnp.zeros(a_tile.shape, jnp.float32)
+        for k in range(depth):
+            deep = lax.dot_general(
+                slab[slot, k], a_tile, (((0,), (0,)), ((), ())),
+                preferred_element_type=jnp.float32,
+            )
+            total = total + deep * c_rows[k : k + 1, :]
+        spot = pl.ds(pl.multiple_of(meta[1, slot] * tile, tile), tile)
+        drive[spot, :] = drive[spot, :] + jnp.where(meta[3, slot] > 0, total, 0.0)
+    for h in range(half):
+        part = drive[:, h * LANES : (h + 1) * LANES]
+        out[:, own * h : own * (h + 1), :] = part.reshape(nr, own, LANES)
+
+
+def wide_kernel(meta, got, slab, a_ref, c_ref, out, b_all, deep_c):
+    slots, depth, tile, _ = slab.shape
+    nr = got.shape[0]
+    nc = out.shape[0]
+    rank = a_ref.shape[2]
+    half, qa, qb = rank // LANES, rank // nc, rank // nr
+    own = b_all.shape[0] // nr
+    for h in range(half):
+        part = got[:, own * h : own * (h + 1), :]
+        b_all[:, h * LANES : (h + 1) * LANES] = part.reshape(nr * own, LANES)
+    deep_c[...] = jnp.zeros_like(deep_c)
+    for slot in range(slots):
+        b_tile = b_all[pl.ds(pl.multiple_of(meta[1, slot] * tile, tile), tile), :]
+        a_tile = a_ref[meta[0, slot]].astype(jnp.float32)
+        c_rows = c_ref[pl.ds(pl.multiple_of(meta[2, slot] * depth, depth), depth), :]
+        c_rows = c_rows.astype(jnp.float32)
+        total = jnp.zeros((tile, rank), jnp.float32)
+        for k in range(depth):
+            wide = jnp.dot(slab[slot, k], b_tile, preferred_element_type=jnp.float32)
+            total = total + wide * c_rows[k : k + 1, :]
+            deep_c[slot * depth + k : slot * depth + k + 1, :] = jnp.sum(
+                wide * a_tile, axis=0, keepdims=True
+            )
+        out[:, slot * qa : (slot + 1) * qa, :] = total.T.reshape(nc, qa, LANES)
+    at = slots * qa
+    whole = b_all[...]
+    gram_b = lax.dot_general(
+        whole, whole, (((0,), (0,)), ((), ())), preferred_element_type=jnp.float32
+    )
+    for h in range(half):
+        part = gram_b[:, h * LANES : (h + 1) * LANES]
+        out[:, at : at + qa, :] = part.reshape(nc, qa, LANES)
+        at += qa
+    pieces = got[:, own * half : own * half + qa, :].astype(jnp.float32)
+    piece = jnp.sum(pieces, axis=0)
+    first = slots * depth
+    moved = pltpu.roll(piece, first, 1) + pltpu.roll(piece, first - qb, 1)
+    lane = lax.broadcasted_iota(jnp.int32, piece.shape, 1)
+    moved = jnp.where((lane >= first) & (lane < first + qb), moved, 0.0)
+    out[:, at : at + qa, :] = deep_c[...].T.reshape(nc, qa, LANES) + moved[None]
+
+
+def call(kernel, shape, scratch, flops, moved, operands):
+    memory = [pltpu.SMEM] + [pltpu.VMEM] * (len(operands) - 1)
+    return pl.pallas_call(
+        kernel,
+        out_shape=jax.ShapeDtypeStruct(shape, jnp.float32),
+        in_specs=[pl.BlockSpec(memory_space=m) for m in memory],
+        out_specs=pl.BlockSpec(memory_space=pltpu.VMEM),
+        scratch_shapes=scratch,
+        cost_estimate=pl.CostEstimate(flops=flops, bytes_accessed=moved, transcendentals=0),
+        compiler_params=pltpu.CompilerParams(vmem_limit_bytes=32 << 20),
+    )(*operands)
 
 
 def bump(state, hess, full, drive, rate):
@@ -90,7 +161,9 @@
     half = rank // LANES
 
     live = lax.iota(jnp.int32, slots) < own
-    spots = jnp.where(live[None, :], places, 0)
+    meta = jnp.concatenate(
+        [jnp.where(live[None, :], places, 0), live[None, :].astype(jnp.int32)], axis=0
+    )
     mine = pad_lanes(jnp.where(live[None, :], places, -1).astype(f32).reshape(1, -1))
     mine = jnp.broadcast_to(mine, (8, LANES))
 
@@ -125,33 +198,23 @@
             [jnp.broadcast_to(fold(b_bf)[None], (nr, own_b * half, LANES)), fold(pair)], axis=1
         )
         got = swap(send, "row")
-        b_got, s_got = take(got, [own_b * half, fold(pair).shape[1]])
-        b_all = unfold(b_got, rank).reshape(tiles_b * tile, rank)
-        gram_b = gram(b_all)
-        s_got = unfold(s_got, pair.shape[2]).astype(f32)
-        piece = jnp.sum(s_got[:, :, :qb] + s_got[:, :, qb : 2 * qb], axis=0)
         gram_c = gram(c_bf)
-        parts_a, parts_c = [], []
-        drive_b = jnp.zeros((tiles_b, tile, rank), f32)
-        for slot in range(slots):
-            ti, tj, tk = spots[0, slot], spots[1, slot], spots[2, slot]
-            a_tile = lax.dynamic_index_in_dim(a_bf3, ti, 0, keepdims=False)
-            b_tile = lax.dynamic_slice_in_dim(b_all, tj * tile, tile, 0)
-            c_rows = lax.dynamic_slice_in_dim(c_bf, tk * depth, depth, 0)
-            da, db, dc = brick_terms(slab[slot], a_tile, b_tile, c_rows)
-            parts_a.append(da.T)
-            parts_c.append(dc.T)
-            here = (lax.iota(jnp.int32, tiles_b) == tj) & live[slot]
-            drive_b = drive_b + jnp.where(here[:, None, None], db[None], 0.0)
-        pieces = [p.reshape(nc, qa, tile) for p in parts_a]
-        pieces.append(fold(gram_b.reshape(nc, qa, rank)))
-        mixed = jnp.concatenate(parts_c, axis=1).reshape(nc, qa, slots * depth)
-        mixed = jnp.concatenate([mixed, jnp.broadcast_to(piece[None], (nc, qa, qb))], axis=2)
-        pieces.append(fold(pad_lanes(mixed)))
-        got = swap(jnp.concatenate(pieces, axis=1), "col")
-        *a_got, s_got, m_got = take(got, [qa] * slots + [qa * half, pieces[-1].shape[1]])
+        work = 2 * slots * depth * tile * tile * rank
+        blocks = call(
+            deep_kernel,
+            (nr, own_b * half, LANES),
+            [pltpu.VMEM((tiles_b * tile, rank), f32)],
+            work, slab.size * 2, (meta, slab, a_bf3, c_bf),
+        )
+        send = call(
+            wide_kernel,
+            (nc, qa * (slots + half + 1), LANES),
+            [pltpu.VMEM((tiles_b * tile, rank), bf16), pltpu.VMEM((LANES, rank), f32)],
+            work, slab.size * 2, (meta, got, slab, a_bf3, c_bf),
+        )
+        got = swap(send, "col")
+        *a_got, s_got, m_got = take(got, [qa] * slots + [qa * half, qa])
         sb_c = unfold(jnp.sum(s_got, axis=0), rank)
-        m_got = unfold(m_got, pad_lanes(mixed).shape[2])
         drive_a = jnp.stack(
             [
                 sum(
@@ -166,7 +229,7 @@
         drive_c = jnp.einsum("sqmk,smb->qbk", c_got, onehot, precision=HIGH).reshape(qa, length)
         strip = m_got[:, :, slots * depth : slots * depth + qb].reshape(rank, qb).T
         pieces = [
-            fold(drive_b.reshape(nr, own_b, rank)),
+            blocks,
             jnp.broadcast_to(fold(strip)[None], (nr, qb * half, LANES)),
             jnp.broadcast_to(fold(drive_c)[None], (nr, qa * tiles_c, LANES)),
         ]

time: 319 us -> 283 us (0.89)
  waiting for transfers between devices: 123 us -> 146 us
  matrix products: 28.2 us -> 7.82 us
  local copies, waits for them, and re-layouts: 45.6 us -> 26 us
  other arithmetic: 29.7 us -> 16.8 us
  Pallas kernels: 0 us -> 7.42 us
  between operations: 9.3 us -> 2.3 us
  starting transfers between devices: 79.7 us -> 74.9 us
    all_to_all x9, waiting for transfers between devices: 123 us -> 146 us  [swap(): return lax.all_to_all(x, axis, 0, 0, tiled=True)]
    dot_general x4 -> x0, matrix products: 10.1 us -> none  [brick_terms(): jnp.einsum('kij,jq->kiq', brick, b_tile, preferred_element_type=jnp.float32)]
    dot_general x6 -> x0, local copies, waits for them, and re-layouts: 9.82 us -> none  [the longest x4 9.62 us: brick_terms(): jnp.einsum('kij,iq->kjq', brick, a_tile, preferred_element_type=jnp.float32)]
    unnamed x4 -> x0, matrix products: 9.27 us -> none
    unnamed x114 -> x60, local copies, waits for them, and re-layouts: 15.7 us -> 7.71 us
    pallas_call x0 -> x4, Pallas kernels: none -> 7.42 us  [call(): pl.pallas_call(kernel, out_shape=jax.ShapeDtypeStruct(shape, jnp.float32)...]
    convert_element_type x8 -> x2, other arithmetic: 8.33 us -> 1.07 us  [the longest x1 1.07 us: shards(): c_bf = jnp.swapaxes(ct3.astype(bf16), 1, 2).reshape(length, rank)]
    reduce_sum x5 -> x0, other arithmetic: 6.5 us -> none  [the longest x3 6.33 us: brick_terms(): along_b = jnp.sum(deep * c_wide, axis=0)]
  transfers between devices with their start and end apart: 9 -> 9, of which waited for: 7 -> 9; matrix products, arithmetic and copies ran while one was open for 11% -> 5% of each run, Pallas kernels for 0% -> 1%
where the time goes in v3:
time: 283 us; the launch traced here: 281 us
  waiting for transfers between devices  146 us (52%)
  starting transfers between devices  74.9 us (26%)
  local copies, waits for them, and re-layouts  26 us (9%)
  other arithmetic  16.8 us (6%)
  matrix products  7.82 us (3%)
  Pallas kernels  7.42 us (3%)
    all_to_all x9, waiting for transfers between devices, swap(): return lax.all_to_all(x, axis, 0, 0, tiled=True)  146 us
    all_to_all x9, starting transfers between devices, swap(): return lax.all_to_all(x, axis, 0, 0, tiled=True)  74.9 us
    unnamed x60, local copies, waits for them, and re-layouts  7.71 us
    pallas_call x4, Pallas kernels, call(): pl.pallas_call(kernel, out_shape=jax.ShapeDtypeStruct(shape, jnp.float32)...  7.42 us
  transfers between devices with their start and end apart: 9, of which 9 were waited for; matrix products, arithmetic and copies ran while one was open for 5% of the time, Pallas kernels for 1%

profile of v3, /device:TPU:1, one launch (start us, length us, event | category | flops | bytes accessed | tf_op | source)
XLA Modules:
  0.0 281.1 jit_solution(1076967582044728752)
XLA Ops:
  3.2 17.4 %all-to-all-start = ((f32[32,40,128]{2,1,0:T(8,128)}), f32[32,40,128]{2,1,0:T(8,128)S(1)}, u32[]{:S(2)}, u32[]{:S(2)}) async-start(f32[32,40,128]{2,1,0:T(8,128)} %broadcast_in_dim.222), calls=%async_computation | async-start | bytes 1310720 | tf_op jit(solution)/shard_map/all_to_all | solution.py:13
  22.1 17.6 %all-to-all-done = f32[32,40,128]{2,1,0:T(8,128)S(1)} async-done(((f32[32,40,128]{2,1,0:T(8,128)}), f32[32,40,128]{2,1,0:T(8,128)S(1)}, u32[]{:S(2)}, u32[]{:S(2)}) %all-to-all-start) | async-done | bytes 655392 | tf_op jit(solution)/shard_map/all_to_all | solution.py:13
  41.8 9.5 %all-to-all-start.1 = ((bf16[16,40,128]{2,1,0:T(8,128)(2,1)}), bf16[16,40,128]{2,1,0:T(8,128)(2,1)S(1)}, u32[]{:S(2)}, u32[]{:S(2)}) async-start(bf16[16,40,128]{2,1,0:T(8,128)(2,1)} %pad_maximum_fusion.4), calls=%async_computation.1 | async-start | bytes 327680 | tf_op jit(solution)/shard_map/all_to_all | solution.py:13
  51.7 7.1 %all-to-all-done.1.got = bf16[16,40,128]{2,1,0:T(8,128)(2,1)S(1)} async-done(((bf16[16,40,128]{2,1,0:T(8,128)(2,1)}), bf16[16,40,128]{2,1,0:T(8,128)(2,1)S(1)}, u32[]{:S(2)}, u32[]{:S(2)}) %all-to-all-start.1) | async-done | bytes 163872 | tf_op jit(solution)/shard_map/all_to_all | solution.py:13
  58.8 2.4 shard_map.94
  61.2 6.6 %all-to-all-start.2 = ((f32[32,40,128]{2,1,0:T(8,128)}), f32[32,40,128]{2,1,0:T(8,128)S(1)}, u32[]{:S(2)}, u32[]{:S(2)}) async-start(f32[32,40,128]{2,1,0:T(8,128)} %shard_map.94), calls=%async_computation.2 | async-start | bytes 1310720 | tf_op jit(solution)/shard_map/all_to_all | solution.py:13
  72.3 14.6 %all-to-all-done.2 = f32[32,40,128]{2,1,0:T(8,128)S(1)} async-done(((f32[32,40,128]{2,1,0:T(8,128)}), f32[32,40,128]{2,1,0:T(8,128)S(1)}, u32[]{:S(2)}, u32[]{:S(2)}) %all-to-all-start.2) | async-done | bytes 655392 | tf_op jit(solution)/shard_map/all_to_all | solution.py:13
  90.0 7.8 %all-to-all-start.3 = ((f32[16,96,128]{2,1,0:T(8,128)}), f32[16,96,128]{2,1,0:T(8,128)}, u32[]{:S(2)}, u32[]{:S(2)}) async-start(f32[16,96,128]{2,1,0:T(8,128)} %pad_maximum_fusion), calls=%async_computation.3 | async-start | bytes 1572864 | tf_op jit(solution)/shard_map/all_to_all | solution.py:13
  99.0 20.2 %all-to-all-done.3 = f32[16,96,128]{2,1,0:T(8,128)} async-done(((f32[16,96,128]{2,1,0:T(8,128)}), f32[16,96,128]{2,1,0:T(8,128)}, u32[]{:S(2)}, u32[]{:S(2)}) %all-to-all-start.3) | async-done | bytes 786464 | tf_op jit(solution)/shard_map/all_to_all | solution.py:13
  124.5 1.7 slice_reduce_fusion.3
  127.1 3.1 %fusion.14 = (f32[4,8,128]{1,2,0:T(8,128)}, f32[4,8,128]{1,2,0:T(8,128)S(1)}) fusion(s32[]{:T(128)S(6)} %select_n.76, f32[1,256,128]{1,2,0:T(8,128)} %get-tuple-element.54, f32[1,256,128]{1,2,0:T(8,128)} %get-tuple-element.53, f32[1,256,128]{1,2,0:T(8,128)} %get-tuple-element.52, f32[1,256,128]{1,2,0:T(8,128)S(1)} %copy-done.6, f32[4,8,128]{1,2,0:T(8,128)S(1)} %copy.180, ...), kind=kLoop, calls=%fused_computation.51 | loop fusion | flops 53248 | bytes 639052 | tf_op jit(solution)/shard_map/max | solution.py:135
  132.5 7.1 %all-to-all-start.4 = ((f32[32,64,128]{2,1,0:T(8,128)}), f32[32,64,128]{2,1,0:T(8,128)}, u32[]{:S(2)}, u32[]{:S(2)}) async-start(f32[32,64,128]{2,1,0:T(8,128)} %broadcast_in_dim.244), calls=%async_computation.4 | async-start | bytes 2097152 | tf_op jit(solution)/shard_map/all_to_all | solution.py:13
  141.9 26.6 %all-to-all-done.4 = f32[32,64,128]{2,1,0:T(8,128)} async-done(((f32[32,64,128]{2,1,0:T(8,128)}), f32[32,64,128]{2,1,0:T(8,128)}, u32[]{:S(2)}, u32[]{:S(2)}) %all-to-all-start.4) | async-done | bytes 1048608 | tf_op jit(solution)/shard_map/all_to_all | solution.py:13
  171.3 4.3 %all-to-all-start.5 = ((bf16[16,40,128]{2,1,0:T(8,128)(2,1)}), bf16[16,40,128]{2,1,0:T(8,128)(2,1)S(1)}, u32[]{:S(2)}, u32[]{:S(2)}) async-start(bf16[16,40,128]{2,1,0:T(8,128)(2,1)} %pad_maximum_fusion.5), calls=%async_computation.5 | async-start | bytes 327680 | tf_op jit(solution)/shard_map/all_to_all | solution.py:13
  176.4 2.0 copy.190
  179.6 3.4 %all-to-all-done.5.got = bf16[16,40,128]{2,1,0:T(8,128)(2,1)S(1)} async-done(((bf16[16,40,128]{2,1,0:T(8,128)(2,1)}), bf16[16,40,128]{2,1,0:T(8,128)(2,1)S(1)}, u32[]{:S(2)}, u32[]{:S(2)}) %all-to-all-start.5) | async-done | bytes 163872 | tf_op jit(solution)/shard_map/all_to_all | solution.py:13
  183.0 2.4 shard_map.96
  185.4 8.8 %all-to-all-start.6 = ((f32[32,40,128]{2,1,0:T(8,128)}), f32[32,40,128]{2,1,0:T(8,128)}, u32[]{:S(2)}, u32[]{:S(2)}) async-start(f32[32,40,128]{2,1,0:T(8,128)} %shard_map.96), calls=%async_computation.6 | async-start | bytes 1310720 | tf_op jit(solution)/shard_map/all_to_all | solution.py:13
  195.5 18.2 %all-to-all-done.6 = f32[32,40,128]{2,1,0:T(8,128)} async-done(((f32[32,40,128]{2,1,0:T(8,128)}), f32[32,40,128]{2,1,0:T(8,128)}, u32[]{:S(2)}, u32[]{:S(2)}) %all-to-all-start.6) | async-done | bytes 655392 | tf_op jit(solution)/shard_map/all_to_all | solution.py:13
  217.3 7.3 %all-to-all-start.7 = ((f32[16,96,128]{2,1,0:T(8,128)}), f32[16,96,128]{2,1,0:T(8,128)S(1)}, u32[]{:S(2)}, u32[]{:S(2)}) async-start(f32[16,96,128]{2,1,0:T(8,128)} %pad_maximum_fusion.1), calls=%async_computation.7 | async-start | bytes 1572864 | tf_op jit(solution)/shard_map/all_to_all | solution.py:13
  227.2 18.8 %all-to-all-done.7 = f32[16,96,128]{2,1,0:T(8,128)S(1)} async-done(((f32[16,96,128]{2,1,0:T(8,128)}), f32[16,96,128]{2,1,0:T(8,128)S(1)}, u32[]{:S(2)}, u32[]{:S(2)}) %all-to-all-start.7) | async-done | bytes 786464 | tf_op jit(solution)/shard_map/all_to_all | solution.py:13
  252.4 6.2 %all-to-all-start.8 = ((f32[32,40,128]{2,1,0:T(8,128)}), f32[32,40,128]{2,1,0:T(8,128)S(1)}, u32[]{:S(2)}, u32[]{:S(2)}) async-start(f32[32,40,128]{2,1,0:T(8,128)} %select_maximum_fusion), calls=%async_computation.8 | async-start | bytes 1310720 | tf_op jit(solution)/shard_map/all_to_all | solution.py:13
  258.6 1.5 fusion.4
  260.1 19.2 %all-to-all-done.8 = f32[32,40,128]{2,1,0:T(8,128)S(1)} async-done(((f32[32,40,128]{2,1,0:T(8,128)}), f32[32,40,128]{2,1,0:T(8,128)S(1)}, u32[]{:S(2)}, u32[]{:S(2)}) %all-to-all-start.8) | async-done | bytes 655392 | tf_op jit(solution)/shard_map/all_to_all | solution.py:13
  (215 shorter events, 45.0 us)
Async XLA Ops:
  0.6 1.6 copy-start.10
  3.2 18.1 %copy-start.1 = (f32[512,256]{1,0:T(8,128)S(1)}, f32[512,256]{1,0:T(8,128)}, u32[]{:S(2)}) copy-start(f32[512,256]{1,0:T(8,128)} %param.13) | copy-start | bytes 1572868
  3.2 36.5 %all-to-all-start = ((f32[32,40,128]{2,1,0:T(8,128)}), f32[32,40,128]{2,1,0:T(8,128)S(1)}, u32[]{:S(2)}, u32[]{:S(2)}) async-start(f32[32,40,128]{2,1,0:T(8,128)} %broadcast_in_dim.222), calls=%async_computation | async-start | bytes 1310720 | tf_op jit(solution)/shard_map/all_to_all | solution.py:13
  41.8 17.0 %copy-start = (bf16[1,1,2,16,128,128]{5,4,3,2,1,0:T(8,128)(2,1)S(1)}, bf16[1,1,2,16,128,128]{5,4,3,2,1,0:T(8,128)(2,1)}, u32[]{:S(2)}) copy-start(bf16[1,1,2,16,128,128]{5,4,3,2,1,0:T(8,128)(2,1)} %param.7) | copy-start | bytes 3145732
  41.8 17.0 %all-to-all-start.1 = ((bf16[16,40,128]{2,1,0:T(8,128)(2,1)}), bf16[16,40,128]{2,1,0:T(8,128)(2,1)S(1)}, u32[]{:S(2)}, u32[]{:S(2)}) async-start(bf16[16,40,128]{2,1,0:T(8,128)(2,1)} %pad_maximum_fusion.4), calls=%async_computation.1 | async-start | bytes 327680 | tf_op jit(solution)/shard_map/all_to_all | solution.py:13
  61.2 6.6 %copy-start.11 = (f32[2,3]{1,0:T(2,128)S(1)}, f32[2,3]{1,0:T(2,128)}, u32[]{:S(2)}) copy-start(f32[2,3]{1,0:T(2,128)} %param.10) | copy-start | bytes 76
  61.2 25.6 %all-to-all-start.2 = ((f32[32,40,128]{2,1,0:T(8,128)}), f32[32,40,128]{2,1,0:T(8,128)S(1)}, u32[]{:S(2)}, u32[]{:S(2)}) async-start(f32[32,40,128]{2,1,0:T(8,128)} %shard_map.94), calls=%async_computation.2 | async-start | bytes 1310720 | tf_op jit(solution)/shard_map/all_to_all | solution.py:13
  90.0 7.8 %copy-start.18 = (pred[32]{0:T(512)(128)(4,1)S(1)}, pred[32]{0:T(512)(128)(4,1)}, u32[]{:S(2)}) copy-start(pred[32]{0:T(512)(128)(4,1)} %get-tuple-element.94) | copy-start | bytes 100
  90.0 7.8 %copy-start.20 = (pred[32]{0:T(512)(128)(4,1)S(1)}, pred[32]{0:T(512)(128)(4,1)}, u32[]{:S(2)}) copy-start(pred[32]{0:T(512)(128)(4,1)} %get-tuple-element.95) | copy-start | bytes 100
  90.0 7.8 %copy-start.22 = (pred[32]{0:T(512)(128)(4,1)S(1)}, pred[32]{0:T(512)(128)(4,1)}, u32[]{:S(2)}) copy-start(pred[32]{0:T(512)(128)(4,1)} %get-tuple-element.96) | copy-start | bytes 100
  90.0 29.2 %all-to-all-start.3 = ((f32[16,96,128]{2,1,0:T(8,128)}), f32[16,96,128]{2,1,0:T(8,128)}, u32[]{:S(2)}, u32[]{:S(2)}) async-start(f32[16,96,128]{2,1,0:T(8,128)} %pad_maximum_fusion), calls=%async_computation.3 | async-start | bytes 1572864 | tf_op jit(solution)/shard_map/all_to_all | solution.py:13
  132.5 7.8 %copy-start.7 = (f32[32,128]{1,0:T(8,128)S(1)}, f32[32,128]{1,0:T(8,128)}, u32[]{:S(2)}) copy-start(f32[32,128]{1,0:T(8,128)} %get-tuple-element.17) | copy-start | bytes 49156
  132.5 36.1 %all-to-all-start.4 = ((f32[32,64,128]{2,1,0:T(8,128)}), f32[32,64,128]{2,1,0:T(8,128)}, u32[]{:S(2)}, u32[]{:S(2)}) async-start(f32[32,64,128]{2,1,0:T(8,128)} %broadcast_in_dim.244), calls=%async_computation.4 | async-start | bytes 2097152 | tf_op jit(solution)/shard_map/all_to_all | solution.py:13
  171.3 11.7 %all-to-all-start.5 = ((bf16[16,40,128]{2,1,0:T(8,128)(2,1)}), bf16[16,40,128]{2,1,0:T(8,128)(2,1)S(1)}, u32[]{:S(2)}, u32[]{:S(2)}) async-start(bf16[16,40,128]{2,1,0:T(8,128)(2,1)} %pad_maximum_fusion.5), calls=%async_computation.5 | async-start | bytes 327680 | tf_op jit(solution)/shard_map/all_to_all | solution.py:13
  185.4 28.3 %all-to-all-start.6 = ((f32[32,40,128]{2,1,0:T(8,128)}), f32[32,40,128]{2,1,0:T(8,128)}, u32[]{:S(2)}, u32[]{:S(2)}) async-start(f32[32,40,128]{2,1,0:T(8,128)} %shard_map.96), calls=%async_computation.6 | async-start | bytes 1310720 | tf_op jit(solution)/shard_map/all_to_all | solution.py:13
  217.3 7.3 %copy-start.13 = (pred[32]{0:T(512)(128)(4,1)S(1)}, pred[32]{0:T(512)(128)(4,1)}, u32[]{:S(2)}) copy-start(pred[32]{0:T(512)(128)(4,1)} %get-tuple-element.91) | copy-start | bytes 100
  217.3 7.3 %copy-start.15 = (pred[32]{0:T(512)(128)(4,1)S(1)}, pred[32]{0:T(512)(128)(4,1)}, u32[]{:S(2)}) copy-start(pred[32]{0:T(512)(128)(4,1)} %get-tuple-element.92) | copy-start | bytes 100
  217.3 7.3 %copy-start.17 = (pred[32]{0:T(512)(128)(4,1)S(1)}, pred[32]{0:T(512)(128)(4,1)}, u32[]{:S(2)}) copy-start(pred[32]{0:T(512)(128)(4,1)} %get-tuple-element.93) | copy-start | bytes 100
  217.3 7.3 %copy-start.19 = (pred[32]{0:T(512)(128)(4,1)S(1)}, pred[32]{0:T(512)(128)(4,1)}, u32[]{:S(2)}) copy-start(pred[32]{0:T(512)(128)(4,1)} %get-tuple-element.94) | copy-start | bytes 100
  217.3 7.3 %copy-start.21 = (pred[32]{0:T(512)(128)(4,1)S(1)}, pred[32]{0:T(512)(128)(4,1)}, u32[]{:S(2)}) copy-start(pred[32]{0:T(512)(128)(4,1)} %get-tuple-element.95) | copy-start | bytes 100
  217.3 7.3 %copy-start.23 = (pred[32]{0:T(512)(128)(4,1)S(1)}, pred[32]{0:T(512)(128)(4,1)}, u32[]{:S(2)}) copy-start(pred[32]{0:T(512)(128)(4,1)} %get-tuple-element.96) | copy-start | bytes 100
  217.3 28.7 %all-to-all-start.7 = ((f32[16,96,128]{2,1,0:T(8,128)}), f32[16,96,128]{2,1,0:T(8,128)S(1)}, u32[]{:S(2)}, u32[]{:S(2)}) async-start(f32[16,96,128]{2,1,0:T(8,128)} %pad_maximum_fusion.1), calls=%async_computation.7 | async-start | bytes 1572864 | tf_op jit(solution)/shard_map/all_to_all | solution.py:13
  247.2 1.6 copy-start.4
  252.4 26.9 %all-to-all-start.8 = ((f32[32,40,128]{2,1,0:T(8,128)}), f32[32,40,128]{2,1,0:T(8,128)S(1)}, u32[]{:S(2)}, u32[]{:S(2)}) async-start(f32[32,40,128]{2,1,0:T(8,128)} %select_maximum_fusion), calls=%async_computation.8 | async-start | bytes 1310720 | tf_op jit(solution)/shard_map/all_to_all | solution.py:13
  (13 other events, 9.9 us)

commit v4 on v3

--- a/solution.py
+++ b/solution.py
@@ -51,8 +51,8 @@
 def deep_kernel(meta, slab, a_ref, c_ref, out, drive):
     slots, depth, tile, _ = slab.shape
     nr, rows, _ = out.shape
-    half = a_ref.shape[2] // LANES
-    own = rows // half
+    tiles = drive.shape[0] // tile
+    own = rows // tiles
     drive[...] = jnp.zeros_like(drive)
     for slot in range(slots):
         a_tile = a_ref[meta[0, slot]]
@@ -67,21 +67,16 @@
             total = total + deep * c_rows[k : k + 1, :]
         spot = pl.ds(pl.multiple_of(meta[1, slot] * tile, tile), tile)
         drive[spot, :] = drive[spot, :] + jnp.where(meta[3, slot] > 0, total, 0.0)
-    for h in range(half):
-        part = drive[:, h * LANES : (h + 1) * LANES]
-        out[:, own * h : own * (h + 1), :] = part.reshape(nr, own, LANES)
-
-
-def wide_kernel(meta, got, slab, a_ref, c_ref, out, b_all, deep_c):
+    for t in range(tiles):
+        part = drive[t * tile : (t + 1) * tile, :].T
+        out[:, own * t : own * (t + 1), :] = part.reshape(nr, own, LANES)
+
+
+def wide_kernel(meta, b_all, slab, a_ref, c_ref, out, deep_c):
     slots, depth, tile, _ = slab.shape
-    nr = got.shape[0]
     nc = out.shape[0]
     rank = a_ref.shape[2]
-    half, qa, qb = rank // LANES, rank // nc, rank // nr
-    own = b_all.shape[0] // nr
-    for h in range(half):
-        part = got[:, own * h : own * (h + 1), :]
-        b_all[:, h * LANES : (h + 1) * LANES] = part.reshape(nr * own, LANES)
+    half, qa = rank // LANES, rank // nc
     deep_c[...] = jnp.zeros_like(deep_c)
     for slot in range(slots):
         b_tile = b_all[pl.ds(pl.multiple_of(meta[1, slot] * tile, tile), tile), :]
@@ -105,13 +100,7 @@
         part = gram_b[:, h * LANES : (h + 1) * LANES]
         out[:, at : at + qa, :] = part.reshape(nc, qa, LANES)
         at += qa
-    pieces = got[:, own * half : own * half + qa, :].astype(jnp.float32)
-    piece = jnp.sum(pieces, axis=0)
-    first = slots * depth
-    moved = pltpu.roll(piece, first, 1) + pltpu.roll(piece, first - qb, 1)
-    lane = lax.broadcasted_iota(jnp.int32, piece.shape, 1)
-    moved = jnp.where((lane >= first) & (lane < first + qb), moved, 0.0)
-    out[:, at : at + qa, :] = deep_c[...].T.reshape(nc, qa, LANES) + moved[None]
+    out[:, at : at + qa, :] = deep_c[...].T.reshape(nc, qa, LANES)
 
 
 def call(kernel, shape, scratch, flops, moved, operands):
@@ -135,10 +124,50 @@
     return jnp.maximum(state - rate * (push - drive) / scale[None, :, None], 0.0)
 
 
-def bump_rows(state, hess, drive, rate):
-    scale = jnp.sum(jnp.abs(hess), axis=1) + 1e-06
-    push = jnp.dot(state, hess, precision=HIGH, preferred_element_type=jnp.float32)
-    return jnp.maximum(state - rate * (push - drive) / scale[None, :], 0.0)
+def steps_of(n):
+    masks = [1 << b for b in range(n.bit_length() - 1)]
+    return masks[::-1][::2] + masks[::-1][1::2]
+
+
+def flip(x, axis, mask):
+    n = lax.axis_size(axis)
+    return lax.ppermute(x, axis, [(i, i ^ mask) for i in range(n)])
+
+
+def ordered(x, order, n):
+    masks = order[::-1]
+    dims = [masks.index(m) for m in sorted(masks, reverse=True)]
+    rest = list(range(len(masks), x.ndim))
+    return x.transpose(dims + rest).reshape((n,) + x.shape[len(masks) :])
+
+
+def gather_by_flips(x, axis):
+    n, me = lax.axis_size(axis), lax.axis_index(axis)
+    order = steps_of(n)
+    for mask in order:
+        y = flip(x, axis, mask)
+        upper = (me & mask) > 0
+        x = jnp.stack([jnp.where(upper, y, x), jnp.where(upper, x, y)])
+    return ordered(x, order, n)
+
+
+def swap_by_flips(x, axis):
+    n, me = lax.axis_size(axis), lax.axis_index(axis)
+    order = steps_of(n)
+    bits = n.bit_length() - 1
+    masks = sorted(order, reverse=True)
+    rest = x.shape[1:]
+    x = x.reshape((2,) * bits + rest)
+    left = list(masks)
+    for mask in order:
+        at = len(masks) - len(left) + left.index(mask)
+        upper = (me & mask) > 0
+        zero, one = lax.index_in_dim(x, 0, at, False), lax.index_in_dim(x, 1, at, False)
+        y = flip(jnp.where(upper, zero, one), axis, mask)
+        keep = jnp.where(upper, one, zero)
+        x = jnp.stack([jnp.where(upper, y, keep), jnp.where(upper, keep, y)])
+        left.remove(mask)
+    return ordered(x, order, n)
 
 
 def lanes(x):
@@ -147,7 +176,7 @@
 
 def shards(bricks, brick_coords, brick_counts, step_sizes, init_a, init_b, init_c):
     nr, nc = lax.axis_size("row"), lax.axis_size("col")
-    col = lax.axis_index("col")
+    row, col = lax.axis_index("row"), lax.axis_index("col")
     slab, places, own = bricks[0, 0], brick_coords[0, 0], brick_counts[0, 0]
     slots, depth, tile, _ = slab.shape
     sweeps = step_sizes.shape[0]
@@ -167,11 +196,17 @@
     mine = pad_lanes(jnp.where(live[None, :], places, -1).astype(f32).reshape(1, -1))
     mine = jnp.broadcast_to(mine, (8, LANES))
 
-    state_b = init_b[0]
     c_bf = init_c.astype(bf16)
 
     for sweep in range(sweeps):
-        b_bf = state_b.astype(bf16)
+        if sweep == 0:
+            b_rows = gather_by_flips(init_b[0], "row").reshape(tiles_b, tile, rank)
+            bt3 = jnp.swapaxes(b_rows, 1, 2)
+        else:
+            chunk = gather_by_flips(new_b.reshape(-1, LANES), "row")
+            bt3 = jnp.swapaxes(chunk.reshape(nr, tiles_b, qb, tile), 0, 1).reshape(tiles_b, rank, tile)
+            b_rows = jnp.swapaxes(bt3, 1, 2)
+        b_all = b_rows.reshape(tiles_b * tile, rank).astype(bf16)
         if sweep == 0:
             got = swap(spread(jnp.concatenate([fold(init_a[0]), mine], 0), nc), "col")
             rows, spots_col = take(got, [own_a * half, 8])
@@ -191,26 +226,19 @@
         a_all = a_bf3.reshape(tiles_a * tile, rank)
         gram_a = gram(a_all)
         slice_a = lax.dynamic_slice_in_dim(gram_a, col * qa, qa, 0)
-        slice_a = jnp.swapaxes(slice_a.reshape(qa, nr, qb), 0, 1)
-        high = lax.reduce_precision(slice_a, 8, 7)
-        pair = pad_lanes(jnp.concatenate([high, slice_a - high], axis=2).astype(bf16))
-        send = jnp.concatenate(
-            [jnp.broadcast_to(fold(b_bf)[None], (nr, own_b * half, LANES)), fold(pair)], axis=1
-        )
-        got = swap(send, "row")
         gram_c = gram(c_bf)
         work = 2 * slots * depth * tile * tile * rank
         blocks = call(
             deep_kernel,
-            (nr, own_b * half, LANES),
+            (nr, tiles_b * qb, LANES),
             [pltpu.VMEM((tiles_b * tile, rank), f32)],
             work, slab.size * 2, (meta, slab, a_bf3, c_bf),
         )
         send = call(
             wide_kernel,
             (nc, qa * (slots + half + 1), LANES),
-            [pltpu.VMEM((tiles_b * tile, rank), bf16), pltpu.VMEM((LANES, rank), f32)],
-            work, slab.size * 2, (meta, got, slab, a_bf3, c_bf),
+            [pltpu.VMEM((LANES, rank), f32)],
+            work, slab.size * 2, (meta, b_all, slab, a_bf3, c_bf),
         )
         got = swap(send, "col")
         *a_got, s_got, m_got = take(got, [qa] * slots + [qa * half, qa])
@@ -227,22 +255,27 @@
         onehot = (spots_col[:, 2, :, None] == lax.iota(jnp.int32, layers)).astype(f32)
         c_got = m_got[:, :, : slots * depth].reshape(nc, qa, slots, depth)
         drive_c = jnp.einsum("sqmk,smb->qbk", c_got, onehot, precision=HIGH).reshape(qa, length)
-        strip = m_got[:, :, slots * depth : slots * depth + qb].reshape(rank, qb).T
         pieces = [
             blocks,
-            jnp.broadcast_to(fold(strip)[None], (nr, qb * half, LANES)),
+            fold(gram_a.reshape(nr, qb, rank)),
+            jnp.broadcast_to(fold(slice_a)[None], (nr, qa * half, LANES)),
             jnp.broadcast_to(fold(drive_c)[None], (nr, qa * tiles_c, LANES)),
         ]
         got = swap(jnp.concatenate(pieces, axis=1), "row")
-        b_got, s_got, c_got = take(got, [p.shape[1] for p in pieces])
-        mine_b = unfold(jnp.sum(b_got, axis=0), rank)
-        sa = unfold(s_got, rank).reshape(rank, rank)
-        mine_c = jnp.sum(c_got, axis=0).reshape(tiles_c, qa, LANES)
+        total = jnp.sum(got, axis=0)[None]
+        b_got, r_got, s_got, c_got = [v[0] for v in take(total, [p.shape[1] for p in pieces])]
+        mine_b = b_got.reshape(tiles_b, qb, tile)
+        sa_r, sa_c = unfold(r_got, rank), unfold(s_got, rank)
+        mine_c = c_got.reshape(tiles_c, qa, LANES)
         cut = lambda x, axis=0: lax.dynamic_slice_in_dim(x, col * qa, qa, axis)
+        cut_r = lambda x, axis=0: lax.dynamic_slice_in_dim(x, row * qb, qb, axis)
         rate = step_sizes[sweep]
         new_a = bump(cut(at3, 1), sb_c * cut(gram_c), at3, drive_a, rate[0])
-        state_b = bump_rows(state_b, sa * gram_c, mine_b, rate[1])
-        new_c = bump(cut(ct3, 1), cut(sa) * sb_c, ct3, mine_c, rate[2])
+        new_b = bump(cut_r(bt3, 1), sa_r * cut_r(gram_c), bt3, mine_b, rate[1])
+        new_c = bump(cut(ct3, 1), sa_c * sb_c, ct3, mine_c, rate[2])
+    per_b = tile // own_b
+    own = new_b.reshape(tiles_b, qb, per_b, own_b).transpose(0, 2, 1, 3).reshape(nr, -1, LANES)
+    out_b = swap_by_flips(own, "row").reshape(rank, own_b).T
     per_a = tile // own_a
     own = new_a.reshape(tiles_a, qa, per_a, own_a).transpose(0, 2, 1, 3).reshape(nc, qa, own_a)
     own = fold(pad_lanes(own))
@@ -252,7 +285,7 @@
     out_a = unfold(a_got, own_a + -own_a % LANES)[:, :, :own_a].reshape(rank, own_a).T
     out_c = jnp.swapaxes(c_got.reshape(nc, tiles_c, qa, LANES), 0, 1).reshape(tiles_c, rank, LANES)
     out_c = jnp.swapaxes(out_c, 1, 2).reshape(length, rank)
-    return out_a[None], state_b[None], out_c
+    return out_a[None], out_b[None], out_c
 
 
 def solution(mesh):

time: 283 us -> 305 us (1.078); the launches traced: 281 us -> 300 us
  starting transfers between devices: 74.9 us -> 109 us
  waiting for transfers between devices: 146 us -> 125 us
  local copies, waits for them, and re-layouts: 26 us -> 31.9 us
    all_to_all x9 -> x7, waiting for transfers between devices: 146 us -> 74.2 us  [swap(): return lax.all_to_all(x, axis, 0, 0, tiled=True)]
    ppermute x0 -> x12, waiting for transfers between devices: none -> 51.2 us  [flip(): return lax.ppermute(x, axis, [(i, i ^ mask) for i in range(n)])]
    ppermute x0 -> x12, starting transfers between devices: none -> 32.4 us  [flip(): return lax.ppermute(x, axis, [(i, i ^ mask) for i in range(n)])]
    unnamed x60 -> x92, local copies, waits for them, and re-layouts: 7.71 us -> 14.9 us
    concatenate x8 -> x0, other arithmetic: 3.45 us -> none  [the longest x2 1.89 us: shards(): got = swap(jnp.concatenate(pieces, axis=1), 'row')]
    all_to_all x9 -> x7, starting transfers between devices: 74.9 us -> 76.1 us  [swap(): return lax.all_to_all(x, axis, 0, 0, tiled=True)]
  transfers between devices with their start and end apart: 9 -> 19, of which waited for: 9 -> 14; matrix products, arithmetic and copies ran while one was open for 5% -> 8% of each run, Pallas kernels for 1% -> 0%
where the time goes in v4:
time: 305 us; the launch traced here: 300 us
  waiting for transfers between devices  125 us (41%)
  starting transfers between devices  109 us (36%)
  local copies, waits for them, and re-layouts  31.9 us (10%)
  other arithmetic  16.8 us (6%)
  Pallas kernels  7.73 us (3%)
  matrix products  6.84 us (2%)
    all_to_all x7, starting transfers between devices, swap(): return lax.all_to_all(x, axis, 0, 0, tiled=True)  76.1 us
    all_to_all x7, waiting for transfers between devices, swap(): return lax.all_to_all(x, axis, 0, 0, tiled=True)  74.2 us
    ppermute x12, waiting for transfers between devices, flip(): return lax.ppermute(x, axis, [(i, i ^ mask) for i in range(n)])  51.2 us
    ppermute x12, starting transfers between devices, flip(): return lax.ppermute(x, axis, [(i, i ^ mask) for i in range(n)])  32.4 us
    unnamed x92, local copies, waits for them, and re-layouts  14.9 us
    pallas_call x4, Pallas kernels, call(): pl.pallas_call(kernel, out_shape=jax.ShapeDtypeStruct(shape, jnp.float32)...  7.73 us
  transfers between devices with their start and end apart: 19, of which 14 were waited for; matrix products, arithmetic and copies ran while one was open for 8% of the time, Pallas kernels for 0%

profile of v4, /device:TPU:1, one launch (start us, length us, event | category | flops | bytes accessed | tf_op | source)
XLA Modules:
  0.0 299.7 jit_solution(5149875101703828447)
XLA Ops:
  0.6 5.5 %collective-permute-start = (f32[16,256]{1,0:T(8,128)}, f32[16,256]{1,0:T(8,128)S(1)}, u32[]{:S(2)}, u32[]{:S(2)}) collective-permute-start(f32[16,256]{1,0:T(8,128)} %bitcast.495), channel_id=1, source_target_pairs={{0,256},{32,288},{64,320},{96,352},{128,384},{160,416},{192,448},{... | collective-permute-start | bytes 49160 | tf_op jit(solution)/shard_map/ppermute | solution.py:134
  8.7 16.8 %all-to-all-start = ((f32[32,40,128]{2,1,0:T(8,128)}), f32[32,40,128]{2,1,0:T(8,128)S(1)}, u32[]{:S(2)}, u32[]{:S(2)}) async-start(f32[32,40,128]{2,1,0:T(8,128)} %broadcast_in_dim.216), calls=%async_computation | async-start | bytes 1310720 | tf_op jit(solution)/shard_map/all_to_all | solution.py:13
  30.5 6.4 %collective-permute-done.1 = f32[2,16,256]{2,1,0:T(8,128)S(1)} collective-permute-done((f32[2,16,256]{2,1,0:T(8,128)S(1)}, f32[2,16,256]{2,1,0:T(8,128)S(1)}, u32[]{:S(2)}, u32[]{:S(2)}) %collective-permute-start.1) | collective-permute-done | bytes 32800 | tf_op jit(solution)/shard_map/ppermute | solution.py:134
  39.2 3.1 %collective-permute-done.2 = f32[2,2,16,256]{3,2,0,1:T(8,128)S(1)} collective-permute-done((f32[2,2,16,256]{3,2,0,1:T(8,128)S(1)}, f32[2,2,16,256]{3,2,0,1:T(8,128)S(1)}, u32[]{:S(2)}, u32[]{:S(2)}) %collective-permute-start.2) | collective-permute-done | bytes 65568 | tf_op jit(solution)/shard_map/ppermute | solution.py:134
  42.3 4.0 %collective-permute-start.3 = (f32[2,2,2,16,256]{4,3,1,0,2:T(8,128)S(1)}, f32[2,2,2,16,256]{4,3,1,0,2:T(8,128)S(1)}, u32[]{:S(2)}, u32[]{:S(2)}) collective-permute-start(f32[2,2,2,16,256]{4,3,1,0,2:T(8,128)S(1)} %pad_maximum_fusion.2), channel_id=1, source_target_pairs={{0,32},{32,0},{64,96},{96,64},{128,160},{160,128},{192,224},{224,1... | collective-permute-start | bytes 393224 | tf_op jit(solution)/shard_map/ppermute | solution.py:134
  54.5 19.4 %all-to-all-start.1 = ((f32[32,40,128]{2,1,0:T(8,128)}), f32[32,40,128]{2,1,0:T(8,128)}, u32[]{:S(2)}, u32[]{:S(2)}) async-start(f32[32,40,128]{2,1,0:T(8,128)} %shard_map.94), calls=%async_computation.1 | async-start | bytes 1310720 | tf_op jit(solution)/shard_map/all_to_all | solution.py:13
  78.1 16.3 %all-to-all-done.1 = f32[32,40,128]{2,1,0:T(8,128)} async-done(((f32[32,40,128]{2,1,0:T(8,128)}), f32[32,40,128]{2,1,0:T(8,128)}, u32[]{:S(2)}, u32[]{:S(2)}) %all-to-all-start.1) | async-done | bytes 655392 | tf_op jit(solution)/shard_map/all_to_all | solution.py:13
  96.6 5.1 %all-to-all-start.2 = ((f32[16,112,128]{2,1,0:T(8,128)}), f32[16,112,128]{2,1,0:T(8,128)S(1)}, u32[]{:S(2)}, u32[]{:S(2)}) async-start(f32[16,112,128]{2,1,0:T(8,128)} %broadcast_dynamic-update-slice_fusion.1), calls=%async_computation.2 | async-start | bytes 1835008 | tf_op jit(solution)/shard_map/all_to_all | solution.py:13
  106.3 19.7 %all-to-all-done.2 = f32[16,112,128]{2,1,0:T(8,128)S(1)} async-done(((f32[16,112,128]{2,1,0:T(8,128)}), f32[16,112,128]{2,1,0:T(8,128)S(1)}, u32[]{:S(2)}, u32[]{:S(2)}) %all-to-all-start.2) | async-done | bytes 917536 | tf_op jit(solution)/shard_map/all_to_all | solution.py:13
  139.5 7.4 %all-to-all-start.3 = ((f32[32,64,128]{2,1,0:T(8,128)}), f32[32,64,128]{2,1,0:T(8,128)}, u32[]{:S(2)}, u32[]{:S(2)}) async-start(f32[32,64,128]{2,1,0:T(8,128)} %broadcast_in_dim.238), calls=%async_computation.3 | async-start | bytes 2097152 | tf_op jit(solution)/shard_map/all_to_all | solution.py:13
  150.7 3.9 %collective-permute-done.4 = f32[32,128]{1,0:T(8,128)S(1)} collective-permute-done((f32[32,128]{1,0:T(8,128)S(1)}, f32[32,128]{1,0:T(8,128)S(1)}, u32[]{:S(2)}, u32[]{:S(2)}) %collective-permute-start.4) | collective-permute-done | bytes 16416 | tf_op jit(solution)/shard_map/ppermute | solution.py:134
  156.6 13.9 %collective-permute-done.5 = f32[2,32,128]{2,1,0:T(8,128)S(1)} collective-permute-done((f32[2,32,128]{2,1,0:T(8,128)S(1)}, f32[2,32,128]{2,1,0:T(8,128)S(1)}, u32[]{:S(2)}, u32[]{:S(2)}) %collective-permute-start.5) | collective-permute-done | bytes 32800 | tf_op jit(solution)/shard_map/ppermute | solution.py:134
  172.5 3.5 %collective-permute-done.6 = f32[2,2,32,128]{3,2,0,1:T(8,128)S(1)} collective-permute-done((f32[2,2,32,128]{3,2,0,1:T(8,128)S(1)}, f32[2,2,32,128]{3,2,0,1:T(8,128)S(1)}, u32[]{:S(2)}, u32[]{:S(2)}) %collective-permute-start.6) | collective-permute-done | bytes 65568 | tf_op jit(solution)/shard_map/ppermute | solution.py:134
  176.0 3.8 %collective-permute-start.7 = (f32[2,2,2,32,128]{4,3,1,0,2:T(8,128)S(1)}, f32[2,2,2,32,128]{4,3,1,0,2:T(8,128)S(1)}, u32[]{:S(2)}, u32[]{:S(2)}) collective-permute-start(f32[2,2,2,32,128]{4,3,1,0,2:T(8,128)S(1)} %pad_maximum_fusion.3), channel_id=1, source_target_pairs={{0,32},{32,0},{64,96},{96,64},{128,160},{160,128},{192,224},{224,1... | collective-permute-start | bytes 393224 | tf_op jit(solution)/shard_map/ppermute | solution.py:134
  189.0 2.5 shard_map.96
  191.5 13.2 %all-to-all-start.4 = ((f32[32,40,128]{2,1,0:T(8,128)}), f32[32,40,128]{2,1,0:T(8,128)S(1)}, u32[]{:S(2)}, u32[]{:S(2)}) async-start(f32[32,40,128]{2,1,0:T(8,128)} %shard_map.96), calls=%async_computation.4 | async-start | bytes 1310720 | tf_op jit(solution)/shard_map/all_to_all | solution.py:13
  207.7 17.2 %all-to-all-done.4 = f32[32,40,128]{2,1,0:T(8,128)S(1)} async-done(((f32[32,40,128]{2,1,0:T(8,128)}), f32[32,40,128]{2,1,0:T(8,128)S(1)}, u32[]{:S(2)}, u32[]{:S(2)}) %all-to-all-start.4) | async-done | bytes 655392 | tf_op jit(solution)/shard_map/all_to_all | solution.py:13
  226.3 6.8 %all-to-all-start.5 = ((f32[16,112,128]{2,1,0:T(8,128)}), f32[16,112,128]{2,1,0:T(8,128)S(1)}, u32[]{:S(2)}, u32[]{:S(2)}) async-start(f32[16,112,128]{2,1,0:T(8,128)} %broadcast_dynamic-update-slice_fusion), calls=%async_computation.5 | async-start | bytes 1835008 | tf_op jit(solution)/shard_map/all_to_all | solution.py:13
  236.4 20.9 %all-to-all-done.5 = f32[16,112,128]{2,1,0:T(8,128)S(1)} async-done(((f32[16,112,128]{2,1,0:T(8,128)}), f32[16,112,128]{2,1,0:T(8,128)S(1)}, u32[]{:S(2)}, u32[]{:S(2)}) %all-to-all-start.5) | async-done | bytes 917536 | tf_op jit(solution)/shard_map/all_to_all | solution.py:13
  261.3 2.5 collective-permute-start.8
  266.9 7.3 %all-to-all-start.6 = ((f32[32,40,128]{2,1,0:T(8,128)}), f32[32,40,128]{2,1,0:T(8,128)S(1)}, u32[]{:S(2)}, u32[]{:S(2)}) async-start(f32[32,40,128]{2,1,0:T(8,128)} %select_maximum_fusion), calls=%async_computation.6 | async-start | bytes 1310720 | tf_op jit(solution)/shard_map/all_to_all | solution.py:13
  276.2 11.6 %collective-permute-done.9 = f32[2,2,2,2,128]{4,3,2,1,0:T(2,128)S(1)} collective-permute-done((f32[2,2,2,2,128]{4,3,2,1,0:T(2,128)S(1)}, f32[2,2,2,2,128]{4,3,2,1,0:T(2,128)S(1)}, u32[]{:S(2)}, u32[]{:S(2)}) %collective-permute-start.9) | collective-permute-done | bytes 8224 | tf_op jit(solution)/shard_map/ppermute | solution.py:134
  289.8 2.8 collective-permute-done.10
  294.5 2.6 collective-permute-done.11
  (285 shorter events, 80.8 us)
Async XLA Ops:
  0.6 7.1 %copy-start.16 = (f32[1,16,256]{2,1,0:T(8,128)S(1)}, f32[1,16,256]{2,1,0:T(8,128)}, u32[]{:S(2)}) copy-start(f32[1,16,256]{2,1,0:T(8,128)} %param.11) | copy-start | bytes 49156
  0.6 26.8 %collective-permute-start = (f32[16,256]{1,0:T(8,128)}, f32[16,256]{1,0:T(8,128)S(1)}, u32[]{:S(2)}, u32[]{:S(2)}) collective-permute-start(f32[16,256]{1,0:T(8,128)} %bitcast.495), channel_id=1, source_target_pairs={{0,256},{32,288},{64,320},{96,352},{128,384},{160,416},{192,448},{... | collective-permute-start | bytes 49160 | tf_op jit(solution)/shard_map/ppermute | solution.py:134
  8.7 16.8 %copy-start.1 = (f32[512,256]{1,0:T(8,128)S(1)}, f32[512,256]{1,0:T(8,128)}, u32[]{:S(2)}) copy-start(f32[512,256]{1,0:T(8,128)} %param.13) | copy-start | bytes 1572868
  8.7 40.8 %all-to-all-start = ((f32[32,40,128]{2,1,0:T(8,128)}), f32[32,40,128]{2,1,0:T(8,128)S(1)}, u32[]{:S(2)}, u32[]{:S(2)}) async-start(f32[32,40,128]{2,1,0:T(8,128)} %broadcast_in_dim.216), calls=%async_computation | async-start | bytes 1310720 | tf_op jit(solution)/shard_map/all_to_all | solution.py:13
  28.1 8.9 %collective-permute-start.1 = (f32[2,16,256]{2,1,0:T(8,128)S(1)}, f32[2,16,256]{2,1,0:T(8,128)S(1)}, u32[]{:S(2)}, u32[]{:S(2)}) collective-permute-start(f32[2,16,256]{2,1,0:T(8,128)S(1)} %pad_maximum_fusion.6), channel_id=1, source_target_pairs={{0,64},{32,96},{64,0},{96,32},{128,192},{160,224},{192,128},{224,1... | collective-permute-start | bytes 98312 | tf_op jit(solution)/shard_map/ppermute | solution.py:134
  37.0 5.3 %collective-permute-start.2 = (f32[2,2,16,256]{3,2,0,1:T(8,128)S(1)}, f32[2,2,16,256]{3,2,0,1:T(8,128)S(1)}, u32[]{:S(2)}, u32[]{:S(2)}) collective-permute-start(f32[2,2,16,256]{3,2,0,1:T(8,128)S(1)} %pad_maximum_fusion.4), channel_id=1, source_target_pairs={{0,128},{32,160},{64,192},{96,224},{128,0},{160,32},{192,64},{224,... | collective-permute-start | bytes 196616 | tf_op jit(solution)/shard_map/ppermute | solution.py:134
  42.3 6.3 %collective-permute-start.3 = (f32[2,2,2,16,256]{4,3,1,0,2:T(8,128)S(1)}, f32[2,2,2,16,256]{4,3,1,0,2:T(8,128)S(1)}, u32[]{:S(2)}, u32[]{:S(2)}) collective-permute-start(f32[2,2,2,16,256]{4,3,1,0,2:T(8,128)S(1)} %pad_maximum_fusion.2), channel_id=1, source_target_pairs={{0,32},{32,0},{64,96},{96,64},{128,160},{160,128},{192,224},{224,1... | collective-permute-start | bytes 393224 | tf_op jit(solution)/shard_map/ppermute | solution.py:134
  54.5 39.9 %all-to-all-start.1 = ((f32[32,40,128]{2,1,0:T(8,128)}), f32[32,40,128]{2,1,0:T(8,128)}, u32[]{:S(2)}, u32[]{:S(2)}) async-start(f32[32,40,128]{2,1,0:T(8,128)} %shard_map.94), calls=%async_computation.1 | async-start | bytes 1310720 | tf_op jit(solution)/shard_map/all_to_all | solution.py:13
  96.6 29.3 %all-to-all-start.2 = ((f32[16,112,128]{2,1,0:T(8,128)}), f32[16,112,128]{2,1,0:T(8,128)S(1)}, u32[]{:S(2)}, u32[]{:S(2)}) async-start(f32[16,112,128]{2,1,0:T(8,128)} %broadcast_dynamic-update-slice_fusion.1), calls=%async_computation.2 | async-start | bytes 1835008 | tf_op jit(solution)/shard_map/all_to_all | solution.py:13
  139.5 7.5 %copy-start.13 = (f32[2,128,16]{1,2,0:T(8,128)S(1)}, f32[2,128,16]{1,2,0:T(8,128)}, u32[]{:S(2)}) copy-start(f32[2,128,16]{1,2,0:T(8,128)} %copy.298) | copy-start | bytes 49156
  139.5 7.5 %copy-start.14 = (f32[1,32,128]{2,1,0:T(8,128)S(1)}, f32[1,32,128]{2,1,0:T(8,128)}, u32[]{:S(2)}) copy-start(f32[1,32,128]{2,1,0:T(8,128)} %get-tuple-element.79) | copy-start | bytes 49156
  139.5 7.5 %copy-start.15 = (f32[1,16,128]{2,1,0:T(8,128)S(1)}, f32[1,16,128]{2,1,0:T(8,128)}, u32[]{:S(2)}) copy-start(f32[1,16,128]{2,1,0:T(8,128)} %convolution_bitcast_fusion.6) | copy-start | bytes 24580
  139.5 44.3 %all-to-all-start.3 = ((f32[32,64,128]{2,1,0:T(8,128)}), f32[32,64,128]{2,1,0:T(8,128)}, u32[]{:S(2)}, u32[]{:S(2)}) async-start(f32[32,64,128]{2,1,0:T(8,128)} %broadcast_in_dim.238), calls=%async_computation.3 | async-start | bytes 2097152 | tf_op jit(solution)/shard_map/all_to_all | solution.py:13
  148.3 6.4 %collective-permute-start.4 = (f32[32,128]{1,0:T(8,128)S(1)}, f32[32,128]{1,0:T(8,128)S(1)}, u32[]{:S(2)}, u32[]{:S(2)}) collective-permute-start(f32[32,128]{1,0:T(8,128)S(1)} %bitcast.493), channel_id=1, source_target_pairs={{0,256},{32,288},{64,320},{96,352},{128,384},{160,416},{192,448},{... | collective-permute-start | bytes 49160 | tf_op jit(solution)/shard_map/ppermute | solution.py:134
  154.7 15.9 %collective-permute-start.5 = (f32[2,32,128]{2,1,0:T(8,128)S(1)}, f32[2,32,128]{2,1,0:T(8,128)S(1)}, u32[]{:S(2)}, u32[]{:S(2)}) collective-permute-start(f32[2,32,128]{2,1,0:T(8,128)S(1)} %pad_maximum_fusion.8), channel_id=1, source_target_pairs={{0,64},{32,96},{64,0},{96,32},{128,192},{160,224},{192,128},{224,1... | collective-permute-start | bytes 98312 | tf_op jit(solution)/shard_map/ppermute | solution.py:134
  170.6 5.4 %collective-permute-start.6 = (f32[2,2,32,128]{3,2,0,1:T(8,128)S(1)}, f32[2,2,32,128]{3,2,0,1:T(8,128)S(1)}, u32[]{:S(2)}, u32[]{:S(2)}) collective-permute-start(f32[2,2,32,128]{3,2,0,1:T(8,128)S(1)} %pad_maximum_fusion.5), channel_id=1, source_target_pairs={{0,128},{32,160},{64,192},{96,224},{128,0},{160,32},{192,64},{224,... | collective-permute-start | bytes 196616 | tf_op jit(solution)/shard_map/ppermute | solution.py:134
  176.0 6.2 %collective-permute-start.7 = (f32[2,2,2,32,128]{4,3,1,0,2:T(8,128)S(1)}, f32[2,2,2,32,128]{4,3,1,0,2:T(8,128)S(1)}, u32[]{:S(2)}, u32[]{:S(2)}) collective-permute-start(f32[2,2,2,32,128]{4,3,1,0,2:T(8,128)S(1)} %pad_maximum_fusion.3), channel_id=1, source_target_pairs={{0,32},{32,0},{64,96},{96,64},{128,160},{160,128},{192,224},{224,1... | collective-permute-start | bytes 393224 | tf_op jit(solution)/shard_map/ppermute | solution.py:134
  191.5 33.5 %all-to-all-start.4 = ((f32[32,40,128]{2,1,0:T(8,128)}), f32[32,40,128]{2,1,0:T(8,128)S(1)}, u32[]{:S(2)}, u32[]{:S(2)}) async-start(f32[32,40,128]{2,1,0:T(8,128)} %shard_map.96), calls=%async_computation.4 | async-start | bytes 1310720 | tf_op jit(solution)/shard_map/all_to_all | solution.py:13
  226.3 31.0 %all-to-all-start.5 = ((f32[16,112,128]{2,1,0:T(8,128)}), f32[16,112,128]{2,1,0:T(8,128)S(1)}, u32[]{:S(2)}, u32[]{:S(2)}) async-start(f32[16,112,128]{2,1,0:T(8,128)} %broadcast_dynamic-update-slice_fusion), calls=%async_computation.5 | async-start | bytes 1835008 | tf_op jit(solution)/shard_map/all_to_all | solution.py:13
  261.3 12.9 %collective-permute-start.8 = (f32[2,2,2,2,128]{4,3,2,1,0:T(2,128)S(1)}, f32[2,2,2,2,128]{4,3,2,1,0:T(2,128)S(1)}, u32[]{:S(2)}, u32[]{:S(2)}) collective-permute-start(f32[2,2,2,2,128]{4,3,2,1,0:T(2,128)S(1)} %select_n.334), channel_id=1, source_target_pairs={{0,256},{32,288},{64,320},{96,352},{128,384},{160,416},{192,448},{... | collective-permute-start | bytes 24584 | tf_op jit(solution)/shard_map/ppermute | solution.py:134
  266.9 31.0 %all-to-all-start.6 = ((f32[32,40,128]{2,1,0:T(8,128)}), f32[32,40,128]{2,1,0:T(8,128)S(1)}, u32[]{:S(2)}, u32[]{:S(2)}) async-start(f32[32,40,128]{2,1,0:T(8,128)} %select_maximum_fusion), calls=%async_computation.6 | async-start | bytes 1310720 | tf_op jit(solution)/shard_map/all_to_all | solution.py:13
  274.3 13.6 %collective-permute-start.9 = (f32[2,2,2,2,128]{4,3,2,1,0:T(2,128)S(1)}, f32[2,2,2,2,128]{4,3,2,1,0:T(2,128)S(1)}, u32[]{:S(2)}, u32[]{:S(2)}) collective-permute-start(f32[2,2,2,2,128]{4,3,2,1,0:T(2,128)S(1)} %fusion.34), channel_id=1, source_target_pairs={{0,64},{32,96},{64,0},{96,32},{128,192},{160,224},{192,128},{224,1... | collective-permute-start | bytes 24584 | tf_op jit(solution)/shard_map/ppermute | solution.py:134
  287.9 4.7 %collective-permute-start.10 = (f32[2,2,2,2,128]{4,3,2,1,0:T(2,128)S(1)}, f32[2,2,2,2,128]{4,3,2,1,0:T(2,128)S(1)}, u32[]{:S(2)}, u32[]{:S(2)}) collective-permute-start(f32[2,2,2,2,128]{4,3,2,1,0:T(2,128)S(1)} %fusion.33), channel_id=1, source_target_pairs={{0,128},{32,160},{64,192},{96,224},{128,0},{160,32},{192,64},{224,... | collective-permute-start | bytes 24584 | tf_op jit(solution)/shard_map/ppermute | solution.py:134
  292.6 4.5 %collective-permute-start.11 = (f32[2,2,2,2,128]{4,3,2,1,0:T(2,128)S(1)}, f32[2,2,2,2,128]{4,3,2,1,0:T(2,128)S(1)}, u32[]{:S(2)}, u32[]{:S(2)}) collective-permute-start(f32[2,2,2,2,128]{4,3,2,1,0:T(2,128)S(1)} %fusion.32), channel_id=1, source_target_pairs={{0,32},{32,0},{64,96},{96,64},{128,160},{160,128},{192,224},{224,1... | collective-permute-start | bytes 24584 | tf_op jit(solution)/shard_map/ppermute | solution.py:134
  (34 other events, 33.4 us)

commit v5 on v3

--- a/solution.py
+++ b/solution.py
@@ -1,3 +1,5 @@
+import functools
+
 import jax
 import jax.numpy as jnp
 from jax import lax
@@ -96,58 +98,124 @@
                 wide * a_tile, axis=0, keepdims=True
             )
         out[:, slot * qa : (slot + 1) * qa, :] = total.T.reshape(nc, qa, LANES)
-    at = slots * qa
     whole = b_all[...]
     gram_b = lax.dot_general(
         whole, whole, (((0,), (0,)), ((), ())), preferred_element_type=jnp.float32
     )
-    for h in range(half):
-        part = gram_b[:, h * LANES : (h + 1) * LANES]
-        out[:, at : at + qa, :] = part.reshape(nc, qa, LANES)
-        at += qa
+    row = meta[4, 0]
+    per = LANES // qb
+    strip = gram_b[:, :LANES]
+    for h in range(1, half):
+        strip = jnp.where(row // per == h, gram_b[:, h * LANES : (h + 1) * LANES], strip)
+    first = slots * depth
+    second = first + qb
+    third = second + qb
+    strip = pltpu.roll(strip, (second + LANES - qb * (row % per)) % LANES, 1)
     pieces = got[:, own * half : own * half + qa, :].astype(jnp.float32)
     piece = jnp.sum(pieces, axis=0)
-    first = slots * depth
     moved = pltpu.roll(piece, first, 1) + pltpu.roll(piece, first - qb, 1)
     lane = lax.broadcasted_iota(jnp.int32, piece.shape, 1)
-    moved = jnp.where((lane >= first) & (lane < first + qb), moved, 0.0)
-    out[:, at : at + qa, :] = deep_c[...].T.reshape(nc, qa, LANES) + moved[None]
-
-
-def call(kernel, shape, scratch, flops, moved, operands):
-    memory = [pltpu.SMEM] + [pltpu.VMEM] * (len(operands) - 1)
+    spots = jnp.zeros(piece.shape, jnp.int32)
+    for m in range(slots):
+        alive = meta[3, m] > 0
+        spots = jnp.where(lane == third + m, jnp.where(alive, meta[0, m], -1), spots)
+        spots = jnp.where(lane == third + slots + m, jnp.where(alive, meta[2, m], -1), spots)
+    moved = jnp.where((lane >= first) & (lane < second), moved, spots.astype(jnp.float32))
+    wide_lane = lax.broadcasted_iota(jnp.int32, strip.shape, 1)
+    mixed = deep_c[...].T
+    mixed = mixed + jnp.where((wide_lane >= second) & (wide_lane < third), strip, 0.0)
+    out[:, slots * qa :, :] = mixed.reshape(nc, qa, LANES) + moved[None]
+
+
+def bump(state, hess, full, drive, rate):
+    scale = jnp.sum(jnp.abs(hess), axis=1, keepdims=True) + 1e-06
+    push = jnp.dot(hess, full, precision=HIGH, preferred_element_type=jnp.float32)
+    return jnp.maximum(state - rate * (push - drive) / scale, 0.0)
+
+
+def project_kernel(sweep, last, meta, steps, got_c, got_r, at3, ct3, gram_c, b_ref, *refs):
+    if last:
+        new_a, new_c, new_b, sa = refs
+    else:
+        send, new_b, sa = refs
+    tiles_a, rank, tile = at3.shape
+    tiles_c = ct3.shape[0]
+    nc, nr = got_c.shape[0], got_r.shape[0]
+    slots = meta.shape[1]
+    half, qa, qb = rank // LANES, rank // nc, rank // nr
+    own = b_ref.shape[0]
+    third = LANES // 2
+    mine = pl.ds(pl.multiple_of(meta[4, 1] * qa, qa), qa)
+    at = own * half
+    for h in range(half):
+        part = got_r[:, at + h * qb : at + (h + 1) * qb, :]
+        sa[:, h * LANES : (h + 1) * LANES] = part.reshape(rank, LANES)
+    drive_b = jnp.concatenate(
+        [jnp.sum(got_r[:, own * h : own * (h + 1), :], axis=0) for h in range(half)], axis=1
+    )
+    at += qb * half
+    drive_c = [
+        jnp.sum(got_r[:, at + t * qa : at + (t + 1) * qa, :], axis=0) for t in range(tiles_c)
+    ]
+    at += tiles_c * qa
+    per = LANES // qb
+    sb_parts = []
+    for h in range(half):
+        part = got_r[h * per, at : at + qa, :]
+        for i in range(1, per):
+            part = part + pltpu.roll(got_r[h * per + i, at : at + qa, :], qb * i, 1)
+        sb_parts.append(part)
+    sb_c = jnp.concatenate(sb_parts, axis=1)
+    drive_a = [jnp.zeros((qa, tile), jnp.float32) for _ in range(tiles_a)]
+    for s in range(nc):
+        for m in range(slots):
+            value = got_c[s, m * qa : (m + 1) * qa, :]
+            spot = got_c[s, slots * qa : (slots + 1) * qa, third + m : third + m + 1]
+            spot = jnp.broadcast_to(spot, value.shape)
+            for t in range(tiles_a):
+                drive_a[t] = drive_a[t] + jnp.where(spot == float(t), value, 0.0)
+    hess = sb_c * gram_c[mine, :]
+    for t in range(tiles_a):
+        new = bump(at3[t, mine, :], hess, at3[t], drive_a[t], steps[sweep, 0])
+        if last:
+            new_a[t] = new
+        else:
+            send[:, t * qa : (t + 1) * qa, :] = jnp.broadcast_to(new[None], (nc,) + new.shape)
+    hess = sa[mine, :] * sb_c
+    for t in range(tiles_c):
+        new = bump(ct3[t, mine, :], hess, ct3[t], drive_c[t], steps[sweep, 2])
+        if last:
+            new_c[t] = new
+        else:
+            at = (tiles_a + t) * qa
+            send[:, at : at + qa, :] = jnp.broadcast_to(new[None], (nc,) + new.shape)
+    hess = sa[...] * gram_c[...]
+    scale = jnp.sum(jnp.abs(hess), axis=0, keepdims=True) + 1e-06
+    old = b_ref[...]
+    push = jnp.dot(old, hess, precision=HIGH, preferred_element_type=jnp.float32)
+    new_b[...] = jnp.maximum(old - steps[sweep, 1] * (push - drive_b) / scale, 0.0)
+
+
+def call(kernel, shapes, scratch, flops, moved, operands, scalars=1):
+    memory = [pltpu.SMEM] * scalars + [pltpu.VMEM] * (len(operands) - scalars)
     return pl.pallas_call(
         kernel,
-        out_shape=jax.ShapeDtypeStruct(shape, jnp.float32),
+        out_shape=[jax.ShapeDtypeStruct(shape, jnp.float32) for shape in shapes],
         in_specs=[pl.BlockSpec(memory_space=m) for m in memory],
-        out_specs=pl.BlockSpec(memory_space=pltpu.VMEM),
+        out_specs=[pl.BlockSpec(memory_space=pltpu.VMEM)] * len(shapes),
         scratch_shapes=scratch,
         cost_estimate=pl.CostEstimate(flops=flops, bytes_accessed=moved, transcendentals=0),
         compiler_params=pltpu.CompilerParams(vmem_limit_bytes=32 << 20),
     )(*operands)
 
 
-def bump(state, hess, full, drive, rate):
-    scale = jnp.sum(jnp.abs(hess), axis=1) + 1e-06
-    push = jnp.stack(
-        [jnp.dot(hess, f, precision=HIGH, preferred_element_type=jnp.float32) for f in full]
-    )
-    return jnp.maximum(state - rate * (push - drive) / scale[None, :, None], 0.0)
-
-
-def bump_rows(state, hess, drive, rate):
-    scale = jnp.sum(jnp.abs(hess), axis=1) + 1e-06
-    push = jnp.dot(state, hess, precision=HIGH, preferred_element_type=jnp.float32)
-    return jnp.maximum(state - rate * (push - drive) / scale[None, :], 0.0)
-
-
 def lanes(x):
     return jnp.stack([x[:, t * LANES : (t + 1) * LANES] for t in range(x.shape[1] // LANES)])
 
 
 def shards(bricks, brick_coords, brick_counts, step_sizes, init_a, init_b, init_c):
     nr, nc = lax.axis_size("row"), lax.axis_size("col")
-    col = lax.axis_index("col")
+    row, col = lax.axis_index("row"), lax.axis_index("col")
     slab, places, own = bricks[0, 0], brick_coords[0, 0], brick_counts[0, 0]
     slots, depth, tile, _ = slab.shape
     sweeps = step_sizes.shape[0]
@@ -162,27 +230,26 @@
 
     live = lax.iota(jnp.int32, slots) < own
     meta = jnp.concatenate(
-        [jnp.where(live[None, :], places, 0), live[None, :].astype(jnp.int32)], axis=0
-    )
-    mine = pad_lanes(jnp.where(live[None, :], places, -1).astype(f32).reshape(1, -1))
-    mine = jnp.broadcast_to(mine, (8, LANES))
-
+        [
+            jnp.where(live[None, :], places, 0),
+            live[None, :].astype(jnp.int32),
+            jnp.zeros((1, slots), jnp.int32).at[0, 0].set(row).at[0, 1].set(col),
+        ],
+        axis=0,
+    )
     state_b = init_b[0]
     c_bf = init_c.astype(bf16)
 
     for sweep in range(sweeps):
         b_bf = state_b.astype(bf16)
         if sweep == 0:
-            got = swap(spread(jnp.concatenate([fold(init_a[0]), mine], 0), nc), "col")
-            rows, spots_col = take(got, [own_a * half, 8])
+            rows = swap(spread(fold(init_a[0]), nc), "col")
             a_rows = unfold(rows, rank).reshape(tiles_a, tile, rank)
             at3 = jnp.swapaxes(a_rows, 1, 2)
             a_bf3 = a_rows.astype(bf16)
-            spots_col = spots_col[:, 0, : 3 * slots].reshape(nc, 3, slots).astype(jnp.int32)
             ct3 = lanes(init_c.T)
         else:
-            send = jnp.concatenate([new_a.reshape(-1, LANES), new_c.reshape(-1, LANES)], 0)
-            got = swap(spread(send, nc), "col")
+            got = swap(send, "col")
             chunk, c_got = take(got, [tiles_a * qa, tiles_c * qa])
             at3 = jnp.swapaxes(chunk.reshape(nc, tiles_a, qa, tile), 0, 1).reshape(tiles_a, rank, tile)
             a_bf3 = jnp.swapaxes(at3.astype(bf16), 1, 2)
@@ -200,49 +267,45 @@
         got = swap(send, "row")
         gram_c = gram(c_bf)
         work = 2 * slots * depth * tile * tile * rank
-        blocks = call(
+        (blocks,) = call(
             deep_kernel,
-            (nr, own_b * half, LANES),
+            [(nr, own_b * half, LANES)],
             [pltpu.VMEM((tiles_b * tile, rank), f32)],
             work, slab.size * 2, (meta, slab, a_bf3, c_bf),
         )
-        send = call(
+        (send,) = call(
             wide_kernel,
-            (nc, qa * (slots + half + 1), LANES),
+            [(nc, qa * (slots + 1), LANES)],
             [pltpu.VMEM((tiles_b * tile, rank), bf16), pltpu.VMEM((LANES, rank), f32)],
             work, slab.size * 2, (meta, got, slab, a_bf3, c_bf),
         )
-        got = swap(send, "col")
-        *a_got, s_got, m_got = take(got, [qa] * slots + [qa * half, qa])
-        sb_c = unfold(jnp.sum(s_got, axis=0), rank)
-        drive_a = jnp.stack(
-            [
-                sum(
-                    jnp.sum(jnp.where((spots_col[:, 0, m] == t)[:, None, None], a_got[m], 0.0), axis=0)
-                    for m in range(slots)
-                )
-                for t in range(tiles_a)
-            ]
+        got_c = swap(send, "col")
+        mixed = got_c[:, slots * qa :]
+        second = slots * depth + qb
+        third = second + qb
+        spots_k = mixed[:, 0, third + slots : third + 2 * slots]
+        onehot = (spots_k[:, :, None] == lax.iota(jnp.int32, layers).astype(f32)).astype(f32)
+        c_got = mixed[:, :, : slots * depth].reshape(nc, qa, slots, depth)
+        drive_c = jnp.einsum("sqmk,smb->qbk", c_got, onehot, precision=HIGH).reshape(qa, length)
+        strip = mixed[:, :, slots * depth : second].reshape(rank, qb).T
+        piece_b = pad_lanes(jnp.sum(mixed[:, :, second:third], axis=0))
+        everyone = jnp.concatenate([fold(strip), fold(drive_c), piece_b], axis=0)
+        everyone = jnp.broadcast_to(everyone[None], (nr,) + everyone.shape)
+        got_r = swap(jnp.concatenate([blocks, everyone], axis=1), "row")
+        last = sweep == sweeps - 1
+        part_a, part_c = (tiles_a, qa, tile), (tiles_c, qa, LANES)
+        shapes = [part_a, part_c] if last else [(nc, (tiles_a + tiles_c) * qa, LANES)]
+        results = call(
+            functools.partial(project_kernel, sweep, last),
+            shapes + [state_b.shape],
+            [pltpu.VMEM((rank, rank), f32)],
+            12 * rank * rank * tile, 8 * rank * rank * 4,
+            (meta, step_sizes, got_c, got_r, at3, ct3, gram_c, state_b), scalars=2,
         )
-        onehot = (spots_col[:, 2, :, None] == lax.iota(jnp.int32, layers)).astype(f32)
-        c_got = m_got[:, :, : slots * depth].reshape(nc, qa, slots, depth)
-        drive_c = jnp.einsum("sqmk,smb->qbk", c_got, onehot, precision=HIGH).reshape(qa, length)
-        strip = m_got[:, :, slots * depth : slots * depth + qb].reshape(rank, qb).T
-        pieces = [
-            blocks,
-            jnp.broadcast_to(fold(strip)[None], (nr, qb * half, LANES)),
-            jnp.broadcast_to(fold(drive_c)[None], (nr, qa * tiles_c, LANES)),
-        ]
-        got = swap(jnp.concatenate(pieces, axis=1), "row")
-        b_got, s_got, c_got = take(got, [p.shape[1] for p in pieces])
-        mine_b = unfold(jnp.sum(b_got, axis=0), rank)
-        sa = unfold(s_got, rank).reshape(rank, rank)
-        mine_c = jnp.sum(c_got, axis=0).reshape(tiles_c, qa, LANES)
-        cut = lambda x, axis=0: lax.dynamic_slice_in_dim(x, col * qa, qa, axis)
-        rate = step_sizes[sweep]
-        new_a = bump(cut(at3, 1), sb_c * cut(gram_c), at3, drive_a, rate[0])
-        state_b = bump_rows(state_b, sa * gram_c, mine_b, rate[1])
-        new_c = bump(cut(ct3, 1), cut(sa) * sb_c, ct3, mine_c, rate[2])
+        if last:
+            new_a, new_c, state_b = results
+        else:
+            send, state_b = results
     per_a = tile // own_a
     own = new_a.reshape(tiles_a, qa, per_a, own_a).transpose(0, 2, 1, 3).reshape(nc, qa, own_a)
     own = fold(pad_lanes(own))

time: 283 us -> 251 us (0.89)
  blocking collectives: 0 us -> 26.5 us
  waiting for transfers between devices: 146 us -> 124 us
  other arithmetic: 16.8 us -> 4.08 us
  starting transfers between devices: 74.9 us -> 62.8 us
  local copies, waits for them, and re-layouts: 26 us -> 16.9 us
  matrix products: 7.82 us -> 1.55 us
  Pallas kernels: 7.42 us -> 11.2 us
    all_to_all x0 -> x1, blocking collectives: none -> 26.5 us  [swap(): return lax.all_to_all(x, axis, 0, 0, tiled=True)]
    all_to_all x9 -> x8, waiting for transfers between devices: 146 us -> 124 us  [swap(): return lax.all_to_all(x, axis, 0, 0, tiled=True)]
    all_to_all x9 -> x8, starting transfers between devices: 74.9 us -> 62.8 us  [swap(): return lax.all_to_all(x, axis, 0, 0, tiled=True)]
    dot_general x18 -> x0, matrix products: 5.54 us -> none  [the longest x16 3.17 us: bump(): jnp.dot(hess, f, precision=HIGH, preferred_element_type=jnp.float32)]
    max x3 -> x0, other arithmetic: 4.58 us -> none  [bump(): jnp.maximum(state - rate * (push - drive) / scale[None, :, None], 0.0)]
    reduce_sum x8 -> x2, other arithmetic: 4.69 us -> 0.26 us  [shards(): piece_b = pad_lanes(jnp.sum(mixed[:, :, second:third], axis=0))]
    pallas_call x4 -> x6, Pallas kernels: 7.42 us -> 11.2 us  [call(): pl.pallas_call(kernel, out_shape=[jax.ShapeDtypeStruct(shape, jnp.float32...]
    unnamed x60 -> x35, local copies, waits for them, and re-layouts: 7.71 us -> 7.2 us
  transfers between devices with their start and end apart: 9 -> 8, of which waited for: 9 -> 8; matrix products, arithmetic and copies ran while one was open for 5% -> 3% of each run, Pallas kernels for 1% -> 1%
where the time goes in v5:
time: 251 us; the launch traced here: 249 us
  waiting for transfers between devices  124 us (49%)
  starting transfers between devices  62.8 us (25%)
  blocking collectives  26.5 us (11%)
  local copies, waits for them, and re-layouts  16.9 us (7%)
  Pallas kernels  11.2 us (4%)
  other arithmetic  4.08 us (2%)
    all_to_all x8, waiting for transfers between devices, swap(): return lax.all_to_all(x, axis, 0, 0, tiled=True)  124 us
    all_to_all x8, starting transfers between devices, swap(): return lax.all_to_all(x, axis, 0, 0, tiled=True)  62.8 us
    all_to_all x1, blocking collectives, swap(): return lax.all_to_all(x, axis, 0, 0, tiled=True)  26.5 us
    pallas_call x6, Pallas kernels, call(): pl.pallas_call(kernel, out_shape=[jax.ShapeDtypeStruct(shape, jnp.float32...  11.2 us
    unnamed x35, local copies, waits for them, and re-layouts  7.2 us
  transfers between devices with their start and end apart: 8, of which 8 were waited for; matrix products, arithmetic and copies ran while one was open for 3% of the time, Pallas kernels for 1%

profile of v5, /device:TPU:1, one launch (start us, length us, event | category | flops | bytes accessed | tf_op | source)
XLA Modules:
  0.0 249.3 jit_solution(13575528048458182846)
XLA Ops:
  2.2 17.2 %all-to-all-start = ((f32[32,32,128]{2,1,0:T(8,128)}), f32[32,32,128]{2,1,0:T(8,128)S(1)}, u32[]{:S(2)}, u32[]{:S(2)}) async-start(f32[32,32,128]{2,1,0:T(8,128)} %broadcast_in_dim.33), calls=%async_computation | async-start | bytes 1048576 | tf_op jit(solution)/shard_map/all_to_all | solution.py:15
  22.2 15.0 %all-to-all-done = f32[32,32,128]{2,1,0:T(8,128)S(1)} async-done(((f32[32,32,128]{2,1,0:T(8,128)}), f32[32,32,128]{2,1,0:T(8,128)S(1)}, u32[]{:S(2)}, u32[]{:S(2)}) %all-to-all-start) | async-done | bytes 524320 | tf_op jit(solution)/shard_map/all_to_all | solution.py:15
  38.7 8.0 %all-to-all-start.1 = ((bf16[16,40,128]{2,1,0:T(8,128)(2,1)}), bf16[16,40,128]{2,1,0:T(8,128)(2,1)S(1)}, u32[]{:S(2)}, u32[]{:S(2)}) async-start(bf16[16,40,128]{2,1,0:T(8,128)(2,1)} %pad_maximum_fusion.3), calls=%async_computation.1 | async-start | bytes 327680 | tf_op jit(solution)/shard_map/all_to_all | solution.py:15
  48.1 6.1 %all-to-all-done.1.got = bf16[16,40,128]{2,1,0:T(8,128)(2,1)S(1)} async-done(((bf16[16,40,128]{2,1,0:T(8,128)(2,1)}), bf16[16,40,128]{2,1,0:T(8,128)(2,1)S(1)}, u32[]{:S(2)}, u32[]{:S(2)}) %all-to-all-start.1) | async-done | bytes 163872 | tf_op jit(solution)/shard_map/all_to_all | solution.py:15
  54.2 2.5 shard_map.94
  56.7 6.5 %all-to-all-start.2 = ((f32[32,24,128]{2,1,0:T(8,128)}), f32[32,24,128]{2,1,0:T(8,128)S(1)}, u32[]{:S(2)}, u32[]{:S(2)}) async-start(f32[32,24,128]{2,1,0:T(8,128)} %shard_map.94), calls=%async_computation.2 | async-start | bytes 786432 | tf_op jit(solution)/shard_map/all_to_all | solution.py:15
  63.2 1.4 shard_map.95
  64.5 13.7 %all-to-all-done.2.got_c = f32[32,24,128]{2,1,0:T(8,128)S(1)} async-done(((f32[32,24,128]{2,1,0:T(8,128)}), f32[32,24,128]{2,1,0:T(8,128)S(1)}, u32[]{:S(2)}, u32[]{:S(2)}) %all-to-all-start.2) | async-done | bytes 393248 | tf_op jit(solution)/shard_map/all_to_all | solution.py:15
  80.3 6.1 %all-to-all-start.3 = ((f32[16,104,128]{2,1,0:T(8,128)}), f32[16,104,128]{2,1,0:T(8,128)S(1)}, u32[]{:S(2)}, u32[]{:S(2)}) async-start(f32[16,104,128]{2,1,0:T(8,128)} %pad_maximum_fusion), calls=%async_computation.3 | async-start | bytes 1703936 | tf_op jit(solution)/shard_map/all_to_all | solution.py:15
  88.9 2.0 copy.87
  90.9 18.3 %all-to-all-done.3.got_r = f32[16,104,128]{2,1,0:T(8,128)S(1)} async-done(((f32[16,104,128]{2,1,0:T(8,128)}), f32[16,104,128]{2,1,0:T(8,128)S(1)}, u32[]{:S(2)}, u32[]{:S(2)}) %all-to-all-start.3) | async-done | bytes 852000 | tf_op jit(solution)/shard_map/all_to_all | solution.py:15
  110.9 1.5 shard_map.96
  113.4 6.0 %all-to-all-start.4 = ((f32[32,64,128]{2,1,0:T(8,128)}), f32[32,64,128]{2,1,0:T(8,128)S(1)}, u32[]{:S(2)}, u32[]{:S(2)}) async-start(f32[32,64,128]{2,1,0:T(8,128)} %copy-done.2), calls=%async_computation.4 | async-start | bytes 2097152 | tf_op jit(solution)/shard_map/all_to_all | solution.py:15
  119.5 28.7 %all-to-all-done.4 = f32[32,64,128]{2,1,0:T(8,128)S(1)} async-done(((f32[32,64,128]{2,1,0:T(8,128)}), f32[32,64,128]{2,1,0:T(8,128)S(1)}, u32[]{:S(2)}, u32[]{:S(2)}) %all-to-all-start.4) | async-done | bytes 1048608 | tf_op jit(solution)/shard_map/all_to_all | solution.py:15
  150.0 4.4 %all-to-all-start.5 = ((bf16[16,40,128]{2,1,0:T(8,128)(2,1)}), bf16[16,40,128]{2,1,0:T(8,128)(2,1)S(1)}, u32[]{:S(2)}, u32[]{:S(2)}) async-start(bf16[16,40,128]{2,1,0:T(8,128)(2,1)} %pad_maximum_fusion.4), calls=%async_computation.5 | async-start | bytes 327680 | tf_op jit(solution)/shard_map/all_to_all | solution.py:15
  154.8 7.0 %all-to-all-done.5.got = bf16[16,40,128]{2,1,0:T(8,128)(2,1)S(1)} async-done(((bf16[16,40,128]{2,1,0:T(8,128)(2,1)}), bf16[16,40,128]{2,1,0:T(8,128)(2,1)S(1)}, u32[]{:S(2)}, u32[]{:S(2)}) %all-to-all-start.5) | async-done | bytes 163872 | tf_op jit(solution)/shard_map/all_to_all | solution.py:15
  161.8 2.5 shard_map.97
  164.3 8.7 %all-to-all-start.6 = ((f32[32,24,128]{2,1,0:T(8,128)}), f32[32,24,128]{2,1,0:T(8,128)S(1)}, u32[]{:S(2)}, u32[]{:S(2)}) async-start(f32[32,24,128]{2,1,0:T(8,128)} %shard_map.97), calls=%async_computation.6 | async-start | bytes 786432 | tf_op jit(solution)/shard_map/all_to_all | solution.py:15
  173.0 1.4 shard_map.98
  174.4 13.8 %all-to-all-done.6.got_c = f32[32,24,128]{2,1,0:T(8,128)S(1)} async-done(((f32[32,24,128]{2,1,0:T(8,128)}), f32[32,24,128]{2,1,0:T(8,128)S(1)}, u32[]{:S(2)}, u32[]{:S(2)}) %all-to-all-start.6) | async-done | bytes 393248 | tf_op jit(solution)/shard_map/all_to_all | solution.py:15
  190.2 5.8 %all-to-all-start.7 = ((f32[16,104,128]{2,1,0:T(8,128)}), f32[16,104,128]{2,1,0:T(8,128)S(1)}, u32[]{:S(2)}, u32[]{:S(2)}) async-start(f32[16,104,128]{2,1,0:T(8,128)} %pad_maximum_fusion.1), calls=%async_computation.7 | async-start | bytes 1703936 | tf_op jit(solution)/shard_map/all_to_all | solution.py:15
  197.2 21.7 %all-to-all-done.7.got_r = f32[16,104,128]{2,1,0:T(8,128)S(1)} async-done(((f32[16,104,128]{2,1,0:T(8,128)}), f32[16,104,128]{2,1,0:T(8,128)S(1)}, u32[]{:S(2)}, u32[]{:S(2)}) %all-to-all-start.7) | async-done | bytes 852000 | tf_op jit(solution)/shard_map/all_to_all | solution.py:15
  218.9 2.0 shard_map.99
  221.1 26.5 %all_to_all.45 = f32[32,40,128]{2,1,0:T(8,128)S(1)} all-to-all(f32[32,40,128]{2,1,0:T(8,128)S(1)} %select_maximum_fusion), channel_id=1, replica_groups=mesh['row'=16,'col'=32] {'col'}, dimensions={0} | all-to-all | bytes 1310720 | tf_op jit(solution)/shard_map/all_to_all | solution.py:15
  (114 shorter events, 20.5 us)
Async XLA Ops:
  2.2 35.0 %all-to-all-start = ((f32[32,32,128]{2,1,0:T(8,128)}), f32[32,32,128]{2,1,0:T(8,128)S(1)}, u32[]{:S(2)}, u32[]{:S(2)}) async-start(f32[32,32,128]{2,1,0:T(8,128)} %broadcast_in_dim.33), calls=%async_computation | async-start | bytes 1048576 | tf_op jit(solution)/shard_map/all_to_all | solution.py:15
  19.4 2.0 copy-start.3
  21.4 0.7 copy-start.9
  37.8 9.0 %copy-start.8 = (f32[512,256]{1,0:T(8,128)S(1)}, f32[512,256]{1,0:T(8,128)}, u32[]{:S(2)}) copy-start(f32[512,256]{1,0:T(8,128)} %param.17) | copy-start | bytes 1572868
  38.7 15.5 %all-to-all-start.1 = ((bf16[16,40,128]{2,1,0:T(8,128)(2,1)}), bf16[16,40,128]{2,1,0:T(8,128)(2,1)S(1)}, u32[]{:S(2)}, u32[]{:S(2)}) async-start(bf16[16,40,128]{2,1,0:T(8,128)(2,1)} %pad_maximum_fusion.3), calls=%async_computation.1 | async-start | bytes 327680 | tf_op jit(solution)/shard_map/all_to_all | solution.py:15
  46.9 7.3 %copy-start = (bf16[1,1,2,16,128,128]{5,4,3,2,1,0:T(8,128)(2,1)S(1)}, bf16[1,1,2,16,128,128]{5,4,3,2,1,0:T(8,128)(2,1)}, u32[]{:S(2)}) copy-start(bf16[1,1,2,16,128,128]{5,4,3,2,1,0:T(8,128)(2,1)} %param.11) | copy-start | bytes 3145732
  47.2 0.8 copy-start.5
  56.7 21.6 %all-to-all-start.2 = ((f32[32,24,128]{2,1,0:T(8,128)}), f32[32,24,128]{2,1,0:T(8,128)S(1)}, u32[]{:S(2)}, u32[]{:S(2)}) async-start(f32[32,24,128]{2,1,0:T(8,128)} %shard_map.94), calls=%async_computation.2 | async-start | bytes 786432 | tf_op jit(solution)/shard_map/all_to_all | solution.py:15
  80.3 28.9 %all-to-all-start.3 = ((f32[16,104,128]{2,1,0:T(8,128)}), f32[16,104,128]{2,1,0:T(8,128)S(1)}, u32[]{:S(2)}, u32[]{:S(2)}) async-start(f32[16,104,128]{2,1,0:T(8,128)} %pad_maximum_fusion), calls=%async_computation.3 | async-start | bytes 1703936 | tf_op jit(solution)/shard_map/all_to_all | solution.py:15
  109.2 0.7 copy-start.4
  109.9 1.0 copy-start.1
  112.4 1.0 copy-start.2
  113.4 34.8 %all-to-all-start.4 = ((f32[32,64,128]{2,1,0:T(8,128)}), f32[32,64,128]{2,1,0:T(8,128)S(1)}, u32[]{:S(2)}, u32[]{:S(2)}) async-start(f32[32,64,128]{2,1,0:T(8,128)} %copy-done.2), calls=%async_computation.4 | async-start | bytes 2097152 | tf_op jit(solution)/shard_map/all_to_all | solution.py:15
  148.3 0.8 copy-start.6
  150.0 11.8 %all-to-all-start.5 = ((bf16[16,40,128]{2,1,0:T(8,128)(2,1)}), bf16[16,40,128]{2,1,0:T(8,128)(2,1)S(1)}, u32[]{:S(2)}, u32[]{:S(2)}) async-start(bf16[16,40,128]{2,1,0:T(8,128)(2,1)} %pad_maximum_fusion.4), calls=%async_computation.5 | async-start | bytes 327680 | tf_op jit(solution)/shard_map/all_to_all | solution.py:15
  164.3 23.9 %all-to-all-start.6 = ((f32[32,24,128]{2,1,0:T(8,128)}), f32[32,24,128]{2,1,0:T(8,128)S(1)}, u32[]{:S(2)}, u32[]{:S(2)}) async-start(f32[32,24,128]{2,1,0:T(8,128)} %shard_map.97), calls=%async_computation.6 | async-start | bytes 786432 | tf_op jit(solution)/shard_map/all_to_all | solution.py:15
  190.2 28.6 %all-to-all-start.7 = ((f32[16,104,128]{2,1,0:T(8,128)}), f32[16,104,128]{2,1,0:T(8,128)S(1)}, u32[]{:S(2)}, u32[]{:S(2)}) async-start(f32[16,104,128]{2,1,0:T(8,128)} %pad_maximum_fusion.1), calls=%async_computation.7 | async-start | bytes 1703936 | tf_op jit(solution)/shard_map/all_to_all | solution.py:15
  196.1 1.0 copy-start.7

commit v6 on v5

--- a/solution.py
+++ b/solution.py
@@ -13,6 +13,16 @@
 
 def swap(x, axis):
     return lax.all_to_all(x, axis, 0, 0, tiled=True)
+
+
+def chip_gather(x):
+    nc = lax.axis_size("col")
+    groups = [[chip * 2 + core for chip in range(nc // 2)] for core in range(2)]
+    near = lax.all_to_all(x, "col", 0, 0, axis_index_groups=groups, tiled=True)
+    far = lax.ppermute(near, "col", [(i, i ^ 1) for i in range(nc)])
+    even = lax.axis_index("col") % 2 == 0
+    pair = jnp.stack([jnp.where(even, near, far), jnp.where(even, far, near)], axis=1)
+    return pair.reshape((nc,) + x.shape[1:])
 
 
 def spread(x, peers):
@@ -180,7 +190,7 @@
         if last:
             new_a[t] = new
         else:
-            send[:, t * qa : (t + 1) * qa, :] = jnp.broadcast_to(new[None], (nc,) + new.shape)
+            send[:, t * qa : (t + 1) * qa, :] = jnp.broadcast_to(new[None], (nc // 2,) + new.shape)
     hess = sa[mine, :] * sb_c
     for t in range(tiles_c):
         new = bump(ct3[t, mine, :], hess, ct3[t], drive_c[t], steps[sweep, 2])
@@ -188,7 +198,7 @@
             new_c[t] = new
         else:
             at = (tiles_a + t) * qa
-            send[:, at : at + qa, :] = jnp.broadcast_to(new[None], (nc,) + new.shape)
+            send[:, at : at + qa, :] = jnp.broadcast_to(new[None], (nc // 2,) + new.shape)
     hess = sa[...] * gram_c[...]
     scale = jnp.sum(jnp.abs(hess), axis=0, keepdims=True) + 1e-06
     old = b_ref[...]
@@ -249,7 +259,7 @@
             a_bf3 = a_rows.astype(bf16)
             ct3 = lanes(init_c.T)
         else:
-            got = swap(send, "col")
+            got = chip_gather(send)
             chunk, c_got = take(got, [tiles_a * qa, tiles_c * qa])
             at3 = jnp.swapaxes(chunk.reshape(nc, tiles_a, qa, tile), 0, 1).reshape(tiles_a, rank, tile)
             a_bf3 = jnp.swapaxes(at3.astype(bf16), 1, 2)
@@ -294,7 +304,7 @@
         got_r = swap(jnp.concatenate([blocks, everyone], axis=1), "row")
         last = sweep == sweeps - 1
         part_a, part_c = (tiles_a, qa, tile), (tiles_c, qa, LANES)
-        shapes = [part_a, part_c] if last else [(nc, (tiles_a + tiles_c) * qa, LANES)]
+        shapes = [part_a, part_c] if last else [(nc // 2, (tiles_a + tiles_c) * qa, LANES)]
         results = call(
             functools.partial(project_kernel, sweep, last),
             shapes + [state_b.shape],

time: 251 us -> 242 us (0.964)
  waiting for transfers between devices: 124 us -> 97 us
  blocking collectives: 26.5 us -> 46.7 us
    all_to_all x8 -> x7, waiting for transfers between devices: 124 us -> 95.5 us  [swap(): return lax.all_to_all(x, axis, 0, 0, tiled=True)]
    all_to_all x0 -> x1, blocking collectives: none -> 20 us  [chip_gather(): near = lax.all_to_all(x, 'col', 0, 0, axis_index_groups=groups, tiled=True)]
    all_to_all x8 -> x7, starting transfers between devices: 62.8 us -> 56 us  [swap(): return lax.all_to_all(x, axis, 0, 0, tiled=True)]
    ppermute x0 -> x1, starting transfers between devices: none -> 5.47 us  [chip_gather(): far = lax.ppermute(near, 'col', [(i, i ^ 1) for i in range(nc)])]
    unnamed x35 -> x33, local copies, waits for them, and re-layouts: 7.2 us -> 6.25 us
where the time goes in v6:
time: 242 us; the launch traced here: 240 us
  waiting for transfers between devices  97 us (40%)
  starting transfers between devices  61.5 us (25%)
  blocking collectives  46.7 us (19%)
  local copies, waits for them, and re-layouts  16 us (7%)
  Pallas kernels  11.1 us (5%)
  other arithmetic  4.3 us (2%)
    all_to_all x7, waiting for transfers between devices, swap(): return lax.all_to_all(x, axis, 0, 0, tiled=True)  95.5 us
    all_to_all x7, starting transfers between devices, swap(): return lax.all_to_all(x, axis, 0, 0, tiled=True)  56 us
    all_to_all x1, blocking collectives, swap(): return lax.all_to_all(x, axis, 0, 0, tiled=True)  26.7 us
    all_to_all x1, blocking collectives, chip_gather(): near = lax.all_to_all(x, 'col', 0, 0, axis_index_groups=groups, tiled=True)  20 us
    pallas_call x6, Pallas kernels, call(): pl.pallas_call(kernel, out_shape=[jax.ShapeDtypeStruct(shape, jnp.float32...  11.1 us
    unnamed x33, local copies, waits for them, and re-layouts  6.25 us
    ppermute x1, starting transfers between devices, chip_gather(): far = lax.ppermute(near, 'col', [(i, i ^ 1) for i in range(nc)])  5.47 us
  transfers between devices with their start and end apart: 8, of which 8 were waited for; matrix products, arithmetic and copies ran while one was open for 3% of the time, Pallas kernels for 1%

profile of v6, /device:TPU:1, one launch (start us, length us, event | category | flops | bytes accessed | tf_op | source)
XLA Modules:
  0.0 240.2 jit_solution(9200712667466639888)
XLA Ops:
  2.2 17.2 %all-to-all-start = ((f32[32,32,128]{2,1,0:T(8,128)}), f32[32,32,128]{2,1,0:T(8,128)S(1)}, u32[]{:S(2)}, u32[]{:S(2)}) async-start(f32[32,32,128]{2,1,0:T(8,128)} %broadcast_in_dim.33), calls=%async_computation | async-start | bytes 1048576 | tf_op jit(solution)/shard_map/all_to_all | solution.py:15
  22.2 15.0 %all-to-all-done = f32[32,32,128]{2,1,0:T(8,128)S(1)} async-done(((f32[32,32,128]{2,1,0:T(8,128)}), f32[32,32,128]{2,1,0:T(8,128)S(1)}, u32[]{:S(2)}, u32[]{:S(2)}) %all-to-all-start) | async-done | bytes 524320 | tf_op jit(solution)/shard_map/all_to_all | solution.py:15
  38.7 8.0 %all-to-all-start.1 = ((bf16[16,40,128]{2,1,0:T(8,128)(2,1)}), bf16[16,40,128]{2,1,0:T(8,128)(2,1)S(1)}, u32[]{:S(2)}, u32[]{:S(2)}) async-start(bf16[16,40,128]{2,1,0:T(8,128)(2,1)} %pad_maximum_fusion.4), calls=%async_computation.1 | async-start | bytes 327680 | tf_op jit(solution)/shard_map/all_to_all | solution.py:15
  48.1 6.1 %all-to-all-done.1.got = bf16[16,40,128]{2,1,0:T(8,128)(2,1)S(1)} async-done(((bf16[16,40,128]{2,1,0:T(8,128)(2,1)}), bf16[16,40,128]{2,1,0:T(8,128)(2,1)S(1)}, u32[]{:S(2)}, u32[]{:S(2)}) %all-to-all-start.1) | async-done | bytes 163872 | tf_op jit(solution)/shard_map/all_to_all | solution.py:15
  54.2 2.5 %shard_map.94 = f32[32,24,128]{2,1,0:T(8,128)} custom-call(s32[5,2]{1,0:T(8,128)S(1)} %copy.105.meta, bf16[16,40,128]{2,1,0:T(8,128)(2,1)S(1)} %all-to-all-done.1.got, bf16[2,16,128,128]{3,2,1,0:T(8,128)(2,1)S(1)} %bitcast.122, bf16[4,128,256]{2,1,0:T(8,128)(2,1)S(1)} %bitcast_convert_fusion.a_ref, bf16[512,256]{1,0:T(8,128)(2,1)S(1)} %convert_element_type.57.c_ref), custom_call_target="tpu_custom_call" | custom-call | flops 268435456 | bytes 1048576 | tf_op jit(solution)/shard_map/pallas_call | solution.py:211
  56.7 6.5 %all-to-all-start.2 = ((f32[32,24,128]{2,1,0:T(8,128)}), f32[32,24,128]{2,1,0:T(8,128)S(1)}, u32[]{:S(2)}, u32[]{:S(2)}) async-start(f32[32,24,128]{2,1,0:T(8,128)} %shard_map.94), calls=%async_computation.2 | async-start | bytes 786432 | tf_op jit(solution)/shard_map/all_to_all | solution.py:15
  64.5 13.7 %all-to-all-done.2.got_c = f32[32,24,128]{2,1,0:T(8,128)S(1)} async-done(((f32[32,24,128]{2,1,0:T(8,128)}), f32[32,24,128]{2,1,0:T(8,128)S(1)}, u32[]{:S(2)}, u32[]{:S(2)}) %all-to-all-start.2) | async-done | bytes 393248 | tf_op jit(solution)/shard_map/all_to_all | solution.py:15
  80.3 6.1 %all-to-all-start.3 = ((f32[16,104,128]{2,1,0:T(8,128)}), f32[16,104,128]{2,1,0:T(8,128)S(1)}, u32[]{:S(2)}, u32[]{:S(2)}) async-start(f32[16,104,128]{2,1,0:T(8,128)} %pad_maximum_fusion.1), calls=%async_computation.3 | async-start | bytes 1703936 | tf_op jit(solution)/shard_map/all_to_all | solution.py:15
  88.9 2.1 copy.87
  90.9 18.3 %all-to-all-done.3.got_r = f32[16,104,128]{2,1,0:T(8,128)S(1)} async-done(((f32[16,104,128]{2,1,0:T(8,128)}), f32[16,104,128]{2,1,0:T(8,128)S(1)}, u32[]{:S(2)}, u32[]{:S(2)}) %all-to-all-start.3) | async-done | bytes 852000 | tf_op jit(solution)/shard_map/all_to_all | solution.py:15
  110.9 1.4 shard_map.96
  112.4 20.0 %all_to_all.45 = f32[16,64,128]{2,1,0:T(8,128)S(1)} all-to-all(f32[16,64,128]{2,1,0:T(8,128)S(1)} %get-tuple-element.33), channel_id=1, replica_groups={{0,2,4,6,8,10,12,14,16,18,20,22,24,26,28,30},{1,3,5,7,9,11,13,15,17,19,..., dimensions={0} | all-to-all | bytes 1048576 | tf_op jit(solution)/shard_map/all_to_all | solution.py:21
  132.4 5.5 %collective-permute-start = (f32[16,64,128]{2,1,0:T(8,128)S(1)}, f32[16,64,128]{2,1,0:T(8,128)S(1)}, u32[]{:S(2)}, u32[]{:S(2)}) collective-permute-start(f32[16,64,128]{2,1,0:T(8,128)S(1)} %all_to_all.45), channel_id=1, source_target_pairs={{0,1},{1,0},{2,3},{3,2},{4,5},{5,4},{6,7},{7,6},{8,9},{9,8},{10,11... | collective-permute-start | bytes 1572872 | tf_op jit(solution)/shard_map/ppermute | solution.py:22
  137.9 1.5 collective-permute-done
  141.4 4.7 %all-to-all-start.5 = ((bf16[16,40,128]{2,1,0:T(8,128)(2,1)}), bf16[16,40,128]{2,1,0:T(8,128)(2,1)S(1)}, u32[]{:S(2)}, u32[]{:S(2)}) async-start(bf16[16,40,128]{2,1,0:T(8,128)(2,1)} %pad_maximum_fusion.5), calls=%async_computation.5 | async-start | bytes 327680 | tf_op jit(solution)/shard_map/all_to_all | solution.py:15
  146.5 7.0 %all-to-all-done.5.got = bf16[16,40,128]{2,1,0:T(8,128)(2,1)S(1)} async-done(((bf16[16,40,128]{2,1,0:T(8,128)(2,1)}), bf16[16,40,128]{2,1,0:T(8,128)(2,1)S(1)}, u32[]{:S(2)}, u32[]{:S(2)}) %all-to-all-start.5) | async-done | bytes 163872 | tf_op jit(solution)/shard_map/all_to_all | solution.py:15
  153.5 2.5 %shard_map.97 = f32[32,24,128]{2,1,0:T(8,128)} custom-call(s32[5,2]{1,0:T(8,128)S(1)} %copy.105.meta, bf16[16,40,128]{2,1,0:T(8,128)(2,1)S(1)} %all-to-all-done.5.got, bf16[2,16,128,128]{3,2,1,0:T(8,128)(2,1)S(1)} %bitcast.124, bf16[4,128,256]{2,1,0:T(8,128)(2,1)S(1)} %copy.97.a_ref, bf16[512,256]{1,0:T(8,128)(2,1)S(1)} %bitcast.126), custom_call_target="tpu_custom_call" | custom-call | flops 268435456 | bytes 1048576 | tf_op jit(solution)/shard_map/pallas_call | solution.py:211
  156.0 7.9 %all-to-all-start.6 = ((f32[32,24,128]{2,1,0:T(8,128)}), f32[32,24,128]{2,1,0:T(8,128)S(1)}, u32[]{:S(2)}, u32[]{:S(2)}) async-start(f32[32,24,128]{2,1,0:T(8,128)} %shard_map.97), calls=%async_computation.6 | async-start | bytes 786432 | tf_op jit(solution)/shard_map/all_to_all | solution.py:15
  163.8 1.4 shard_map.98
  165.2 13.7 %all-to-all-done.6.got_c = f32[32,24,128]{2,1,0:T(8,128)S(1)} async-done(((f32[32,24,128]{2,1,0:T(8,128)}), f32[32,24,128]{2,1,0:T(8,128)S(1)}, u32[]{:S(2)}, u32[]{:S(2)}) %all-to-all-start.6) | async-done | bytes 393248 | tf_op jit(solution)/shard_map/all_to_all | solution.py:15
  181.0 5.7 %all-to-all-start.7 = ((f32[16,104,128]{2,1,0:T(8,128)}), f32[16,104,128]{2,1,0:T(8,128)S(1)}, u32[]{:S(2)}, u32[]{:S(2)}) async-start(f32[16,104,128]{2,1,0:T(8,128)} %pad_maximum_fusion.2), calls=%async_computation.7 | async-start | bytes 1703936 | tf_op jit(solution)/shard_map/all_to_all | solution.py:15
  187.8 21.7 %all-to-all-done.7.got_r = f32[16,104,128]{2,1,0:T(8,128)S(1)} async-done(((f32[16,104,128]{2,1,0:T(8,128)}), f32[16,104,128]{2,1,0:T(8,128)S(1)}, u32[]{:S(2)}, u32[]{:S(2)}) %all-to-all-start.7) | async-done | bytes 852000 | tf_op jit(solution)/shard_map/all_to_all | solution.py:15
  209.5 2.0 shard_map.99
  211.7 26.7 %all_to_all.46 = f32[32,40,128]{2,1,0:T(8,128)S(1)} all-to-all(f32[32,40,128]{2,1,0:T(8,128)S(1)} %select_maximum_fusion), channel_id=1, replica_groups=mesh['row'=16,'col'=32] {'col'}, dimensions={0} | all-to-all | bytes 1310720 | tf_op jit(solution)/shard_map/all_to_all | solution.py:15
  (116 shorter events, 21.2 us)
Async XLA Ops:
  2.2 35.0 %all-to-all-start = ((f32[32,32,128]{2,1,0:T(8,128)}), f32[32,32,128]{2,1,0:T(8,128)S(1)}, u32[]{:S(2)}, u32[]{:S(2)}) async-start(f32[32,32,128]{2,1,0:T(8,128)} %broadcast_in_dim.33), calls=%async_computation | async-start | bytes 1048576 | tf_op jit(solution)/shard_map/all_to_all | solution.py:15
  19.4 2.0 copy-start.2
  21.4 0.7 copy-start.8
  37.8 9.1 %copy-start.7 = (f32[512,256]{1,0:T(8,128)S(1)}, f32[512,256]{1,0:T(8,128)}, u32[]{:S(2)}) copy-start(f32[512,256]{1,0:T(8,128)} %param.17) | copy-start | bytes 1572868
  38.7 15.5 %all-to-all-start.1 = ((bf16[16,40,128]{2,1,0:T(8,128)(2,1)}), bf16[16,40,128]{2,1,0:T(8,128)(2,1)S(1)}, u32[]{:S(2)}, u32[]{:S(2)}) async-start(bf16[16,40,128]{2,1,0:T(8,128)(2,1)} %pad_maximum_fusion.4), calls=%async_computation.1 | async-start | bytes 327680 | tf_op jit(solution)/shard_map/all_to_all | solution.py:15
  46.9 7.3 %copy-start = (bf16[1,1,2,16,128,128]{5,4,3,2,1,0:T(8,128)(2,1)S(1)}, bf16[1,1,2,16,128,128]{5,4,3,2,1,0:T(8,128)(2,1)}, u32[]{:S(2)}) copy-start(bf16[1,1,2,16,128,128]{5,4,3,2,1,0:T(8,128)(2,1)} %param.11) | copy-start | bytes 3145732
  47.3 0.8 copy-start.4
  56.7 21.6 %all-to-all-start.2 = ((f32[32,24,128]{2,1,0:T(8,128)}), f32[32,24,128]{2,1,0:T(8,128)S(1)}, u32[]{:S(2)}, u32[]{:S(2)}) async-start(f32[32,24,128]{2,1,0:T(8,128)} %shard_map.94), calls=%async_computation.2 | async-start | bytes 786432 | tf_op jit(solution)/shard_map/all_to_all | solution.py:15
  80.3 28.9 %all-to-all-start.3 = ((f32[16,104,128]{2,1,0:T(8,128)}), f32[16,104,128]{2,1,0:T(8,128)S(1)}, u32[]{:S(2)}, u32[]{:S(2)}) async-start(f32[16,104,128]{2,1,0:T(8,128)} %pad_maximum_fusion.1), calls=%async_computation.3 | async-start | bytes 1703936 | tf_op jit(solution)/shard_map/all_to_all | solution.py:15
  109.2 0.7 copy-start.3
  109.9 1.0 copy-start.1
  132.4 7.0 %collective-permute-start = (f32[16,64,128]{2,1,0:T(8,128)S(1)}, f32[16,64,128]{2,1,0:T(8,128)S(1)}, u32[]{:S(2)}, u32[]{:S(2)}) collective-permute-start(f32[16,64,128]{2,1,0:T(8,128)S(1)} %all_to_all.45), channel_id=1, source_target_pairs={{0,1},{1,0},{2,3},{3,2},{4,5},{5,4},{6,7},{7,6},{8,9},{9,8},{10,11... | collective-permute-start | bytes 1572872 | tf_op jit(solution)/shard_map/ppermute | solution.py:22
  139.7 0.8 copy-start.5
  141.4 12.1 %all-to-all-start.5 = ((bf16[16,40,128]{2,1,0:T(8,128)(2,1)}), bf16[16,40,128]{2,1,0:T(8,128)(2,1)S(1)}, u32[]{:S(2)}, u32[]{:S(2)}) async-start(bf16[16,40,128]{2,1,0:T(8,128)(2,1)} %pad_maximum_fusion.5), calls=%async_computation.5 | async-start | bytes 327680 | tf_op jit(solution)/shard_map/all_to_all | solution.py:15
  156.0 23.0 %all-to-all-start.6 = ((f32[32,24,128]{2,1,0:T(8,128)}), f32[32,24,128]{2,1,0:T(8,128)S(1)}, u32[]{:S(2)}, u32[]{:S(2)}) async-start(f32[32,24,128]{2,1,0:T(8,128)} %shard_map.97), calls=%async_computation.6 | async-start | bytes 786432 | tf_op jit(solution)/shard_map/all_to_all | solution.py:15
  181.0 28.5 %all-to-all-start.7 = ((f32[16,104,128]{2,1,0:T(8,128)}), f32[16,104,128]{2,1,0:T(8,128)S(1)}, u32[]{:S(2)}, u32[]{:S(2)}) async-start(f32[16,104,128]{2,1,0:T(8,128)} %pad_maximum_fusion.2), calls=%async_computation.7 | async-start | bytes 1703936 | tf_op jit(solution)/shard_map/all_to_all | solution.py:15
  186.7 1.0 copy-start.6

commit v7 on v6

--- a/solution.py
+++ b/solution.py
@@ -253,7 +253,7 @@
     for sweep in range(sweeps):
         b_bf = state_b.astype(bf16)
         if sweep == 0:
-            rows = swap(spread(fold(init_a[0]), nc), "col")
+            rows = chip_gather(spread(fold(init_a[0]), nc // 2))
             a_rows = unfold(rows, rank).reshape(tiles_a, tile, rank)
             at3 = jnp.swapaxes(a_rows, 1, 2)
             a_bf3 = a_rows.astype(bf16)
@@ -317,12 +317,15 @@
         else:
             send, state_b = results
     per_a = tile // own_a
-    own = new_a.reshape(tiles_a, qa, per_a, own_a).transpose(0, 2, 1, 3).reshape(nc, qa, own_a)
+    own = new_a.reshape(tiles_a, qa, per_a, own_a).transpose(0, 2, 1, 3)
+    own = own.reshape(nc // 2, 2, qa, own_a).swapaxes(1, 2).reshape(nc // 2, qa, 2 * own_a)
     own = fold(pad_lanes(own))
-    everyone = jnp.broadcast_to(new_c.reshape(1, -1, LANES), (nc, qa * tiles_c, LANES))
-    got = swap(jnp.concatenate([own, everyone], axis=1), "col")
+    everyone = jnp.broadcast_to(new_c.reshape(1, -1, LANES), (nc // 2, qa * tiles_c, LANES))
+    got = chip_gather(jnp.concatenate([own, everyone], axis=1))
     a_got, c_got = take(got, [own.shape[1], qa * tiles_c])
-    out_a = unfold(a_got, own_a + -own_a % LANES)[:, :, :own_a].reshape(rank, own_a).T
+    a_got = unfold(a_got, 2 * own_a + -2 * own_a % LANES)
+    a_got = jnp.where(col % 2 == 0, a_got[:, :, :own_a], a_got[:, :, own_a : 2 * own_a])
+    out_a = a_got.reshape(rank, own_a).T
     out_c = jnp.swapaxes(c_got.reshape(nc, tiles_c, qa, LANES), 0, 1).reshape(tiles_c, rank, LANES)
     out_c = jnp.swapaxes(out_c, 1, 2).reshape(length, rank)
     return out_a[None], state_b[None], out_c

time: 242 us -> 234 us (0.967)
  blocking collectives: 46.7 us -> 36.6 us
  starting transfers between devices: 61.5 us -> 67.2 us
  waiting for transfers between devices: 97 us -> 92.7 us
    all_to_all x1 -> x0, blocking collectives: 26.7 us -> none  [swap(): return lax.all_to_all(x, axis, 0, 0, tiled=True)]
    all_to_all x7 -> x6, starting transfers between devices: 56 us -> 36.5 us  [swap(): return lax.all_to_all(x, axis, 0, 0, tiled=True)]
    all_to_all x1 -> x2, blocking collectives: 20 us -> 36.6 us  [chip_gather(): near = lax.all_to_all(x, 'col', 0, 0, axis_index_groups=groups, tiled=True)]
    all_to_all x0 -> x1, starting transfers between devices: none -> 16.2 us  [chip_gather(): near = lax.all_to_all(x, 'col', 0, 0, axis_index_groups=groups, tiled=True)]
    all_to_all x7 -> x6, waiting for transfers between devices: 95.5 us -> 80.6 us  [swap(): return lax.all_to_all(x, axis, 0, 0, tiled=True)]
    ppermute x1 -> x3, starting transfers between devices: 5.47 us -> 14.5 us  [chip_gather(): far = lax.ppermute(near, 'col', [(i, i ^ 1) for i in range(nc)])]
    all_to_all x0 -> x1, waiting for transfers between devices: none -> 8.26 us  [chip_gather(): near = lax.all_to_all(x, 'col', 0, 0, axis_index_groups=groups, tiled=True)]
    unnamed x33 -> x32, local copies, waits for them, and re-layouts: 6.25 us -> 6.81 us
  transfers between devices with their start and end apart: 8 -> 10, of which waited for: 8 -> 10; matrix products, arithmetic and copies ran while one was open for 3% -> 3% of each run, Pallas kernels for 1% -> 1%
where the time goes in v7:
time: 234 us; the launch traced here: 233 us
  waiting for transfers between devices  92.7 us (40%)
  starting transfers between devices  67.2 us (29%)
  blocking collectives  36.6 us (16%)
  local copies, waits for them, and re-layouts  17 us (7%)
  Pallas kernels  11.1 us (5%)
  other arithmetic  4.62 us (2%)
    all_to_all x6, waiting for transfers between devices, swap(): return lax.all_to_all(x, axis, 0, 0, tiled=True)  80.6 us
    all_to_all x2, blocking collectives, chip_gather(): near = lax.all_to_all(x, 'col', 0, 0, axis_index_groups=groups, tiled=True)  36.6 us
    all_to_all x6, starting transfers between devices, swap(): return lax.all_to_all(x, axis, 0, 0, tiled=True)  36.5 us
    all_to_all x1, starting transfers between devices, chip_gather(): near = lax.all_to_all(x, 'col', 0, 0, axis_index_groups=groups, tiled=True)  16.2 us
    ppermute x3, starting transfers between devices, chip_gather(): far = lax.ppermute(near, 'col', [(i, i ^ 1) for i in range(nc)])  14.5 us
    pallas_call x6, Pallas kernels, call(): pl.pallas_call(kernel, out_shape=[jax.ShapeDtypeStruct(shape, jnp.float32...  11.1 us
    all_to_all x1, waiting for transfers between devices, chip_gather(): near = lax.all_to_all(x, 'col', 0, 0, axis_index_groups=groups, tiled=True)  8.26 us
    unnamed x32, local copies, waits for them, and re-layouts  6.81 us
  transfers between devices with their start and end apart: 10, of which 10 were waited for; matrix products, arithmetic and copies ran while one was open for 3% of the time, Pallas kernels for 1%

profile of v7, /device:TPU:1, one launch (start us, length us, event | category | flops | bytes accessed | tf_op | source)
XLA Modules:
  0.0 232.8 jit_solution(9201075682862448973)
XLA Ops:
  2.2 16.2 %all-to-all-start = ((f32[16,32,128]{2,1,0:T(8,128)}), f32[16,32,128]{2,1,0:T(8,128)S(1)}, u32[]{:S(2)}, u32[]{:S(2)}) async-start(f32[16,32,128]{2,1,0:T(8,128)} %broadcast_in_dim.33), calls=%async_computation | async-start | bytes 524288 | tf_op jit(solution)/shard_map/all_to_all | solution.py:21
  22.0 8.3 %all-to-all-done = f32[16,32,128]{2,1,0:T(8,128)S(1)} async-done(((f32[16,32,128]{2,1,0:T(8,128)}), f32[16,32,128]{2,1,0:T(8,128)S(1)}, u32[]{:S(2)}, u32[]{:S(2)}) %all-to-all-start) | async-done | bytes 262176 | tf_op jit(solution)/shard_map/all_to_all | solution.py:21
  30.2 4.0 %collective-permute-start = (f32[16,32,128]{2,1,0:T(8,128)S(1)}, f32[16,32,128]{2,1,0:T(8,128)S(1)}, u32[]{:S(2)}, u32[]{:S(2)}) collective-permute-start(f32[16,32,128]{2,1,0:T(8,128)S(1)} %all-to-all-done), channel_id=1, source_target_pairs={{0,1},{1,0},{2,3},{3,2},{4,5},{5,4},{6,7},{7,6},{8,9},{9,8},{10,11... | collective-permute-start | bytes 786440 | tf_op jit(solution)/shard_map/ppermute | solution.py:22
  37.2 6.5 %all-to-all-start.1 = ((bf16[16,40,128]{2,1,0:T(8,128)(2,1)}), bf16[16,40,128]{2,1,0:T(8,128)(2,1)S(1)}, u32[]{:S(2)}, u32[]{:S(2)}) async-start(bf16[16,40,128]{2,1,0:T(8,128)(2,1)} %pad_maximum_fusion.7), calls=%async_computation.1 | async-start | bytes 327680 | tf_op jit(solution)/shard_map/all_to_all | solution.py:15
  44.9 6.2 %all-to-all-done.1.got = bf16[16,40,128]{2,1,0:T(8,128)(2,1)S(1)} async-done(((bf16[16,40,128]{2,1,0:T(8,128)(2,1)}), bf16[16,40,128]{2,1,0:T(8,128)(2,1)S(1)}, u32[]{:S(2)}, u32[]{:S(2)}) %all-to-all-start.1) | async-done | bytes 163872 | tf_op jit(solution)/shard_map/all_to_all | solution.py:15
  51.1 2.5 %shard_map.94 = f32[32,24,128]{2,1,0:T(8,128)} custom-call(s32[5,2]{1,0:T(8,128)S(1)} %copy.111.meta, bf16[16,40,128]{2,1,0:T(8,128)(2,1)S(1)} %all-to-all-done.1.got, bf16[2,16,128,128]{3,2,1,0:T(8,128)(2,1)S(1)} %bitcast.136, bf16[4,128,256]{2,1,0:T(8,128)(2,1)S(1)} %bitcast_convert_fusion.a_ref, bf16[512,256]{1,0:T(8,128)(2,1)S(1)} %convert_element_type.57.c_ref), custom_call_target="tpu_custom_call" | custom-call | flops 268435456 | bytes 1048576 | tf_op jit(solution)/shard_map/pallas_call | solution.py:211
  53.5 6.1 %all-to-all-start.2 = ((f32[32,24,128]{2,1,0:T(8,128)}), f32[32,24,128]{2,1,0:T(8,128)S(1)}, u32[]{:S(2)}, u32[]{:S(2)}) async-start(f32[32,24,128]{2,1,0:T(8,128)} %shard_map.94), calls=%async_computation.2 | async-start | bytes 786432 | tf_op jit(solution)/shard_map/all_to_all | solution.py:15
  61.0 13.7 %all-to-all-done.2.got_c = f32[32,24,128]{2,1,0:T(8,128)S(1)} async-done(((f32[32,24,128]{2,1,0:T(8,128)}), f32[32,24,128]{2,1,0:T(8,128)S(1)}, u32[]{:S(2)}, u32[]{:S(2)}) %all-to-all-start.2) | async-done | bytes 393248 | tf_op jit(solution)/shard_map/all_to_all | solution.py:15
  76.7 5.7 %all-to-all-start.3 = ((f32[16,104,128]{2,1,0:T(8,128)}), f32[16,104,128]{2,1,0:T(8,128)S(1)}, u32[]{:S(2)}, u32[]{:S(2)}) async-start(f32[16,104,128]{2,1,0:T(8,128)} %pad_maximum_fusion.1), calls=%async_computation.3 | async-start | bytes 1703936 | tf_op jit(solution)/shard_map/all_to_all | solution.py:15
  84.9 2.0 copy.93
  86.9 18.3 %all-to-all-done.3.got_r = f32[16,104,128]{2,1,0:T(8,128)S(1)} async-done(((f32[16,104,128]{2,1,0:T(8,128)}), f32[16,104,128]{2,1,0:T(8,128)S(1)}, u32[]{:S(2)}, u32[]{:S(2)}) %all-to-all-start.3) | async-done | bytes 852000 | tf_op jit(solution)/shard_map/all_to_all | solution.py:15
  108.4 20.3 %all_to_all.45 = f32[16,64,128]{2,1,0:T(8,128)S(1)} all-to-all(f32[16,64,128]{2,1,0:T(8,128)S(1)} %get-tuple-element.33), channel_id=1, replica_groups={{0,2,4,6,8,10,12,14,16,18,20,22,24,26,28,30},{1,3,5,7,9,11,13,15,17,19,..., dimensions={0} | all-to-all | bytes 1048576 | tf_op jit(solution)/shard_map/all_to_all | solution.py:21
  128.7 5.5 %collective-permute-start.1 = (f32[16,64,128]{2,1,0:T(8,128)S(1)}, f32[16,64,128]{2,1,0:T(8,128)S(1)}, u32[]{:S(2)}, u32[]{:S(2)}) collective-permute-start(f32[16,64,128]{2,1,0:T(8,128)S(1)} %all_to_all.45), channel_id=1, source_target_pairs={{0,1},{1,0},{2,3},{3,2},{4,5},{5,4},{6,7},{7,6},{8,9},{9,8},{10,11... | collective-permute-start | bytes 1572872 | tf_op jit(solution)/shard_map/ppermute | solution.py:22
  134.3 1.5 collective-permute-done.1
  137.9 4.7 %all-to-all-start.5 = ((bf16[16,40,128]{2,1,0:T(8,128)(2,1)}), bf16[16,40,128]{2,1,0:T(8,128)(2,1)S(1)}, u32[]{:S(2)}, u32[]{:S(2)}) async-start(bf16[16,40,128]{2,1,0:T(8,128)(2,1)} %pad_maximum_fusion.8), calls=%async_computation.5 | async-start | bytes 327680 | tf_op jit(solution)/shard_map/all_to_all | solution.py:15
  142.9 7.0 %all-to-all-done.5.got = bf16[16,40,128]{2,1,0:T(8,128)(2,1)S(1)} async-done(((bf16[16,40,128]{2,1,0:T(8,128)(2,1)}), bf16[16,40,128]{2,1,0:T(8,128)(2,1)S(1)}, u32[]{:S(2)}, u32[]{:S(2)}) %all-to-all-start.5) | async-done | bytes 163872 | tf_op jit(solution)/shard_map/all_to_all | solution.py:15
  149.9 2.5 %shard_map.97 = f32[32,24,128]{2,1,0:T(8,128)} custom-call(s32[5,2]{1,0:T(8,128)S(1)} %copy.111.meta, bf16[16,40,128]{2,1,0:T(8,128)(2,1)S(1)} %all-to-all-done.5.got, bf16[2,16,128,128]{3,2,1,0:T(8,128)(2,1)S(1)} %bitcast.138, bf16[4,128,256]{2,1,0:T(8,128)(2,1)S(1)} %copy.103.a_ref, bf16[512,256]{1,0:T(8,128)(2,1)S(1)} %bitcast.140), custom_call_target="tpu_custom_call" | custom-call | flops 268435456 | bytes 1048576 | tf_op jit(solution)/shard_map/pallas_call | solution.py:211
  152.4 7.9 %all-to-all-start.6 = ((f32[32,24,128]{2,1,0:T(8,128)}), f32[32,24,128]{2,1,0:T(8,128)S(1)}, u32[]{:S(2)}, u32[]{:S(2)}) async-start(f32[32,24,128]{2,1,0:T(8,128)} %shard_map.97), calls=%async_computation.6 | async-start | bytes 786432 | tf_op jit(solution)/shard_map/all_to_all | solution.py:15
  161.6 13.7 %all-to-all-done.6.got_c = f32[32,24,128]{2,1,0:T(8,128)S(1)} async-done(((f32[32,24,128]{2,1,0:T(8,128)}), f32[32,24,128]{2,1,0:T(8,128)S(1)}, u32[]{:S(2)}, u32[]{:S(2)}) %all-to-all-start.6) | async-done | bytes 393248 | tf_op jit(solution)/shard_map/all_to_all | solution.py:15
  177.4 5.7 %all-to-all-start.7 = ((f32[16,104,128]{2,1,0:T(8,128)}), f32[16,104,128]{2,1,0:T(8,128)S(1)}, u32[]{:S(2)}, u32[]{:S(2)}) async-start(f32[16,104,128]{2,1,0:T(8,128)} %pad_maximum_fusion.2), calls=%async_computation.7 | async-start | bytes 1703936 | tf_op jit(solution)/shard_map/all_to_all | solution.py:15
  184.2 21.7 %all-to-all-done.7.got_r = f32[16,104,128]{2,1,0:T(8,128)S(1)} async-done(((f32[16,104,128]{2,1,0:T(8,128)}), f32[16,104,128]{2,1,0:T(8,128)S(1)}, u32[]{:S(2)}, u32[]{:S(2)}) %all-to-all-start.7) | async-done | bytes 852000 | tf_op jit(solution)/shard_map/all_to_all | solution.py:15
  205.9 2.0 shard_map.99
  208.3 16.3 %all_to_all.46 = f32[16,40,128]{2,1,0:T(8,128)S(1)} all-to-all(f32[16,40,128]{2,1,0:T(8,128)S(1)} %select_maximum_fusion), channel_id=1, replica_groups={{0,2,4,6,8,10,12,14,16,18,20,22,24,26,28,30},{1,3,5,7,9,11,13,15,17,19,..., dimensions={0} | all-to-all | bytes 655360 | tf_op jit(solution)/shard_map/all_to_all | solution.py:21
  224.6 5.0 %collective-permute-start.2 = (f32[16,40,128]{2,1,0:T(8,128)S(1)}, f32[16,40,128]{2,1,0:T(8,128)S(1)}, u32[]{:S(2)}, u32[]{:S(2)}) collective-permute-start(f32[16,40,128]{2,1,0:T(8,128)S(1)} %all_to_all.46), channel_id=1, source_target_pairs={{0,1},{1,0},{2,3},{3,2},{4,5},{5,4},{6,7},{7,6},{8,9},{9,8},{10,11... | collective-permute-start | bytes 983048 | tf_op jit(solution)/shard_map/ppermute | solution.py:22
  (126 shorter events, 27.6 us)
Async XLA Ops:
  0.6 20.6 %copy-start.7 = (f32[512,256]{1,0:T(8,128)S(1)}, f32[512,256]{1,0:T(8,128)}, u32[]{:S(2)}) copy-start(f32[512,256]{1,0:T(8,128)} %param.17) | copy-start | bytes 1572868
  2.2 28.1 %all-to-all-start = ((f32[16,32,128]{2,1,0:T(8,128)}), f32[16,32,128]{2,1,0:T(8,128)S(1)}, u32[]{:S(2)}, u32[]{:S(2)}) async-start(f32[16,32,128]{2,1,0:T(8,128)} %broadcast_in_dim.33), calls=%async_computation | async-start | bytes 524288 | tf_op jit(solution)/shard_map/all_to_all | solution.py:21
  19.0 0.7 copy-start.8
  21.2 0.7 copy-start.2
  30.2 5.2 %collective-permute-start = (f32[16,32,128]{2,1,0:T(8,128)S(1)}, f32[16,32,128]{2,1,0:T(8,128)S(1)}, u32[]{:S(2)}, u32[]{:S(2)}) collective-permute-start(f32[16,32,128]{2,1,0:T(8,128)S(1)} %all-to-all-done), channel_id=1, source_target_pairs={{0,1},{1,0},{2,3},{3,2},{4,5},{5,4},{6,7},{7,6},{8,9},{9,8},{10,11... | collective-permute-start | bytes 786440 | tf_op jit(solution)/shard_map/ppermute | solution.py:22
  37.2 13.9 %all-to-all-start.1 = ((bf16[16,40,128]{2,1,0:T(8,128)(2,1)}), bf16[16,40,128]{2,1,0:T(8,128)(2,1)S(1)}, u32[]{:S(2)}, u32[]{:S(2)}) async-start(bf16[16,40,128]{2,1,0:T(8,128)(2,1)} %pad_maximum_fusion.7), calls=%async_computation.1 | async-start | bytes 327680 | tf_op jit(solution)/shard_map/all_to_all | solution.py:15
  43.7 7.3 %copy-start = (bf16[1,1,2,16,128,128]{5,4,3,2,1,0:T(8,128)(2,1)S(1)}, bf16[1,1,2,16,128,128]{5,4,3,2,1,0:T(8,128)(2,1)}, u32[]{:S(2)}) copy-start(bf16[1,1,2,16,128,128]{5,4,3,2,1,0:T(8,128)(2,1)} %param.11) | copy-start | bytes 3145732
  44.1 0.8 copy-start.4
  53.5 21.2 %all-to-all-start.2 = ((f32[32,24,128]{2,1,0:T(8,128)}), f32[32,24,128]{2,1,0:T(8,128)S(1)}, u32[]{:S(2)}, u32[]{:S(2)}) async-start(f32[32,24,128]{2,1,0:T(8,128)} %shard_map.94), calls=%async_computation.2 | async-start | bytes 786432 | tf_op jit(solution)/shard_map/all_to_all | solution.py:15
  76.7 28.5 %all-to-all-start.3 = ((f32[16,104,128]{2,1,0:T(8,128)}), f32[16,104,128]{2,1,0:T(8,128)S(1)}, u32[]{:S(2)}, u32[]{:S(2)}) async-start(f32[16,104,128]{2,1,0:T(8,128)} %pad_maximum_fusion.1), calls=%async_computation.3 | async-start | bytes 1703936 | tf_op jit(solution)/shard_map/all_to_all | solution.py:15
  105.2 0.7 copy-start.3
  105.9 1.0 copy-start.1
  128.7 7.0 %collective-permute-start.1 = (f32[16,64,128]{2,1,0:T(8,128)S(1)}, f32[16,64,128]{2,1,0:T(8,128)S(1)}, u32[]{:S(2)}, u32[]{:S(2)}) collective-permute-start(f32[16,64,128]{2,1,0:T(8,128)S(1)} %all_to_all.45), channel_id=1, source_target_pairs={{0,1},{1,0},{2,3},{3,2},{4,5},{5,4},{6,7},{7,6},{8,9},{9,8},{10,11... | collective-permute-start | bytes 1572872 | tf_op jit(solution)/shard_map/ppermute | solution.py:22
  136.1 0.8 copy-start.5
  137.9 12.1 %all-to-all-start.5 = ((bf16[16,40,128]{2,1,0:T(8,128)(2,1)}), bf16[16,40,128]{2,1,0:T(8,128)(2,1)S(1)}, u32[]{:S(2)}, u32[]{:S(2)}) async-start(bf16[16,40,128]{2,1,0:T(8,128)(2,1)} %pad_maximum_fusion.8), calls=%async_computation.5 | async-start | bytes 327680 | tf_op jit(solution)/shard_map/all_to_all | solution.py:15
  152.4 23.0 %all-to-all-start.6 = ((f32[32,24,128]{2,1,0:T(8,128)}), f32[32,24,128]{2,1,0:T(8,128)S(1)}, u32[]{:S(2)}, u32[]{:S(2)}) async-start(f32[32,24,128]{2,1,0:T(8,128)} %shard_map.97), calls=%async_computation.6 | async-start | bytes 786432 | tf_op jit(solution)/shard_map/all_to_all | solution.py:15
  177.4 28.5 %all-to-all-start.7 = ((f32[16,104,128]{2,1,0:T(8,128)}), f32[16,104,128]{2,1,0:T(8,128)S(1)}, u32[]{:S(2)}, u32[]{:S(2)}) async-start(f32[16,104,128]{2,1,0:T(8,128)} %pad_maximum_fusion.2), calls=%async_computation.7 | async-start | bytes 1703936 | tf_op jit(solution)/shard_map/all_to_all | solution.py:15
  183.1 1.0 copy-start.6
  224.6 6.3 %collective-permute-start.2 = (f32[16,40,128]{2,1,0:T(8,128)S(1)}, f32[16,40,128]{2,1,0:T(8,128)S(1)}, u32[]{:S(2)}, u32[]{:S(2)}) collective-permute-start(f32[16,40,128]{2,1,0:T(8,128)S(1)} %all_to_all.46), channel_id=1, source_target_pairs={{0,1},{1,0},{2,3},{3,2},{4,5},{5,4},{6,7},{7,6},{8,9},{9,8},{10,11... | collective-permute-start | bytes 983048 | tf_op jit(solution)/shard_map/ppermute | solution.py:22

commit v8 on v7

--- a/solution.py
+++ b/solution.py
@@ -60,7 +60,7 @@
     )
 
 
-def deep_kernel(meta, slab, a_ref, c_ref, out, drive):
+def deep_kernel(meta, steps, slab, a_ref, c_ref, out, drive):
     slots, depth, tile, _ = slab.shape
     nr, rows, _ = out.shape
     half = a_ref.shape[2] // LANES
@@ -157,13 +157,27 @@
     third = LANES // 2
     mine = pl.ds(pl.multiple_of(meta[4, 1] * qa, qa), qa)
     at = own * half
-    for h in range(half):
-        part = got_r[:, at + h * qb : at + (h + 1) * qb, :]
-        sa[:, h * LANES : (h + 1) * LANES] = part.reshape(rank, LANES)
+    tail = at + qb + tiles_c * qa
+    lane = lax.broadcasted_iota(jnp.int32, (qb, LANES), 1)
+    for r in range(nr):
+        rest = got_r[r, tail : tail + qb // 2, :]
+        rest = jnp.concatenate(
+            [pltpu.roll(rest, LANES - qb, 1), pltpu.roll(rest, LANES - 2 * qb, 1)], axis=0
+        )
+        parts = [got_r[r, at : at + qb, :], jnp.where(lane < qb, rest, 0.0)]
+        whole, shift = divmod(r * qb, LANES)
+        if shift:
+            turned = [pltpu.roll(part, shift, 1) for part in parts]
+            parts = [jnp.where(lane < shift, turned[1 - h], turned[h]) for h in range(2)]
+        for h in range(2):
+            slot = (h + whole) % 2
+            sa[r * qb : (r + 1) * qb, slot * LANES : (slot + 1) * LANES] = parts[h]
+    upper = sa[...]
+    sa[...] = upper + upper.T
     drive_b = jnp.concatenate(
         [jnp.sum(got_r[:, own * h : own * (h + 1), :], axis=0) for h in range(half)], axis=1
     )
-    at += qb * half
+    at += qb
     drive_c = [
         jnp.sum(got_r[:, at + t * qa : at + (t + 1) * qa, :], axis=0) for t in range(tiles_c)
     ]
@@ -171,9 +185,11 @@
     per = LANES // qb
     sb_parts = []
     for h in range(half):
-        part = got_r[h * per, at : at + qa, :]
-        for i in range(1, per):
-            part = part + pltpu.roll(got_r[h * per + i, at : at + qa, :], qb * i, 1)
+        part = jnp.zeros((qa, LANES), jnp.float32)
+        for i in range(per):
+            piece = got_r[h * per + i, at : at + qa, :]
+            piece = jnp.where(lax.broadcasted_iota(jnp.int32, piece.shape, 1) < qb, piece, 0.0)
+            part = part + (pltpu.roll(piece, qb * i, 1) if i else piece)
         sb_parts.append(part)
     sb_c = jnp.concatenate(sb_parts, axis=1)
     drive_a = [jnp.zeros((qa, tile), jnp.float32) for _ in range(tiles_a)]
@@ -267,6 +283,8 @@
             c_bf = jnp.swapaxes(ct3.astype(bf16), 1, 2).reshape(length, rank)
         a_all = a_bf3.reshape(tiles_a * tile, rank)
         gram_a = gram(a_all)
+        if sweep == 0:
+            a_bf3, at3, ct3 = lax.optimization_barrier((a_bf3, at3, ct3))
         slice_a = lax.dynamic_slice_in_dim(gram_a, col * qa, qa, 0)
         slice_a = jnp.swapaxes(slice_a.reshape(qa, nr, qb), 0, 1)
         high = lax.reduce_precision(slice_a, 8, 7)
@@ -281,7 +299,7 @@
             deep_kernel,
             [(nr, own_b * half, LANES)],
             [pltpu.VMEM((tiles_b * tile, rank), f32)],
-            work, slab.size * 2, (meta, slab, a_bf3, c_bf),
+            work, slab.size * 2, (meta, step_sizes, slab, a_bf3, c_bf), scalars=2,
         )
         (send,) = call(
             wide_kernel,
@@ -297,9 +315,16 @@
         onehot = (spots_k[:, :, None] == lax.iota(jnp.int32, layers).astype(f32)).astype(f32)
         c_got = mixed[:, :, : slots * depth].reshape(nc, qa, slots, depth)
         drive_c = jnp.einsum("sqmk,smb->qbk", c_got, onehot, precision=HIGH).reshape(qa, length)
-        strip = mixed[:, :, slots * depth : second].reshape(rank, qb).T
-        piece_b = pad_lanes(jnp.sum(mixed[:, :, second:third], axis=0))
-        everyone = jnp.concatenate([fold(strip), fold(drive_c), piece_b], axis=0)
+        strip = mixed[:, :, slots * depth : second].reshape(rank, qb)
+        kept = LANES + qb
+        strip = lax.dynamic_slice_in_dim(jnp.concatenate([strip, strip]), row * qb, kept, 0)
+        place = lax.broadcasted_iota(jnp.int32, strip.shape, 0)
+        strip = jnp.where((place < qb) | (place >= LANES), 0.5 * strip, strip).T
+        rest = jnp.concatenate([strip[: qb // 2, LANES:], strip[qb // 2 :, LANES:]], axis=1)
+        rest = jnp.pad(rest, [(0, qa - qb // 2), (0, 0)])
+        piece_b = jnp.sum(mixed[:, :, second:third], axis=0)
+        piece_b = pad_lanes(jnp.concatenate([piece_b, rest], axis=1))
+        everyone = jnp.concatenate([strip[:, :LANES], fold(drive_c), piece_b], axis=0)
         everyone = jnp.broadcast_to(everyone[None], (nr,) + everyone.shape)
         got_r = swap(jnp.concatenate([blocks, everyone], axis=1), "row")
         last = sweep == sweeps - 1

time: 234 us -> 228 us (0.974)
  local copies, waits for them, and re-layouts: 17 us -> 12.2 us
  waiting for transfers between devices: 92.7 us -> 89.4 us
    all_to_all x6, waiting for transfers between devices: 80.6 us -> 76.9 us  [swap(): return lax.all_to_all(x, axis, 0, 0, tiled=True)]
    unnamed x32 -> x30, local copies, waits for them, and re-layouts: 6.81 us -> 5.01 us
  transfers between devices with their start and end apart: 10 -> 10, of which waited for: 10 -> 10; matrix products, arithmetic and copies ran while one was open for 3% -> 2% of each run, Pallas kernels for 1% -> 1%
where the time goes in v8:
time: 228 us; the launch traced here: 227 us
  waiting for transfers between devices  89.4 us (39%)
  starting transfers between devices  67.7 us (30%)
  blocking collectives  36.3 us (16%)
  local copies, waits for them, and re-layouts  12.2 us (5%)
  Pallas kernels  11.3 us (5%)
  other arithmetic  5.9 us (3%)
    all_to_all x6, waiting for transfers between devices, swap(): return lax.all_to_all(x, axis, 0, 0, tiled=True)  76.9 us
    all_to_all x6, starting transfers between devices, swap(): return lax.all_to_all(x, axis, 0, 0, tiled=True)  36.6 us
    all_to_all x2, blocking collectives, chip_gather(): near = lax.all_to_all(x, 'col', 0, 0, axis_index_groups=groups, tiled=True)  36.3 us
    all_to_all x1, starting transfers between devices, chip_gather(): near = lax.all_to_all(x, 'col', 0, 0, axis_index_groups=groups, tiled=True)  16.4 us
    ppermute x3, starting transfers between devices, chip_gather(): far = lax.ppermute(near, 'col', [(i, i ^ 1) for i in range(nc)])  14.7 us
    pallas_call x6, Pallas kernels, call(): pl.pallas_call(kernel, out_shape=[jax.ShapeDtypeStruct(shape, jnp.float32...  11.3 us
    all_to_all x1, waiting for transfers between devices, chip_gather(): near = lax.all_to_all(x, 'col', 0, 0, axis_index_groups=groups, tiled=True)  8.96 us
    unnamed x30, local copies, waits for them, and re-layouts  5.01 us
  transfers between devices with their start and end apart: 10, of which 10 were waited for; matrix products, arithmetic and copies ran while one was open for 2% of the time, Pallas kernels for 1%

profile of v8, /device:TPU:1, one launch (start us, length us, event | category | flops | bytes accessed | tf_op | source)
XLA Modules:
  0.0 227.1 jit_solution(5929267076178695248)
XLA Ops:
  2.2 16.4 %all-to-all-start = ((f32[16,32,128]{2,1,0:T(8,128)}), f32[16,32,128]{2,1,0:T(8,128)S(1)}, u32[]{:S(2)}, u32[]{:S(2)}) async-start(f32[16,32,128]{2,1,0:T(8,128)} %broadcast_in_dim.33), calls=%async_computation | async-start | bytes 524288 | tf_op jit(solution)/shard_map/all_to_all | solution.py:21
  21.4 9.0 %all-to-all-done = f32[16,32,128]{2,1,0:T(8,128)S(1)} async-done(((f32[16,32,128]{2,1,0:T(8,128)}), f32[16,32,128]{2,1,0:T(8,128)S(1)}, u32[]{:S(2)}, u32[]{:S(2)}) %all-to-all-start) | async-done | bytes 262176 | tf_op jit(solution)/shard_map/all_to_all | solution.py:21
  30.4 4.0 %collective-permute-start = (f32[16,32,128]{2,1,0:T(8,128)S(1)}, f32[16,32,128]{2,1,0:T(8,128)S(1)}, u32[]{:S(2)}, u32[]{:S(2)}) collective-permute-start(f32[16,32,128]{2,1,0:T(8,128)S(1)} %all-to-all-done), channel_id=1, source_target_pairs={{0,1},{1,0},{2,3},{3,2},{4,5},{5,4},{6,7},{7,6},{8,9},{9,8},{10,11... | collective-permute-start | bytes 786440 | tf_op jit(solution)/shard_map/ppermute | solution.py:22
  37.3 6.5 %all-to-all-start.1 = ((bf16[16,40,128]{2,1,0:T(8,128)(2,1)}), bf16[16,40,128]{2,1,0:T(8,128)(2,1)S(1)}, u32[]{:S(2)}, u32[]{:S(2)}) async-start(bf16[16,40,128]{2,1,0:T(8,128)(2,1)} %pad_maximum_fusion.7), calls=%async_computation.1 | async-start | bytes 327680 | tf_op jit(solution)/shard_map/all_to_all | solution.py:15
  46.0 5.2 %all-to-all-done.1.got = bf16[16,40,128]{2,1,0:T(8,128)(2,1)S(1)} async-done(((bf16[16,40,128]{2,1,0:T(8,128)(2,1)}), bf16[16,40,128]{2,1,0:T(8,128)(2,1)S(1)}, u32[]{:S(2)}, u32[]{:S(2)}) %all-to-all-start.1) | async-done | bytes 163872 | tf_op jit(solution)/shard_map/all_to_all | solution.py:15
  51.2 2.5 %shard_map.94 = f32[32,24,128]{2,1,0:T(8,128)} custom-call(s32[5,2]{1,0:T(8,128)S(1)} %copy.119.meta, bf16[16,40,128]{2,1,0:T(8,128)(2,1)S(1)} %all-to-all-done.1.got, bf16[2,16,128,128]{3,2,1,0:T(8,128)(2,1)S(1)} %bitcast.138, bf16[4,128,256]{2,1,0:T(8,128)(2,1)S(1)} %bitcast_convert_fusion.a_ref, bf16[512,256]{1,0:T(8,128)(2,1)S(1)} %convert_element_type.59.c_ref), custom_call_target="tpu_custom_call" | custom-call | flops 268435456 | bytes 1048576 | tf_op jit(solution)/shard_map/pallas_call | solution.py:227
  53.7 6.1 %all-to-all-start.2 = ((f32[32,24,128]{2,1,0:T(8,128)}), f32[32,24,128]{2,1,0:T(8,128)S(1)}, u32[]{:S(2)}, u32[]{:S(2)}) async-start(f32[32,24,128]{2,1,0:T(8,128)} %shard_map.94), calls=%async_computation.2 | async-start | bytes 786432 | tf_op jit(solution)/shard_map/all_to_all | solution.py:15
  61.8 13.0 %all-to-all-done.2.got_c = f32[32,24,128]{2,1,0:T(8,128)S(1)} async-done(((f32[32,24,128]{2,1,0:T(8,128)}), f32[32,24,128]{2,1,0:T(8,128)S(1)}, u32[]{:S(2)}, u32[]{:S(2)}) %all-to-all-start.2) | async-done | bytes 393248 | tf_op jit(solution)/shard_map/all_to_all | solution.py:15
  77.0 5.7 %all-to-all-start.3 = ((f32[16,88,128]{2,1,0:T(8,128)}), f32[16,88,128]{2,1,0:T(8,128)S(1)}, u32[]{:S(2)}, u32[]{:S(2)}) async-start(f32[16,88,128]{2,1,0:T(8,128)} %pad_maximum_fusion.1), calls=%async_computation.3 | async-start | bytes 1441792 | tf_op jit(solution)/shard_map/all_to_all | solution.py:15
  83.7 19.1 %all-to-all-done.3.got_r = f32[16,88,128]{2,1,0:T(8,128)S(1)} async-done(((f32[16,88,128]{2,1,0:T(8,128)}), f32[16,88,128]{2,1,0:T(8,128)S(1)}, u32[]{:S(2)}, u32[]{:S(2)}) %all-to-all-start.3) | async-done | bytes 720928 | tf_op jit(solution)/shard_map/all_to_all | solution.py:15
  103.7 1.5 shard_map.96
  105.2 20.1 %all_to_all.45 = f32[16,64,128]{2,1,0:T(8,128)S(1)} all-to-all(f32[16,64,128]{2,1,0:T(8,128)S(1)} %get-tuple-element.39), channel_id=1, replica_groups={{0,2,4,6,8,10,12,14,16,18,20,22,24,26,28,30},{1,3,5,7,9,11,13,15,17,19,..., dimensions={0} | all-to-all | bytes 1048576 | tf_op jit(solution)/shard_map/all_to_all | solution.py:21
  125.3 5.4 %collective-permute-start.1 = (f32[16,64,128]{2,1,0:T(8,128)S(1)}, f32[16,64,128]{2,1,0:T(8,128)S(1)}, u32[]{:S(2)}, u32[]{:S(2)}) collective-permute-start(f32[16,64,128]{2,1,0:T(8,128)S(1)} %all_to_all.45), channel_id=1, source_target_pairs={{0,1},{1,0},{2,3},{3,2},{4,5},{5,4},{6,7},{7,6},{8,9},{9,8},{10,11... | collective-permute-start | bytes 1572872 | tf_op jit(solution)/shard_map/ppermute | solution.py:22
  130.7 1.5 collective-permute-done.1
  134.4 5.0 %all-to-all-start.5 = ((bf16[16,40,128]{2,1,0:T(8,128)(2,1)}), bf16[16,40,128]{2,1,0:T(8,128)(2,1)S(1)}, u32[]{:S(2)}, u32[]{:S(2)}) async-start(bf16[16,40,128]{2,1,0:T(8,128)(2,1)} %pad_maximum_fusion.8), calls=%async_computation.5 | async-start | bytes 327680 | tf_op jit(solution)/shard_map/all_to_all | solution.py:15
  139.7 7.0 %all-to-all-done.5.got = bf16[16,40,128]{2,1,0:T(8,128)(2,1)S(1)} async-done(((bf16[16,40,128]{2,1,0:T(8,128)(2,1)}), bf16[16,40,128]{2,1,0:T(8,128)(2,1)S(1)}, u32[]{:S(2)}, u32[]{:S(2)}) %all-to-all-start.5) | async-done | bytes 163872 | tf_op jit(solution)/shard_map/all_to_all | solution.py:15
  146.7 2.5 %shard_map.97 = f32[32,24,128]{2,1,0:T(8,128)} custom-call(s32[5,2]{1,0:T(8,128)S(1)} %copy.119.meta, bf16[16,40,128]{2,1,0:T(8,128)(2,1)S(1)} %all-to-all-done.5.got, bf16[2,16,128,128]{3,2,1,0:T(8,128)(2,1)S(1)} %bitcast.140, bf16[4,128,256]{2,1,0:T(8,128)(2,1)S(1)} %copy.110.a_ref, bf16[512,256]{1,0:T(8,128)(2,1)S(1)} %bitcast.142), custom_call_target="tpu_custom_call" | custom-call | flops 268435456 | bytes 1048576 | tf_op jit(solution)/shard_map/pallas_call | solution.py:227
  149.2 7.7 %all-to-all-start.6 = ((f32[32,24,128]{2,1,0:T(8,128)}), f32[32,24,128]{2,1,0:T(8,128)S(1)}, u32[]{:S(2)}, u32[]{:S(2)}) async-start(f32[32,24,128]{2,1,0:T(8,128)} %shard_map.97), calls=%async_computation.6 | async-start | bytes 786432 | tf_op jit(solution)/shard_map/all_to_all | solution.py:15
  158.4 13.7 %all-to-all-done.6.got_c = f32[32,24,128]{2,1,0:T(8,128)S(1)} async-done(((f32[32,24,128]{2,1,0:T(8,128)}), f32[32,24,128]{2,1,0:T(8,128)S(1)}, u32[]{:S(2)}, u32[]{:S(2)}) %all-to-all-start.6) | async-done | bytes 393248 | tf_op jit(solution)/shard_map/all_to_all | solution.py:15
  174.2 5.7 %all-to-all-start.7 = ((f32[16,88,128]{2,1,0:T(8,128)}), f32[16,88,128]{2,1,0:T(8,128)S(1)}, u32[]{:S(2)}, u32[]{:S(2)}) async-start(f32[16,88,128]{2,1,0:T(8,128)} %pad_maximum_fusion.2), calls=%async_computation.7 | async-start | bytes 1441792 | tf_op jit(solution)/shard_map/all_to_all | solution.py:15
  181.1 18.9 %all-to-all-done.7.got_r = f32[16,88,128]{2,1,0:T(8,128)S(1)} async-done(((f32[16,88,128]{2,1,0:T(8,128)}), f32[16,88,128]{2,1,0:T(8,128)S(1)}, u32[]{:S(2)}, u32[]{:S(2)}) %all-to-all-start.7) | async-done | bytes 720928 | tf_op jit(solution)/shard_map/all_to_all | solution.py:15
  200.0 2.1 shard_map.99
  202.4 16.2 %all_to_all.46 = f32[16,40,128]{2,1,0:T(8,128)S(1)} all-to-all(f32[16,40,128]{2,1,0:T(8,128)S(1)} %select_maximum_fusion), channel_id=1, replica_groups={{0,2,4,6,8,10,12,14,16,18,20,22,24,26,28,30},{1,3,5,7,9,11,13,15,17,19,..., dimensions={0} | all-to-all | bytes 655360 | tf_op jit(solution)/shard_map/all_to_all | solution.py:21
  218.6 5.3 %collective-permute-start.2 = (f32[16,40,128]{2,1,0:T(8,128)S(1)}, f32[16,40,128]{2,1,0:T(8,128)S(1)}, u32[]{:S(2)}, u32[]{:S(2)}) collective-permute-start(f32[16,40,128]{2,1,0:T(8,128)S(1)} %all_to_all.46), channel_id=1, source_target_pairs={{0,1},{1,0},{2,3},{3,2},{4,5},{5,4},{6,7},{7,6},{8,9},{9,8},{10,11... | collective-permute-start | bytes 983048 | tf_op jit(solution)/shard_map/ppermute | solution.py:22
  (129 shorter events, 25.2 us)
Async XLA Ops:
  0.6 19.9 %copy-start.7 = (f32[512,256]{1,0:T(8,128)S(1)}, f32[512,256]{1,0:T(8,128)}, u32[]{:S(2)}) copy-start(f32[512,256]{1,0:T(8,128)} %param.17) | copy-start | bytes 1572868
  2.2 17.0 %copy-start.2 = (f32[1,16,256]{2,1,0:T(8,128)S(1)}, f32[1,16,256]{2,1,0:T(8,128)}, u32[]{:S(2)}) copy-start(f32[1,16,256]{2,1,0:T(8,128)} %param.16) | copy-start | bytes 49156
  2.2 28.2 %all-to-all-start = ((f32[16,32,128]{2,1,0:T(8,128)}), f32[16,32,128]{2,1,0:T(8,128)S(1)}, u32[]{:S(2)}, u32[]{:S(2)}) async-start(f32[16,32,128]{2,1,0:T(8,128)} %broadcast_in_dim.33), calls=%async_computation | async-start | bytes 524288 | tf_op jit(solution)/shard_map/all_to_all | solution.py:21
  19.2 0.7 copy-start.8
  30.4 5.2 %collective-permute-start = (f32[16,32,128]{2,1,0:T(8,128)S(1)}, f32[16,32,128]{2,1,0:T(8,128)S(1)}, u32[]{:S(2)}, u32[]{:S(2)}) collective-permute-start(f32[16,32,128]{2,1,0:T(8,128)S(1)} %all-to-all-done), channel_id=1, source_target_pairs={{0,1},{1,0},{2,3},{3,2},{4,5},{5,4},{6,7},{7,6},{8,9},{9,8},{10,11... | collective-permute-start | bytes 786440 | tf_op jit(solution)/shard_map/ppermute | solution.py:22
  37.3 13.9 %all-to-all-start.1 = ((bf16[16,40,128]{2,1,0:T(8,128)(2,1)}), bf16[16,40,128]{2,1,0:T(8,128)(2,1)S(1)}, u32[]{:S(2)}, u32[]{:S(2)}) async-start(bf16[16,40,128]{2,1,0:T(8,128)(2,1)} %pad_maximum_fusion.7), calls=%async_computation.1 | async-start | bytes 327680 | tf_op jit(solution)/shard_map/all_to_all | solution.py:15
  44.2 0.8 copy-start.4
  44.2 7.0 %copy-start = (bf16[1,1,2,16,128,128]{5,4,3,2,1,0:T(8,128)(2,1)S(1)}, bf16[1,1,2,16,128,128]{5,4,3,2,1,0:T(8,128)(2,1)}, u32[]{:S(2)}) copy-start(bf16[1,1,2,16,128,128]{5,4,3,2,1,0:T(8,128)(2,1)} %param.11) | copy-start | bytes 3145732
  53.7 21.2 %all-to-all-start.2 = ((f32[32,24,128]{2,1,0:T(8,128)}), f32[32,24,128]{2,1,0:T(8,128)S(1)}, u32[]{:S(2)}, u32[]{:S(2)}) async-start(f32[32,24,128]{2,1,0:T(8,128)} %shard_map.94), calls=%async_computation.2 | async-start | bytes 786432 | tf_op jit(solution)/shard_map/all_to_all | solution.py:15
  59.8 0.7 copy-start.3
  77.0 25.7 %all-to-all-start.3 = ((f32[16,88,128]{2,1,0:T(8,128)}), f32[16,88,128]{2,1,0:T(8,128)S(1)}, u32[]{:S(2)}, u32[]{:S(2)}) async-start(f32[16,88,128]{2,1,0:T(8,128)} %pad_maximum_fusion.1), calls=%async_computation.3 | async-start | bytes 1441792 | tf_op jit(solution)/shard_map/all_to_all | solution.py:15
  102.7 1.0 copy-start.1
  125.3 7.0 %collective-permute-start.1 = (f32[16,64,128]{2,1,0:T(8,128)S(1)}, f32[16,64,128]{2,1,0:T(8,128)S(1)}, u32[]{:S(2)}, u32[]{:S(2)}) collective-permute-start(f32[16,64,128]{2,1,0:T(8,128)S(1)} %all_to_all.45), channel_id=1, source_target_pairs={{0,1},{1,0},{2,3},{3,2},{4,5},{5,4},{6,7},{7,6},{8,9},{9,8},{10,11... | collective-permute-start | bytes 1572872 | tf_op jit(solution)/shard_map/ppermute | solution.py:22
  132.7 0.8 copy-start.5
  134.4 12.4 %all-to-all-start.5 = ((bf16[16,40,128]{2,1,0:T(8,128)(2,1)}), bf16[16,40,128]{2,1,0:T(8,128)(2,1)S(1)}, u32[]{:S(2)}, u32[]{:S(2)}) async-start(bf16[16,40,128]{2,1,0:T(8,128)(2,1)} %pad_maximum_fusion.8), calls=%async_computation.5 | async-start | bytes 327680 | tf_op jit(solution)/shard_map/all_to_all | solution.py:15
  149.2 22.8 %all-to-all-start.6 = ((f32[32,24,128]{2,1,0:T(8,128)}), f32[32,24,128]{2,1,0:T(8,128)S(1)}, u32[]{:S(2)}, u32[]{:S(2)}) async-start(f32[32,24,128]{2,1,0:T(8,128)} %shard_map.97), calls=%async_computation.6 | async-start | bytes 786432 | tf_op jit(solution)/shard_map/all_to_all | solution.py:15
  174.2 25.7 %all-to-all-start.7 = ((f32[16,88,128]{2,1,0:T(8,128)}), f32[16,88,128]{2,1,0:T(8,128)S(1)}, u32[]{:S(2)}, u32[]{:S(2)}) async-start(f32[16,88,128]{2,1,0:T(8,128)} %pad_maximum_fusion.2), calls=%async_computation.7 | async-start | bytes 1441792 | tf_op jit(solution)/shard_map/all_to_all | solution.py:15
  179.9 1.0 copy-start.6
  218.6 6.5 %collective-permute-start.2 = (f32[16,40,128]{2,1,0:T(8,128)S(1)}, f32[16,40,128]{2,1,0:T(8,128)S(1)}, u32[]{:S(2)}, u32[]{:S(2)}) collective-permute-start(f32[16,40,128]{2,1,0:T(8,128)S(1)} %all_to_all.46), channel_id=1, source_target_pairs={{0,1},{1,0},{2,3},{3,2},{4,5},{5,4},{6,7},{7,6},{8,9},{9,8},{10,11... | collective-permute-start | bytes 983048 | tf_op jit(solution)/shard_map/ppermute | solution.py:22
